TPU v7x, 256 devices: a whole 4x4x8 slice. The times are simulated.
256 devices in a mesh: gx: 32 (over z, x_lo, core), gy: 8 (over y, x_hi).
Axes of the slice: x: 4 (x_hi: 2, x_lo: 2; x = x_hi * 2 + x_lo), y: 4, z: 8, core: 2. Of those that a mesh axis runs over, the one named last changes fastest.
Arguments:
- fine_old: float32 [2, 3, 40, 64, 2048], P(None, None, None, 'gx', 'gy'), may hold values from -6 to 6
- fine_now: float32 [2, 3, 40, 64, 2048], P(None, None, None, 'gx', 'gy'), may hold values from -6 to 6
- coarse_old: float32 [2, 3, 80, 32, 1024], P(None, None, None, 'gx', 'gy'), may hold values from -6 to 6
- coarse_now: float32 [2, 3, 80, 32, 1024], P(None, None, None, 'gx', 'gy'), may hold values from -6 to 6
- shear_fine: float32 [40, 64, 2048], P(None, 'gx', 'gy'), may hold values from 0.3 to 1.2
- lame_fine: float32 [40, 64, 2048], P(None, 'gx', 'gy'), may hold values from 0.5 to 2
- shear_coarse: float32 [80, 32, 1024], P(None, 'gx', 'gy'), may hold values from 0.3 to 1.2
- lame_coarse: float32 [80, 32, 1024], P(None, 'gx', 'gy'), may hold values from 0.5 to 2
- topography: int32 [64, 2048], P('gx', 'gy'), may hold values from 0 to 512
Outputs:
- fine_field: float32 [2, 3, 40, 64, 2048], P(None, None, None, 'gx', 'gy')
- coarse_field: float32 [2, 3, 80, 32, 1024], P(None, None, None, 'gx', 'gy')
- fine_kernel: float32 [40, 64, 2048], P(None, 'gx', 'gy')
- coarse_kernel: float32 [80, 32, 1024], P(None, 'gx', 'gy')
All inputs are finite; a program needn't handle non-finite values.
Results may differ from a plain program's by a relative error of at most 0.0003.
Values sent between devices are 32-bit elements; how exact they have to be, the bound alone decides.
No kernel may reach another device: no remote copies, remote signals or barrier semaphores. Data moves between devices by JAX's collectives and lax.ppermute only.
A program may use at most 64 MiB of HBM per device.

v0:
```python
import jax
import jax.numpy as jnp
from jax import lax
from jax.sharding import PartitionSpec as P

STEPS = 2


STEP_SQUARED = 0.04


def with_halo(cells, sides, width):
    for axis, dim in sides:
        count = lax.axis_size(axis)
        ends = count - 1
        head = lax.slice_in_dim(cells, 0, width, axis=dim)
        tail = lax.slice_in_dim(cells, cells.shape[dim] - width, cells.shape[dim], axis=dim)
        cells = jnp.concatenate(
            [
                lax.ppermute(tail, axis, [(i, (i + 1) % count) for i in range(ends)]),
                cells,
                lax.ppermute(head, axis, [((i + 1) % count, i) for i in range(ends)]),
            ],
            axis=dim,
        )
    return cells


def offset(padded, up_down, along_x, along_y):
    depth_cells = padded.shape[2] - 2
    row_count = padded.shape[3] - 2
    column_count = padded.shape[4] - 2
    return padded[
        :,
        :,
        1 + up_down : 1 + up_down + depth_cells,
        1 + along_x : 1 + along_x + row_count,
        1 + along_y : 1 + along_y + column_count,
    ]


def accelerate(padded, spacing_pad, grid_step, shear, lame):
    center = offset(padded, 0, 0, 0)
    spacing = spacing_pad[1:-1, 1:-1]
    inverse_area = 1.0 / (grid_step * grid_step)
    curve_xx = (offset(padded, 0, 1, 0) - 2.0 * center + offset(padded, 0, -1, 0)) * inverse_area
    curve_yy = (offset(padded, 0, 0, 1) - 2.0 * center + offset(padded, 0, 0, -1)) * inverse_area
    curve_zz = (offset(padded, 1, 0, 0) - 2.0 * center + offset(padded, -1, 0, 0)) / (
        spacing * spacing
    )
    mixed_xy = (
        offset(padded, 0, 1, 1)
        - offset(padded, 0, 1, -1)
        - offset(padded, 0, -1, 1)
        + offset(padded, 0, -1, -1)
    ) * (0.25 * inverse_area)
    east_side = (offset(padded, 1, 1, 0) - offset(padded, -1, 1, 0)) / (2.0 * spacing_pad[2:, 1:-1])
    west_side = (offset(padded, 1, -1, 0) - offset(padded, -1, -1, 0)) / (
        2.0 * spacing_pad[:-2, 1:-1]
    )
    mixed_xz = (east_side - west_side) * (0.5 / grid_step)
    north_side = (offset(padded, 1, 0, 1) - offset(padded, -1, 0, 1)) / (
        2.0 * spacing_pad[1:-1, 2:]
    )
    south_side = (offset(padded, 1, 0, -1) - offset(padded, -1, 0, -1)) / (
        2.0 * spacing_pad[1:-1, :-2]
    )
    mixed_yz = (north_side - south_side) * (0.5 / grid_step)
    laplace = curve_xx + curve_yy + curve_zz
    grad_div = jnp.stack(
        [
            curve_xx[:, 0] + mixed_xy[:, 1] + mixed_xz[:, 2],
            mixed_xy[:, 0] + curve_yy[:, 1] + mixed_yz[:, 2],
            mixed_xz[:, 0] + mixed_yz[:, 1] + curve_zz[:, 2],
        ],
        axis=1,
    )
    return shear * laplace + (lame + shear) * grad_div


def restrict(plane):
    row_sums = plane[..., 0::2, :] + plane[..., 1::2, :]
    summed = row_sums[..., 0::2] + row_sums[..., 1::2]
    return 0.25 * summed


def prolong(padded_plane):
    middle = 0.75 * padded_plane[..., 1:-1, :]
    even_rows = middle + 0.25 * padded_plane[..., :-2, :]
    odd_rows = middle + 0.25 * padded_plane[..., 2:, :]
    plane_dims = even_rows.shape
    row_pairs = jnp.stack([even_rows, odd_rows], axis=-2).reshape(
        plane_dims[:-2] + (2 * plane_dims[-2], plane_dims[-1])
    )
    center_cols = 0.75 * row_pairs[..., 1:-1]
    even_cols = center_cols + 0.25 * row_pairs[..., :-2]
    odd_cols = center_cols + 0.25 * row_pairs[..., 2:]
    col_dims = even_cols.shape
    return jnp.stack([even_cols, odd_cols], axis=-1).reshape(col_dims[:-1] + (2 * col_dims[-1],))


def on_device(
    fine_old,
    fine_now,
    coarse_old,
    coarse_now,
    shear_fine,
    lame_fine,
    shear_coarse,
    lame_coarse,
    topography,
):
    heights = with_halo(topography, (("gx", 0), ("gy", 1)), 1)
    fine_space = 1.0 + heights.astype(jnp.float32) / 1024.0
    fine_kernel = jnp.zeros(shear_fine.shape, jnp.float32)
    coarse_kernel = jnp.zeros(shear_coarse.shape, jnp.float32)
    coarse_space = jnp.full((coarse_now.shape[3] + 2, coarse_now.shape[4] + 2), 2.0, jnp.float32)
    for time_level in range(STEPS):
        ridge = restrict(fine_now[:, :, -1])
        floor_plane = jnp.zeros_like(ridge)
        coarse_ext = jnp.concatenate(
            [ridge[:, :, None], coarse_now, floor_plane[:, :, None]], axis=2
        )
        coarse_pad = with_halo(coarse_ext, (("gx", 3), ("gy", 4)), 1)
        ghost = prolong(coarse_pad[:, :, 1])
        fine_ext = jnp.concatenate([fine_now[:, :, :1], fine_now, ghost[:, :, None]], axis=2)
        fine_pad = with_halo(fine_ext, (("gx", 3), ("gy", 4)), 1)
        fine_next = (
            2.0 * fine_now
            - fine_old
            + STEP_SQUARED * accelerate(fine_pad, fine_space, 1.0, shear_fine, lame_fine)
        )
        coarse_next = (
            2.0 * coarse_now
            - coarse_old
            + STEP_SQUARED * accelerate(coarse_pad, coarse_space, 2.0, shear_coarse, lame_coarse)
        )
        fine_kernel = fine_kernel + jnp.sum(fine_next[0] * fine_next[1], axis=0)
        coarse_kernel = coarse_kernel + jnp.sum(coarse_next[0] * coarse_next[1], axis=0)
        fine_old, fine_now = (fine_now, fine_next)
        coarse_old, coarse_now = (coarse_now, coarse_next)
    return (fine_now, coarse_now, fine_kernel, coarse_kernel)


def solution(mesh):
    return jax.shard_map(
        on_device,
        mesh=mesh,
        in_specs=(
            P(None, None, None, "gx", "gy"),
            P(None, None, None, "gx", "gy"),
            P(None, None, None, "gx", "gy"),
            P(None, None, None, "gx", "gy"),
            P(None, "gx", "gy"),
            P(None, "gx", "gy"),
            P(None, "gx", "gy"),
            P(None, "gx", "gy"),
            P("gx", "gy"),
        ),
        out_specs=(
            P(None, None, None, "gx", "gy"),
            P(None, None, None, "gx", "gy"),
            P(None, "gx", "gy"),
            P(None, "gx", "gy"),
        ),
        check_vma=False,
    )
```

profile of v0, /device:TPU:127, one launch (start us, length us, event | category | flops | bytes accessed | tf_op | source)
XLA Modules:
  0.0 186.9 jit_solution(6025769704296736340)
XLA Ops:
  0.7 1.5 copy.145
  2.6 1.1 copy.149
  3.9 2.6 %collective-permute-start.1 = (f32[2,3,82,1,128]{4,0,1,3,2:T(2,128)S(1)}, f32[2,3,82,1,128]{4,0,1,3,2:T(2,128)S(1)}, u32[]{:S(2)}, u32[]{:S(2)}) collective-permute-start(f32[2,3,82,1,128]{4,0,1,3,2:T(2,128)S(1)} %pad_maximum_fusion.19), channel_id=1, source_target_pairs={{8,0},{16,8},{24,16},{32,24},{40,32},{48,40},{56,48},{64,56},{72,6... | collective-permute-start | bytes 755720 | tf_op jit(solution)/shard_map/ppermute | solution.py:22
  6.4 5.1 %collective-permute-start = (f32[2,3,82,1,128]{4,0,1,3,2:T(2,128)S(1)}, f32[2,3,82,1,128]{4,0,1,3,2:T(2,128)S(1)}, u32[]{:S(2)}, u32[]{:S(2)}) collective-permute-start(f32[2,3,82,1,128]{4,0,1,3,2:T(2,128)S(1)} %pad_maximum_fusion.19), channel_id=1, source_target_pairs={{0,8},{8,16},{16,24},{24,32},{32,40},{40,48},{48,56},{56,64},{64,7... | collective-permute-start | bytes 755720 | tf_op jit(solution)/shard_map/ppermute | solution.py:20
  11.6 2.2 %collective-permute-start.8 = (s32[1,256]{1,0:T(1,128)S(1)}, s32[1,256]{1,0:T(1,128)S(1)}, u32[]{:S(2)}, u32[]{:S(2)}) collective-permute-start(s32[1,256]{1,0:T(1,128)S(1)} %get-tuple-element.98), channel_id=1, source_target_pairs={{0,8},{8,16},{16,24},{24,32},{32,40},{40,48},{48,56},{56,64},{64,7... | collective-permute-start | bytes 3080 | tf_op jit(solution)/shard_map/ppermute | solution.py:20
  13.8 2.1 %collective-permute-start.9 = (s32[1,256]{1,0:T(1,128)S(1)}, s32[1,256]{1,0:T(1,128)S(1)}, u32[]{:S(2)}, u32[]{:S(2)}) collective-permute-start(s32[1,256]{1,0:T(1,128)S(1)} %get-tuple-element.99), channel_id=1, source_target_pairs={{8,0},{16,8},{24,16},{32,24},{40,32},{48,40},{56,48},{64,56},{72,6... | collective-permute-start | bytes 3080 | tf_op jit(solution)/shard_map/ppermute | solution.py:22
  15.9 0.9 fusion.36
  16.9 3.9 %collective-permute-done.9 = s32[1,256]{1,0:T(1,128)S(1)} collective-permute-done((s32[1,256]{1,0:T(1,128)S(1)}, s32[1,256]{1,0:T(1,128)S(1)}, u32[]{:S(2)}, u32[]{:S(2)}) %collective-permute-start.9) | collective-permute-done | bytes 1056 | tf_op jit(solution)/shard_map/ppermute | solution.py:22
  20.9 1.3 collective-permute-start.10
  22.2 5.5 %collective-permute-start.11 = (s32[4,1]{1,0:T(4,128)S(1)}, s32[4,1]{1,0:T(4,128)S(1)}, u32[]{:S(2)}, u32[]{:S(2)}) collective-permute-start(s32[4,1]{1,0:T(4,128)S(1)} %get-tuple-element.97), channel_id=1, source_target_pairs={{1,0},{2,1},{3,2},{4,3},{5,4},{6,5},{7,6},{9,8},{10,9},{11,10},{12... | collective-permute-start | bytes 56 | tf_op jit(solution)/shard_map/ppermute | solution.py:22
  27.7 0.7 collective-permute-done.11
  28.8 1.0 fusion.102
  30.7 5.1 %collective-permute-start.3 = (f32[2,3,82,3,1]{2,0,4,3,1:T(2,128)S(1)}, f32[2,3,82,3,1]{2,0,4,3,1:T(2,128)S(1)}, u32[]{:S(2)}, u32[]{:S(2)}) collective-permute-start(f32[2,3,82,3,1]{2,0,4,3,1:T(2,128)S(1)} %copy.151), channel_id=1, source_target_pairs={{1,0},{2,1},{3,2},{4,3},{5,4},{6,5},{7,6},{9,8},{10,9},{11,10},{12... | collective-permute-start | bytes 17720 | tf_op jit(solution)/shard_map/ppermute | solution.py:22
  35.8 1.3 collective-permute-start.2
  37.2 4.5 %collective-permute-done.2 = f32[2,3,82,3,1]{2,0,4,3,1:T(2,128)S(1)} collective-permute-done((f32[2,3,82,3,1]{2,0,4,3,1:T(2,128)S(1)}, f32[2,3,82,3,1]{2,0,4,3,1:T(2,128)S(1)}, u32[]{:S(2)}, u32[]{:S(2)}) %collective-permute-start.2) | collective-permute-done | bytes 5936 | tf_op jit(solution)/shard_map/ppermute | solution.py:20
  42.9 1.2 copy.184
  44.1 1.6 reshape.216
  46.1 4.8 %collective-permute-start.5 = (f32[2,3,42,1,256]{4,0,1,3,2:T(2,128)S(1)}, f32[2,3,42,1,256]{4,0,1,3,2:T(2,128)S(1)}, u32[]{:S(2)}, u32[]{:S(2)}) collective-permute-start(f32[2,3,42,1,256]{4,0,1,3,2:T(2,128)S(1)} %get-tuple-element.58), channel_id=1, source_target_pairs={{0,8},{8,16},{16,24},{24,32},{32,40},{40,48},{48,56},{56,64},{64,7... | collective-permute-start | bytes 774152 | tf_op jit(solution)/shard_map/ppermute | solution.py:20
  51.0 2.1 %collective-permute-start.4 = (f32[2,3,42,1,256]{4,0,1,3,2:T(2,128)S(1)}, f32[2,3,42,1,256]{4,0,1,3,2:T(2,128)S(1)}, u32[]{:S(2)}, u32[]{:S(2)}) collective-permute-start(f32[2,3,42,1,256]{4,0,1,3,2:T(2,128)S(1)} %get-tuple-element.59), channel_id=1, source_target_pairs={{8,0},{16,8},{24,16},{32,24},{40,32},{48,40},{56,48},{64,56},{72,6... | collective-permute-start | bytes 774152 | tf_op jit(solution)/shard_map/ppermute | solution.py:22
  53.0 4.1 %fusion.8 = (f32[2,3,82,3,129]{4,0,1,3,2:T(2,128)S(1)}, f32[2,3,82,3,129]{4,0,1,3,2:T(2,128)S(1)}) fusion(f32[2,3,1,1,128]{4,0,1,3,2:T(2,128)S(1)} %broadcast.88, f32[2,3,82,3,1]{4,0,1,3,2:T(2,128)S(1)} %copy.153, f32[2,3,82,1,128]{4,0,1,3,2:T(2,128)S(1)} %collective-permute-done.1, f32[2,3,80,1,128]{4,0,1,3,2:T(2,128)S(1)} %copy.149, ...), kind=kLoop, calls=%fused_computation.16 | loop fusion | flops 1904040 | bytes 2290752 | tf_op jit(solution)/shard_map/concatenate | solution.py:18
  57.2 1.7 fusion.59
  58.9 1.1 slice_add_fusion.34
  61.3 0.7 fusion.100
  62.0 5.6 %collective-permute-start.6 = (f32[2,3,42,4,1]{4,0,1,3,2:T(2,128)S(1)}, f32[2,3,42,4,1]{4,0,1,3,2:T(2,128)S(1)}, u32[]{:S(2)}, u32[]{:S(2)}) collective-permute-start(f32[2,3,42,4,1]{4,0,1,3,2:T(2,128)S(1)} %get-tuple-element.42), channel_id=1, source_target_pairs={{1,0},{2,1},{3,2},{4,3},{5,4},{6,5},{7,6},{9,8},{10,9},{11,10},{12... | collective-permute-start | bytes 12104 | tf_op jit(solution)/shard_map/ppermute | solution.py:22
  67.6 1.5 collective-permute-start.7
  69.1 0.7 pad_maximum_fusion.10
  69.9 1.7 slice_add_fusion.5
  71.5 6.2 %collective-permute-done.6 = f32[2,3,42,4,1]{4,0,1,3,2:T(2,128)S(1)} collective-permute-done((f32[2,3,42,4,1]{4,0,1,3,2:T(2,128)S(1)}, f32[2,3,42,4,1]{4,0,1,3,2:T(2,128)S(1)}, u32[]{:S(2)}, u32[]{:S(2)}) %collective-permute-start.6) | collective-permute-done | bytes 4064 | tf_op jit(solution)/shard_map/ppermute | solution.py:22
  77.7 11.2 %collective-permute-done.7 = f32[2,3,42,4,1]{4,0,1,3,2:T(2,128)S(1)} collective-permute-done((f32[2,3,42,4,1]{4,0,1,3,2:T(2,128)S(1)}, f32[2,3,42,4,1]{4,0,1,3,2:T(2,128)S(1)}, u32[]{:S(2)}, u32[]{:S(2)}) %collective-permute-start.7) | collective-permute-done | bytes 4064 | tf_op jit(solution)/shard_map/ppermute | solution.py:20
  89.0 3.7 %pad_maximum_fusion.4 = (f32[2,3,42,4,257]{4,0,1,3,2:T(2,128)S(1)}, f32[2,3,42,4,257]{4,0,1,3,2:T(2,128)S(1)}) fusion(f32[2,3,42,4,1]{4,0,1,3,2:T(2,128)S(1)} %collective-permute-done.6, f32[2,3,42,1,256]{4,0,1,3,2:T(2,128)S(1)} %collective-permute-done.4, f32[2,3,1,2,256]{4,0,1,3,2:T(2,128)S(1)} %reshape.216, f32[2,3,40,2,256]{4,0,1,3,2:T(2,128)S(1)} %copy.145, ...), kind=kLoop, calls=%fused_computation.4 | loop fusion | flops 2590560 | bytes 3112704 | tf_op jit(solution)/shard_map/concatenate | solution.py:18
  92.7 2.8 %fusion.20 = (f32[2,3,40,2,256]{4,0,1,3,2:T(2,128)S(1)}, f32[2,3,40,2,256]{4,0,1,3,2:T(2,128)S(1)}, f32[2,3,40,2,256]{4,0,1,3,2:T(2,128)S(1)}) fusion(f32[2,3,42,4,257]{4,0,1,3,2:T(2,128)S(1)} %get-tuple-element.41, f32[2,3,42,4,257]{4,0,1,3,2:T(2,128)S(1)} %get-tuple-element.40, f32[2,256]{1,0:T(2,128)S(1)} %get-tuple-element.92, ...), kind=kLoop, calls=%fused_computation.60 | loop fusion | flops 1597440 | bytes 6885376 | tf_op jit(solution)/shard_map/mul | solution.py:51
  95.9 0.7 copy-done.6
  96.6 1.5 fusion.26
  98.7 1.9 %collective-permute-start.13 = (f32[2,3,82,1,128]{4,0,1,3,2:T(2,128)S(1)}, f32[2,3,82,1,128]{4,0,1,3,2:T(2,128)S(1)}, u32[]{:S(2)}, u32[]{:S(2)}) collective-permute-start(f32[2,3,82,1,128]{4,0,1,3,2:T(2,128)S(1)} %pad_maximum_fusion.18), channel_id=1, source_target_pairs={{8,0},{16,8},{24,16},{32,24},{40,32},{48,40},{56,48},{64,56},{72,6... | collective-permute-start | bytes 755720 | tf_op jit(solution)/shard_map/ppermute | solution.py:22
  100.6 5.8 %collective-permute-start.12 = (f32[2,3,82,1,128]{4,0,1,3,2:T(2,128)S(1)}, f32[2,3,82,1,128]{4,0,1,3,2:T(2,128)S(1)}, u32[]{:S(2)}, u32[]{:S(2)}) collective-permute-start(f32[2,3,82,1,128]{4,0,1,3,2:T(2,128)S(1)} %pad_maximum_fusion.18), channel_id=1, source_target_pairs={{0,8},{8,16},{16,24},{24,32},{32,40},{40,48},{48,56},{56,64},{64,7... | collective-permute-start | bytes 755720 | tf_op jit(solution)/shard_map/ppermute | solution.py:20
  106.4 0.9 fusion.70
  107.2 0.9 fusion.39
  108.5 1.1 collective-permute-done.12
  109.9 1.0 fusion.101
  110.9 1.1 copy.167
  112.6 5.9 %collective-permute-start.15 = (f32[2,3,82,3,1]{2,3,4,1,0:T(4,128)S(1)}, f32[2,3,82,3,1]{2,3,4,1,0:T(4,128)}, u32[]{:S(2)}, u32[]{:S(2)}) collective-permute-start(f32[2,3,82,3,1]{2,3,4,1,0:T(4,128)S(1)} %copy.168), channel_id=1, source_target_pairs={{1,0},{2,1},{3,2},{4,3},{5,4},{6,5},{7,6},{9,8},{10,9},{11,10},{12... | collective-permute-start | bytes 17720 | tf_op jit(solution)/shard_map/ppermute | solution.py:22
  118.5 1.3 collective-permute-start.14
  119.8 1.1 fusion.68
  120.9 3.7 %collective-permute-done.14 = f32[2,3,82,3,1]{2,3,4,1,0:T(4,128)S(1)} collective-permute-done((f32[2,3,82,3,1]{2,3,4,1,0:T(4,128)}, f32[2,3,82,3,1]{2,3,4,1,0:T(4,128)S(1)}, u32[]{:S(2)}, u32[]{:S(2)}) %collective-permute-start.14) | collective-permute-done | bytes 5936 | tf_op jit(solution)/shard_map/ppermute | solution.py:20
  125.1 1.2 copy.170
  126.5 1.2 copy.187
  127.8 1.6 reshape.217
  129.8 7.3 %collective-permute-start.17 = (f32[2,3,42,1,256]{4,0,1,3,2:T(2,128)S(1)}, f32[2,3,42,1,256]{4,0,1,3,2:T(2,128)S(1)}, u32[]{:S(2)}, u32[]{:S(2)}) collective-permute-start(f32[2,3,42,1,256]{4,0,1,3,2:T(2,128)S(1)} %get-tuple-element.54), channel_id=1, source_target_pairs={{0,8},{8,16},{16,24},{24,32},{32,40},{40,48},{48,56},{56,64},{64,7... | collective-permute-start | bytes 774152 | tf_op jit(solution)/shard_map/ppermute | solution.py:20
  137.1 2.1 %collective-permute-start.16 = (f32[2,3,42,1,256]{4,0,1,3,2:T(2,128)S(1)}, f32[2,3,42,1,256]{4,0,1,3,2:T(2,128)S(1)}, u32[]{:S(2)}, u32[]{:S(2)}) collective-permute-start(f32[2,3,42,1,256]{4,0,1,3,2:T(2,128)S(1)} %get-tuple-element.55), channel_id=1, source_target_pairs={{8,0},{16,8},{24,16},{32,24},{40,32},{48,40},{56,48},{64,56},{72,6... | collective-permute-start | bytes 774152 | tf_op jit(solution)/shard_map/ppermute | solution.py:22
  139.2 4.1 %fusion.11 = (f32[2,3,82,3,129]{4,0,1,3,2:T(2,128)S(1)}, f32[2,3,82,3,129]{4,0,1,3,2:T(2,128)S(1)}) fusion(f32[2,3,1,1,128]{4,0,1,3,2:T(2,128)S(1)} %broadcast.88, f32[2,3,82,3,1]{4,0,1,3,2:T(2,128)S(1)} %copy.170, f32[2,3,82,1,128]{4,0,1,3,2:T(2,128)S(1)} %collective-permute-done.13, f32[2,3,80,1,128]{4,0,1,3,2:T(2,128)S(1)} %fusion.64, ...), kind=kLoop, calls=%fused_computation.19 | loop fusion | flops 1904040 | bytes 2290752 | tf_op jit(solution)/shard_map/concatenate | solution.py:18
  143.4 1.7 fusion.48
  145.1 1.1 slice_add_fusion.28
  146.8 0.9 copy.183
  149.0 0.7 fusion.99
  149.7 3.2 %collective-permute-start.18 = (f32[2,3,42,4,1]{4,0,1,3,2:T(2,128)S(1)}, f32[2,3,42,4,1]{4,0,1,3,2:T(2,128)S(1)}, u32[]{:S(2)}, u32[]{:S(2)}) collective-permute-start(f32[2,3,42,4,1]{4,0,1,3,2:T(2,128)S(1)} %get-tuple-element.38), channel_id=1, source_target_pairs={{1,0},{2,1},{3,2},{4,3},{5,4},{6,5},{7,6},{9,8},{10,9},{11,10},{12... | collective-permute-start | bytes 12104 | tf_op jit(solution)/shard_map/ppermute | solution.py:22
  152.9 1.3 collective-permute-start.19
  154.2 0.7 pad_maximum_fusion.11
  155.6 6.4 %collective-permute-done.18 = f32[2,3,42,4,1]{4,0,1,3,2:T(2,128)S(1)} collective-permute-done((f32[2,3,42,4,1]{4,0,1,3,2:T(2,128)S(1)}, f32[2,3,42,4,1]{4,0,1,3,2:T(2,128)S(1)}, u32[]{:S(2)}, u32[]{:S(2)}) %collective-permute-start.18) | collective-permute-done | bytes 4064 | tf_op jit(solution)/shard_map/ppermute | solution.py:22
  162.0 13.7 %collective-permute-done.19 = f32[2,3,42,4,1]{4,0,1,3,2:T(2,128)S(1)} collective-permute-done((f32[2,3,42,4,1]{4,0,1,3,2:T(2,128)S(1)}, f32[2,3,42,4,1]{4,0,1,3,2:T(2,128)S(1)}, u32[]{:S(2)}, u32[]{:S(2)}) %collective-permute-start.19) | collective-permute-done | bytes 4064 | tf_op jit(solution)/shard_map/ppermute | solution.py:20
  175.8 3.7 %pad_maximum_fusion.5 = (f32[2,3,42,4,257]{4,0,1,3,2:T(2,128)S(1)}, f32[2,3,42,4,257]{4,0,1,3,2:T(2,128)S(1)}) fusion(f32[2,3,42,4,1]{4,0,1,3,2:T(2,128)S(1)} %collective-permute-done.18, f32[2,3,42,1,256]{4,0,1,3,2:T(2,128)S(1)} %collective-permute-done.16, f32[2,3,1,2,256]{4,0,1,3,2:T(2,128)S(1)} %reshape.217, f32[2,3,40,2,256]{4,0,1,3,2:T(2,128)S(1)} %fusion.26, ...), kind=kLoop, calls=%fused_computation.6 | loop fusion | flops 2590560 | bytes 3112704 | tf_op jit(solution)/shard_map/concatenate | solution.py:18
  179.5 3.0 %fusion.16 = (f32[2,3,40,2,256]{4,0,1,3,2:T(2,128)S(1)}, f32[2,3,40,2,256]{4,0,1,3,2:T(2,128)S(1)}, f32[2,3,40,2,256]{4,0,1,3,2:T(2,128)S(1)}, f32[2,3,40,2,256]{4,0,1,3,2:T(2,128)S(1)}) fusion(f32[2,3,42,4,257]{4,0,1,3,2:T(2,128)S(1)} %get-tuple-element.37, f32[2,3,42,4,257]{4,0,1,3,2:T(2,128)S(1)} %get-tuple-element.36, ...), kind=kLoop, calls=%fused_computation.43 | loop fusion | flops 2211840 | bytes 7403520 | tf_op jit(solution)/shard_map/mul | solution.py:51
  183.4 1.2 fusion.29
  185.1 1.0 copy.182
  186.2 0.7 add.359
  (98 shorter events, 12.1 us)
Async XLA Ops:
  0.6 10.9 %copy-start.16 = (s32[2,256]{1,0:T(2,128)S(1)}, s32[2,256]{1,0:T(2,128)}, u32[]{:S(2)}) copy-start(s32[2,256]{1,0:T(2,128)} %param.17) | copy-start | bytes 6148
  0.6 16.1 %copy-start.7 = (f32[80,1,128]{2,1,0:T(1,128)S(1)}, f32[80,1,128]{2,1,0:T(1,128)}, u32[]{:S(2)}) copy-start(f32[80,1,128]{2,1,0:T(1,128)} %param.15) | copy-start | bytes 122884
  0.7 16.1 %copy-start.15 = (f32[80,1,128]{2,1,0:T(1,128)S(1)}, f32[80,1,128]{2,1,0:T(1,128)}, u32[]{:S(2)}) copy-start(f32[80,1,128]{2,1,0:T(1,128)} %param.16) | copy-start | bytes 122884
  0.7 16.2 %copy-start.2 = (f32[40,2,256]{2,1,0:T(2,128)S(1)}, f32[40,2,256]{2,1,0:T(2,128)}, u32[]{:S(2)}) copy-start(f32[40,2,256]{2,1,0:T(2,128)} %param.13) | copy-start | bytes 245764
  0.7 16.2 %copy-start.14 = (f32[40,2,256]{2,1,0:T(2,128)S(1)}, f32[40,2,256]{2,1,0:T(2,128)}, u32[]{:S(2)}) copy-start(f32[40,2,256]{2,1,0:T(2,128)} %param.14) | copy-start | bytes 245764
  3.9 24.6 %collective-permute-start.1 = (f32[2,3,82,1,128]{4,0,1,3,2:T(2,128)S(1)}, f32[2,3,82,1,128]{4,0,1,3,2:T(2,128)S(1)}, u32[]{:S(2)}, u32[]{:S(2)}) collective-permute-start(f32[2,3,82,1,128]{4,0,1,3,2:T(2,128)S(1)} %pad_maximum_fusion.19), channel_id=1, source_target_pairs={{8,0},{16,8},{24,16},{32,24},{40,32},{48,40},{56,48},{64,56},{72,6... | collective-permute-start | bytes 755720 | tf_op jit(solution)/shard_map/ppermute | solution.py:22
  6.4 22.0 %collective-permute-start = (f32[2,3,82,1,128]{4,0,1,3,2:T(2,128)S(1)}, f32[2,3,82,1,128]{4,0,1,3,2:T(2,128)S(1)}, u32[]{:S(2)}, u32[]{:S(2)}) collective-permute-start(f32[2,3,82,1,128]{4,0,1,3,2:T(2,128)S(1)} %pad_maximum_fusion.19), channel_id=1, source_target_pairs={{0,8},{8,16},{16,24},{24,32},{32,40},{40,48},{48,56},{56,64},{64,7... | collective-permute-start | bytes 755720 | tf_op jit(solution)/shard_map/ppermute | solution.py:20
  11.6 5.4 %collective-permute-start.8 = (s32[1,256]{1,0:T(1,128)S(1)}, s32[1,256]{1,0:T(1,128)S(1)}, u32[]{:S(2)}, u32[]{:S(2)}) collective-permute-start(s32[1,256]{1,0:T(1,128)S(1)} %get-tuple-element.98), channel_id=1, source_target_pairs={{0,8},{8,16},{16,24},{24,32},{32,40},{40,48},{48,56},{56,64},{64,7... | collective-permute-start | bytes 3080 | tf_op jit(solution)/shard_map/ppermute | solution.py:20
  13.8 7.0 %collective-permute-start.9 = (s32[1,256]{1,0:T(1,128)S(1)}, s32[1,256]{1,0:T(1,128)S(1)}, u32[]{:S(2)}, u32[]{:S(2)}) collective-permute-start(s32[1,256]{1,0:T(1,128)S(1)} %get-tuple-element.99), channel_id=1, source_target_pairs={{8,0},{16,8},{24,16},{32,24},{40,32},{48,40},{56,48},{64,56},{72,6... | collective-permute-start | bytes 3080 | tf_op jit(solution)/shard_map/ppermute | solution.py:22
  16.8 43.1 %copy-start.9 = (f32[80,1,128]{2,1,0:T(1,128)}, f32[80,1,128]{2,1,0:T(1,128)S(1)}, u32[]{:S(2)}) copy-start(f32[80,1,128]{2,1,0:T(1,128)S(1)} %add.317) | copy-start | bytes 122884
  16.9 79.0 %copy-start.4 = (f32[40,2,256]{2,1,0:T(2,128)}, f32[40,2,256]{2,1,0:T(2,128)S(1)}, u32[]{:S(2)}) copy-start(f32[40,2,256]{2,1,0:T(2,128)S(1)} %add.300) | copy-start | bytes 245764
  20.9 6.8 %collective-permute-start.10 = (s32[4,1]{1,0:T(4,128)S(1)}, s32[4,1]{1,0:T(4,128)S(1)}, u32[]{:S(2)}, u32[]{:S(2)}) collective-permute-start(s32[4,1]{1,0:T(4,128)S(1)} %get-tuple-element.96), channel_id=1, source_target_pairs={{0,1},{1,2},{2,3},{3,4},{4,5},{5,6},{6,7},{8,9},{9,10},{10,11},{11... | collective-permute-start | bytes 56 | tf_op jit(solution)/shard_map/ppermute | solution.py:20
  22.2 6.2 %collective-permute-start.11 = (s32[4,1]{1,0:T(4,128)S(1)}, s32[4,1]{1,0:T(4,128)S(1)}, u32[]{:S(2)}, u32[]{:S(2)}) collective-permute-start(s32[4,1]{1,0:T(4,128)S(1)} %get-tuple-element.97), channel_id=1, source_target_pairs={{1,0},{2,1},{3,2},{4,3},{5,4},{6,5},{7,6},{9,8},{10,9},{11,10},{12... | collective-permute-start | bytes 56 | tf_op jit(solution)/shard_map/ppermute | solution.py:22
  30.7 11.5 %collective-permute-start.3 = (f32[2,3,82,3,1]{2,0,4,3,1:T(2,128)S(1)}, f32[2,3,82,3,1]{2,0,4,3,1:T(2,128)S(1)}, u32[]{:S(2)}, u32[]{:S(2)}) collective-permute-start(f32[2,3,82,3,1]{2,0,4,3,1:T(2,128)S(1)} %copy.151), channel_id=1, source_target_pairs={{1,0},{2,1},{3,2},{4,3},{5,4},{6,5},{7,6},{9,8},{10,9},{11,10},{12... | collective-permute-start | bytes 17720 | tf_op jit(solution)/shard_map/ppermute | solution.py:22
  35.8 5.9 %collective-permute-start.2 = (f32[2,3,82,3,1]{2,0,4,3,1:T(2,128)S(1)}, f32[2,3,82,3,1]{2,0,4,3,1:T(2,128)S(1)}, u32[]{:S(2)}, u32[]{:S(2)}) collective-permute-start(f32[2,3,82,3,1]{2,0,4,3,1:T(2,128)S(1)} %copy.150), channel_id=1, source_target_pairs={{0,1},{1,2},{2,3},{3,4},{4,5},{5,6},{6,7},{8,9},{9,10},{10,11},{11... | collective-permute-start | bytes 17720 | tf_op jit(solution)/shard_map/ppermute | solution.py:20
  46.1 14.5 %collective-permute-start.5 = (f32[2,3,42,1,256]{4,0,1,3,2:T(2,128)S(1)}, f32[2,3,42,1,256]{4,0,1,3,2:T(2,128)S(1)}, u32[]{:S(2)}, u32[]{:S(2)}) collective-permute-start(f32[2,3,42,1,256]{4,0,1,3,2:T(2,128)S(1)} %get-tuple-element.58), channel_id=1, source_target_pairs={{0,8},{8,16},{16,24},{24,32},{32,40},{40,48},{48,56},{56,64},{64,7... | collective-permute-start | bytes 774152 | tf_op jit(solution)/shard_map/ppermute | solution.py:20
  50.9 6.2 %copy-start.1 = (f32[2,3,80,1,128]{4,3,2,1,0:T(1,128)S(1)}, f32[2,3,80,1,128]{4,3,2,1,0:T(1,128)}, u32[]{:S(2)}) copy-start(f32[2,3,80,1,128]{4,3,2,1,0:T(1,128)} %param.12) | copy-start | bytes 737284
  51.0 9.9 %collective-permute-start.4 = (f32[2,3,42,1,256]{4,0,1,3,2:T(2,128)S(1)}, f32[2,3,42,1,256]{4,0,1,3,2:T(2,128)S(1)}, u32[]{:S(2)}, u32[]{:S(2)}) collective-permute-start(f32[2,3,42,1,256]{4,0,1,3,2:T(2,128)S(1)} %get-tuple-element.59), channel_id=1, source_target_pairs={{8,0},{16,8},{24,16},{32,24},{40,32},{48,40},{56,48},{64,56},{72,6... | collective-permute-start | bytes 774152 | tf_op jit(solution)/shard_map/ppermute | solution.py:22
  57.2 2.8 %copy-start.12 = (f32[2,3,80,1,128]{4,3,2,1,0:T(1,128)S(1)}, f32[2,3,80,1,128]{4,3,2,1,0:T(1,128)}, u32[]{:S(2)}) copy-start(f32[2,3,80,1,128]{4,3,2,1,0:T(1,128)} %param.11) | copy-start | bytes 737284
  62.0 7.8 %copy-start = (f32[2,3,40,2,256]{4,3,2,1,0:T(2,128)S(1)}, f32[2,3,40,2,256]{4,3,2,1,0:T(2,128)}, u32[]{:S(2)}) copy-start(f32[2,3,40,2,256]{4,3,2,1,0:T(2,128)} %param.10) | copy-start | bytes 1474564
  62.0 15.7 %collective-permute-start.6 = (f32[2,3,42,4,1]{4,0,1,3,2:T(2,128)S(1)}, f32[2,3,42,4,1]{4,0,1,3,2:T(2,128)S(1)}, u32[]{:S(2)}, u32[]{:S(2)}) collective-permute-start(f32[2,3,42,4,1]{4,0,1,3,2:T(2,128)S(1)} %get-tuple-element.42), channel_id=1, source_target_pairs={{1,0},{2,1},{3,2},{4,3},{5,4},{6,5},{7,6},{9,8},{10,9},{11,10},{12... | collective-permute-start | bytes 12104 | tf_op jit(solution)/shard_map/ppermute | solution.py:22
  67.6 21.4 %collective-permute-start.7 = (f32[2,3,42,4,1]{4,0,1,3,2:T(2,128)S(1)}, f32[2,3,42,4,1]{4,0,1,3,2:T(2,128)S(1)}, u32[]{:S(2)}, u32[]{:S(2)}) collective-permute-start(f32[2,3,42,4,1]{4,0,1,3,2:T(2,128)S(1)} %get-tuple-element.43), channel_id=1, source_target_pairs={{0,1},{1,2},{2,3},{3,4},{4,5},{5,6},{6,7},{8,9},{9,10},{10,11},{11... | collective-permute-start | bytes 12104 | tf_op jit(solution)/shard_map/ppermute | solution.py:20
  95.5 1.0 copy-start.6
  98.7 9.8 %collective-permute-start.13 = (f32[2,3,82,1,128]{4,0,1,3,2:T(2,128)S(1)}, f32[2,3,82,1,128]{4,0,1,3,2:T(2,128)S(1)}, u32[]{:S(2)}, u32[]{:S(2)}) collective-permute-start(f32[2,3,82,1,128]{4,0,1,3,2:T(2,128)S(1)} %pad_maximum_fusion.18), channel_id=1, source_target_pairs={{8,0},{16,8},{24,16},{32,24},{40,32},{48,40},{56,48},{64,56},{72,6... | collective-permute-start | bytes 755720 | tf_op jit(solution)/shard_map/ppermute | solution.py:22
  100.6 8.9 %collective-permute-start.12 = (f32[2,3,82,1,128]{4,0,1,3,2:T(2,128)S(1)}, f32[2,3,82,1,128]{4,0,1,3,2:T(2,128)S(1)}, u32[]{:S(2)}, u32[]{:S(2)}) collective-permute-start(f32[2,3,82,1,128]{4,0,1,3,2:T(2,128)S(1)} %pad_maximum_fusion.18), channel_id=1, source_target_pairs={{0,8},{8,16},{16,24},{24,32},{32,40},{40,48},{48,56},{56,64},{64,7... | collective-permute-start | bytes 755720 | tf_op jit(solution)/shard_map/ppermute | solution.py:20
  112.6 12.5 %collective-permute-start.15 = (f32[2,3,82,3,1]{2,3,4,1,0:T(4,128)S(1)}, f32[2,3,82,3,1]{2,3,4,1,0:T(4,128)}, u32[]{:S(2)}, u32[]{:S(2)}) collective-permute-start(f32[2,3,82,3,1]{2,3,4,1,0:T(4,128)S(1)} %copy.168), channel_id=1, source_target_pairs={{1,0},{2,1},{3,2},{4,3},{5,4},{6,5},{7,6},{9,8},{10,9},{11,10},{12... | collective-permute-start | bytes 17720 | tf_op jit(solution)/shard_map/ppermute | solution.py:22
  118.5 6.1 %collective-permute-start.14 = (f32[2,3,82,3,1]{2,3,4,1,0:T(4,128)}, f32[2,3,82,3,1]{2,3,4,1,0:T(4,128)S(1)}, u32[]{:S(2)}, u32[]{:S(2)}) collective-permute-start(f32[2,3,82,3,1]{2,3,4,1,0:T(4,128)} %copy.167), channel_id=1, source_target_pairs={{0,1},{1,2},{2,3},{3,4},{4,5},{5,6},{6,7},{8,9},{9,10},{10,11},{11... | collective-permute-start | bytes 17720 | tf_op jit(solution)/shard_map/ppermute | solution.py:20
  129.8 18.8 %collective-permute-start.17 = (f32[2,3,42,1,256]{4,0,1,3,2:T(2,128)S(1)}, f32[2,3,42,1,256]{4,0,1,3,2:T(2,128)S(1)}, u32[]{:S(2)}, u32[]{:S(2)}) collective-permute-start(f32[2,3,42,1,256]{4,0,1,3,2:T(2,128)S(1)} %get-tuple-element.54), channel_id=1, source_target_pairs={{0,8},{8,16},{16,24},{24,32},{32,40},{40,48},{48,56},{56,64},{64,7... | collective-permute-start | bytes 774152 | tf_op jit(solution)/shard_map/ppermute | solution.py:20
  137.1 11.5 %collective-permute-start.16 = (f32[2,3,42,1,256]{4,0,1,3,2:T(2,128)S(1)}, f32[2,3,42,1,256]{4,0,1,3,2:T(2,128)S(1)}, u32[]{:S(2)}, u32[]{:S(2)}) collective-permute-start(f32[2,3,42,1,256]{4,0,1,3,2:T(2,128)S(1)} %get-tuple-element.55), channel_id=1, source_target_pairs={{8,0},{16,8},{24,16},{32,24},{40,32},{48,40},{56,48},{64,56},{72,6... | collective-permute-start | bytes 774152 | tf_op jit(solution)/shard_map/ppermute | solution.py:22
  143.4 2.8 %copy-start.8 = (f32[80,1,128]{2,1,0:T(1,128)S(1)}, f32[80,1,128]{2,1,0:T(1,128)}, u32[]{:S(2)}) copy-start(f32[80,1,128]{2,1,0:T(1,128)} %param.15) | copy-start | bytes 122884
  143.4 2.8 %copy-start.10 = (f32[80,1,128]{2,1,0:T(1,128)S(1)}, f32[80,1,128]{2,1,0:T(1,128)}, u32[]{:S(2)}) copy-start(f32[80,1,128]{2,1,0:T(1,128)} %copy-done.9) | copy-start | bytes 122884
  145.1 2.8 %copy-start.13 = (f32[80,128]{1,0:T(8,128)S(1)}, f32[80,128]{1,0:T(8,128)}, u32[]{:S(2)}) copy-start(f32[80,128]{1,0:T(8,128)} %fusion.70) | copy-start | bytes 122884
  149.7 12.3 %collective-permute-start.18 = (f32[2,3,42,4,1]{4,0,1,3,2:T(2,128)S(1)}, f32[2,3,42,4,1]{4,0,1,3,2:T(2,128)S(1)}, u32[]{:S(2)}, u32[]{:S(2)}) collective-permute-start(f32[2,3,42,4,1]{4,0,1,3,2:T(2,128)S(1)} %get-tuple-element.38), channel_id=1, source_target_pairs={{1,0},{2,1},{3,2},{4,3},{5,4},{6,5},{7,6},{9,8},{10,9},{11,10},{12... | collective-permute-start | bytes 12104 | tf_op jit(solution)/shard_map/ppermute | solution.py:22
  152.9 22.8 %collective-permute-start.19 = (f32[2,3,42,4,1]{4,0,1,3,2:T(2,128)S(1)}, f32[2,3,42,4,1]{4,0,1,3,2:T(2,128)S(1)}, u32[]{:S(2)}, u32[]{:S(2)}) collective-permute-start(f32[2,3,42,4,1]{4,0,1,3,2:T(2,128)S(1)} %get-tuple-element.39), channel_id=1, source_target_pairs={{0,1},{1,2},{2,3},{3,4},{4,5},{5,6},{6,7},{8,9},{9,10},{10,11},{11... | collective-permute-start | bytes 12104 | tf_op jit(solution)/shard_map/ppermute | solution.py:20
  182.5 0.9 copy-start.3
  182.5 0.9 copy-start.5
  184.6 1.6 copy-start.11
where the time goes:
time: 188 us; the launch traced here: 187 us
  starting transfers between devices  68 us (36%)
  waiting for transfers between devices  52.2 us (28%)
  other arithmetic  44 us (23%)
  local copies, waits for them, and re-layouts  21.3 us (11%)
    ppermute x10, starting transfers between devices, with_halo(): lax.ppermute(head, axis, [((i + 1) % count, i) for i in range(ends)])  36.1 us
    ppermute x10, waiting for transfers between devices, with_halo(): lax.ppermute(tail, axis, [(i, (i + 1) % count) for i in range(ends)])  34.3 us
    ppermute x10, starting transfers between devices, with_halo(): lax.ppermute(tail, axis, [(i, (i + 1) % count) for i in range(ends)])  31.8 us
    concatenate x12, other arithmetic, with_halo(): jnp.concatenate([lax.ppermute(tail, axis, [(i, (i + 1) % count) for i in...  18.8 us
    ppermute x10, waiting for transfers between devices, with_halo(): lax.ppermute(head, axis, [((i + 1) % count, i) for i in range(ends)])  17.9 us
    mul x4, other arithmetic, accelerate(): (offset(padded, 0, 1, 1) - offset(padded, 0, 1, -1) - offset(padded, 0, -...  9.22 us
    unnamed x38, local copies, waits for them, and re-layouts  5.83 us
    another operation x4, local copies, waits for them, and re-layouts, on_device(): ghost[:, :, None]  5.59 us
  transfers between devices with their start and end apart: 20, of which 11 were waited for; matrix products, arithmetic and copies ran while one was open for 14% of the time, Pallas kernels for 0%

commit v1 on v0

v1 whole, which is shorter than its diff:
```python
import jax
import jax.numpy as jnp
import ml_dtypes
import numpy as np
from jax import lax
from jax.experimental import pallas as pl
from jax.experimental.pallas import tpu as pltpu
from jax.sharding import PartitionSpec as P

F = 6
FZ = 40
CZ = 80
L = 128
ZP = 8
DT2 = 0.04
F32 = jnp.float32

FINE_ROWS = F * FZ * 4
COARSE_ROWS = F * CZ
BULK = 2 * F * FZ + F * CZ + 8
RIDGE_AT = 2 * F * FZ + F * CZ
TOPO_AT = RIDGE_AT + F
VM = pl.BlockSpec(memory_space=pltpu.VMEM)
PARAMS = pltpu.CompilerParams(vmem_limit_bytes=48 * 1024 * 1024)


def pool_weights():
    w = np.zeros((384, 256), np.float32)
    for n in range(384):
        if n < 256:
            w[n, n // 2] = 0.25
        else:
            k = n - 256
            w[n, 128 + (k // 2 if k < 64 else 64 + k // 2)] = 0.25
    return w.astype(ml_dtypes.bfloat16)


def spread_weights():
    w = np.zeros((256, 384), np.float32)
    for n in range(384):
        col = n if n < 320 else n - 384
        j = col // 2
        w[j % 256, n] += 0.75
        w[(j + (1 if col % 2 else -1)) % 256, n] += 0.25
    return w.astype(ml_dtypes.bfloat16)


POOL = pool_weights()
SPREAD = spread_weights()


def exact_dot(rows, weights):
    hi = rows.astype(jnp.bfloat16)
    rest = rows - hi.astype(F32)
    mid = rest.astype(jnp.bfloat16)
    low = (rest - mid.astype(F32)).astype(jnp.bfloat16)
    dot = lambda part: jnp.dot(part, weights, preferred_element_type=F32)
    return dot(hi) + (dot(mid) + dot(low))


def lanes(shape):
    return lax.broadcasted_iota(jnp.int32, shape, len(shape) - 1)


def fine_rows(f, lt, x, start=0, size=FZ):
    return pl.ds((f * FZ + start) * 4 + lt * 2 + x, size, stride=4)


def coef_rows(lt, x, start=0, size=FZ):
    return pl.ds(start * 4 + lt * 2 + x, size, stride=4)


def first_pack(fn, fo, cn, co, sf, lf, sc, lc, tp, pool, mxa, mxb, mya, myb, tmp):
    px = lax.rem(lax.axis_index("gx"), 2)
    py = lax.rem(lax.axis_index("gy"), 2)
    tmp[...] = jnp.zeros_like(tmp)
    for f in range(F):
        for lt in range(2):
            tmp[f : f + 1, lt * L : (lt + 1) * L] = fn[pl.ds((f * FZ + FZ - 1) * 4 + lt * 2, 1), :] + fn[pl.ds((f * FZ + FZ - 1) * 4 + lt * 2 + 1, 1), :]
    ridge = exact_dot(tmp[...], pool[0:256, 0:L])
    for out, row in ((mxa, 1 - px), (mxb, px)):
        for f in range(F):
            for lt in range(2):
                out[f * 80 + lt * 40 : f * 80 + lt * 40 + 40, :] = fn[fine_rows(f, lt, row), :]
        out[480:960, :] = cn[...]
        out[RIDGE_AT : RIDGE_AT + 8, :] = ridge
        for lt in range(2):
            out[TOPO_AT + lt : TOPO_AT + lt + 1, :] = tp[pl.ds(lt * 2 + row, 1), :].astype(F32)
    group = lanes((FZ, L)) >> 2
    for out, right in ((mya, 1 - py), (myb, py)):
        base = 4 * right
        acc = jnp.zeros((FZ, L), F32)
        for arr, at in ((fn, 0), (fo, 12)):
            for f in range(F):
                for x in range(2):
                    g = at + f * 2 + x
                    acc = jnp.where(group == g, pltpu.roll(arr[fine_rows(f, right, x), :], lax.rem(base + 4 * g, L), 1), acc)
        for arr, at in ((sf, 24), (lf, 26)):
            for x in range(2):
                g = at + x
                acc = jnp.where(group == g, pltpu.roll(arr[coef_rows(right, x), :], lax.rem(base + 4 * g, L), 1), acc)
        for x in range(2):
            g = 28 + x
            plane = jnp.broadcast_to(tp[pl.ds(right * 2 + x, 1), :].astype(F32), (FZ, L))
            acc = jnp.where(group == g, pltpu.roll(plane, lax.rem(base + 4 * g, L), 1), acc)
        out[0:40, :] = acc
        acc = jnp.zeros((FZ, L), F32)
        for arr, at, count in ((cn, 0, F), (co, 12, F), (sc, 24, 1), (lc, 26, 1)):
            for f in range(count):
                for h in range(2):
                    g = at + f * 2 + h
                    acc = jnp.where(group == g, pltpu.roll(arr[f * CZ + h * 40 : f * CZ + h * 40 + 40, :], lax.rem(base + 4 * g, L), 1), acc)
        out[40:80, :] = acc


def open_y(rya, ryb, fn, pool, fh, foh, sh, th, ch, coh, sch, rg, mca, mcb, tmp):
    px = lax.rem(lax.axis_index("gx"), 2)
    py = lax.rem(lax.axis_index("gy"), 2)
    lane = lanes((FZ, L))
    in_a = ((lane + 4 * py) & 127) < 4
    in_b = ((lane + 4 * (1 - py)) & 127) < 4

    def halo(g, part):
        a = pltpu.roll(rya[part * 40 : part * 40 + 40, :], lax.rem(256 - 4 * g - 4 * py, L), 1)
        b = pltpu.roll(ryb[part * 40 : part * 40 + 40, :], lax.rem(256 - 4 * g - 4 * (1 - py), L), 1)
        return jnp.where(in_a, a, jnp.where(in_b, b, 0.0))

    for q in range(12):
        fh[q] = halo(q, 0)
        foh[q] = halo(12 + q, 0)
    for q in range(4):
        sh[q] = halo(24 + q, 0)
    for x in range(2):
        th[x] = halo(28 + x, 0)[0:8, :]
    for f in range(F):
        for h in range(2):
            ch[f, h * 40 : h * 40 + 40, :] = halo(f * 2 + h, 1)
            coh[f, h * 40 : h * 40 + 40, :] = halo(12 + f * 2 + h, 1)
    for q in range(2):
        for h in range(2):
            sch[q, h * 40 : h * 40 + 40, :] = halo(24 + q * 2 + h, 1)
    tmp[...] = jnp.zeros_like(tmp)
    for f in range(F):
        for lt in range(2):
            tmp[f : f + 1, lt * L : (lt + 1) * L] = fn[pl.ds((f * FZ + FZ - 1) * 4 + lt * 2, 1), :] + fn[pl.ds((f * FZ + FZ - 1) * 4 + lt * 2 + 1, 1), :]
        tmp[f : f + 1, 2 * L : 3 * L] = fh[f * 2, 39:40, :] + fh[f * 2 + 1, 39:40, :]
    rg[...] = exact_dot(tmp[...], pool[...])
    group = lane >> 3
    for out, row in ((mca, 1 - px), (mcb, px)):
        acc = jnp.zeros((FZ, L), F32)
        for f in range(F):
            acc = jnp.where(group == f, pltpu.roll(fh[f * 2 + row], 4 + 8 * f, 1), acc)
        acc = jnp.where(group == 6, pltpu.roll(jnp.broadcast_to(th[row, 0:1, :], (FZ, L)), 4 + 8 * 6, 1), acc)
        for f in range(F):
            g = 7 + f
            acc = jnp.where(group == g, pltpu.roll(jnp.broadcast_to(rg[f : f + 1, L : 2 * L], (FZ, L)), 4 + 8 * g, 1), acc)
        out[0:40, :] = acc
    acc = jnp.zeros((FZ, L), F32)
    for f in range(F):
        for h in range(2):
            g = f * 2 + h
            acc = jnp.where(group == g, pltpu.roll(ch[f, h * 40 : h * 40 + 40, :], (4 + 8 * g) % L, 1), acc)
    mca[40:80, :] = acc
    mcb[40:80, :] = acc


def ring_sum_diff(tiles_sum, tiles_diff, lane):
    def shifted(tiles):
        up = [pltpu.roll(t, L - 1, 1) for t in tiles]
        down = [pltpu.roll(t, 1, 1) for t in tiles]
        n = len(tiles)
        up = [jnp.where(lane < L - 1, up[t], up[(t + 1) % n]) for t in range(n)]
        down = [jnp.where(lane > 0, down[t], down[(t - 1) % n]) for t in range(n)]
        return up, down

    a, b = shifted(tiles_sum)
    c, d = shifted(tiles_diff)
    return [p + q for p, q in zip(a, b)], [p - q for p, q in zip(c, d)]


def vector_piece(load, own, nt, inv2j, invjj, h, lane):
    ia = 1.0 / (h * h)
    q = 0.25 * ia
    s = 0.5 / h
    cache = {}

    def u(i, r, t, dz=0):
        key = (i, r, t, dz)
        if key not in cache:
            cache[key] = load(i, r, t, dz)
        return cache[key]

    grads = {}

    def g(i, r, t):
        key = (i, r, t)
        if key not in grads:
            grads[key] = (u(i, r, t, 1) - u(i, r, t, -1)) * (inv2j(r, t) * s)
        return grads[key]

    out = {}
    ts = range(nt)
    for r in own:
        inner = (
            [q * (u(1, r + 1, t) - u(1, r - 1, t)) for t in ts],
            [q * (u(0, r + 1, t) - u(0, r - 1, t)) + g(2, r, t) for t in ts],
            [g(1, r, t) for t in ts],
        )
        for i in range(3):
            side, mixed = ring_sum_diff([u(i, r, t) for t in ts], inner[i], lane)
            for t in ts:
                c = u(i, r, t)
                c2 = c + c
                xx = (u(i, r + 1, t) + u(i, r - 1, t) - c2) * ia
                yy = (side[t] - c2) * ia
                zz = (u(i, r, t, 1) + u(i, r, t, -1) - c2) * invjj(r, t)
                cross = mixed[t]
                if i == 0:
                    cross = cross + (g(2, r + 1, t) - g(2, r - 1, t))
                if i == 2:
                    cross = cross + (g(0, r + 1, t) - g(0, r - 1, t))
                out[i, r, t] = (c2, xx + yy + zz, (xx, yy, zz)[i] + cross)
    return out


def interpolate(cc, spread, edges, lane8):
    left, right, low, high = edges
    a, b, c = cc[0], cc[1], cc[2]
    zero = jnp.zeros_like(a)
    mixes = [
        jnp.where(left, 0.75 * a + 0.25 * b, zero),
        0.75 * b + 0.25 * a,
        0.75 * b + 0.25 * c,
        jnp.where(right, 0.75 * c + 0.25 * b, zero),
    ]
    plane = exact_dot(jnp.concatenate(mixes, axis=0), spread[...])
    keep = (lane8 < 2 * L) | ((lane8 < 2 * L + 64) & high) | ((lane8 >= 2 * L + 64) & low)
    return jnp.where(keep, plane, 0.0)


def edges_here():
    x, y = lax.axis_index("gx"), lax.axis_index("gy")
    return x > 0, x < lax.axis_size("gx") - 1, y > 0, y < lax.axis_size("gy") - 1


def fill_ghosts(U, V, cc, spread, edges):
    for f in range(F):
        for r in range(3):
            for t in range(2):
                cc[r, f : f + 1, t * L : (t + 1) * L] = V[f, r, t, ZP : ZP + 1, :]
    plane = interpolate(cc, spread, edges, lanes((32, 384)))
    for f in range(F):
        for r in range(4):
            for t in range(3):
                U[f, r, t, ZP + FZ : ZP + FZ + 1, :] = plane[r * 8 + f : r * 8 + f + 1, t * L : (t + 1) * L]
                U[f, r, t, ZP - 1 : ZP, :] = U[f, r, t, ZP : ZP + 1, :]
        for r in range(3):
            for t in range(2):
                V[f, r, t, ZP + CZ : ZP + CZ + 1, :] = jnp.zeros((1, L), F32)


def step_one(
    fn, fo, cn, co, sf, lf, sc, lc, tp, fh, foh, sh, th, ch, coh, sch, rg, rxa, rxb, rca, rcb, spread, pool,
    f1, c1, rg1, mxa, mxb, jv, cf, cv, U, V, cc, tmp,
):
    px = lax.rem(lax.axis_index("gx"), 2)
    edges = edges_here()
    lane = lanes((8, L))
    lane40 = lanes((FZ, L))
    near40 = ((lane40 + 4) & 127) < 8

    def corner(rc, part, g):
        return jnp.where(near40, pltpu.roll(rc[part * 40 : part * 40 + 40, :], (2 * L - 4 - 8 * g) % L, 1), 0.0)

    cc[...] = jnp.zeros_like(cc)
    body = slice(ZP, ZP + FZ)
    for f in range(F):
        for x in range(2):
            for t in range(2):
                U[f, 1 + x, t, body, :] = fn[fine_rows(f, t, x), :]
            U[f, 1 + x, 2, body, :] = fh[f * 2 + x]
        V[f, 1, 0, ZP : ZP + CZ, :] = cn[f * CZ : (f + 1) * CZ, :]
        V[f, 1, 1, ZP : ZP + CZ, :] = ch[f]
        for t in range(2):
            V[f, 1, t, ZP - 1 : ZP, :] = rg[f : f + 1, t * L : (t + 1) * L]
    for rx, rc, fr, cr in ((rxa, rca, 3 * (1 - px), 2 * (1 - px)), (rxb, rcb, 3 * px, 2 * px)):
        for f in range(F):
            for t in range(2):
                U[f, fr, t, body, :] = rx[f * 80 + t * 40 : f * 80 + t * 40 + 40, :]
            U[f, fr, 2, body, :] = corner(rc, 0, f)
            V[f, cr, 0, ZP : ZP + CZ, :] = rx[480 + f * CZ : 480 + (f + 1) * CZ, :]
            for half in range(2):
                V[f, cr, 1, ZP + half * 40 : ZP + half * 40 + 40, :] = corner(rc, 1, f * 2 + half)
            V[f, cr, 0, ZP - 1 : ZP, :] = rx[RIDGE_AT + f : RIDGE_AT + f + 1, :]
            V[f, cr, 1, ZP - 1 : ZP, :] = corner(rc, 0, 7 + f)[0:1, :]
        for t in range(2):
            jv[0, fr, t] = jnp.broadcast_to(rx[TOPO_AT + t : TOPO_AT + t + 1, :], (8, L))
        jv[0, fr, 2] = corner(rc, 0, 6)[0:8, :]
    for x in range(2):
        for t in range(2):
            jv[0, 1 + x, t] = jnp.broadcast_to(tp[t * 2 + x : t * 2 + x + 1, :].astype(F32), (8, L))
        jv[0, 1 + x, 2] = th[x]
    for r in range(4):
        for t in range(3):
            spacing = 1.0 + jv[0, r, t] * (1.0 / 1024.0)
            jv[0, r, t] = 1.0 / (2.0 * spacing)
            jv[1, r, t] = 1.0 / (spacing * spacing)
    for x in range(2):
        for t in range(3):
            shear = sf[coef_rows(t, x), :] if t < 2 else sh[x]
            lame = lf[coef_rows(t, x), :] if t < 2 else sh[2 + x]
            cf[0, x, t] = DT2 * shear
            cf[1, x, t] = DT2 * (lame + shear)
    for t in range(2):
        shear = sc[...] if t == 0 else sch[0]
        lame = lc[...] if t == 0 else sch[1]
        cv[0, t] = DT2 * shear
        cv[1, t] = DT2 * (lame + shear)
    fill_ghosts(U, V, cc, spread, edges)
    keep = ((lane < 64) & edges[3]) | ((lane >= 64) & edges[2])

    def fine(a, _):
        for k in range(FZ // 8):
            at = ZP + 8 * k
            parts = vector_piece(
                lambda i, r, t, dz: U[a * 3 + i, r, t, at + dz : at + dz + 8, :], (1, 2), 3,
                lambda r, t: jv[0, r, t], lambda r, t: jv[1, r, t], 1.0, lane,
            )
            for (i, r, t), (c2, lap, gd) in parts.items():
                x = r - 1
                zs = slice(8 * k, 8 * k + 8)
                old = fo[fine_rows(a * 3 + i, t, x, 8 * k, 8), :] if t < 2 else foh[(a * 3 + i) * 2 + x, zs, :]
                new = c2 - old + cf[0, x, t, zs, :] * lap + cf[1, x, t, zs, :] * gd
                f1[(a * 3 + i) * 2 + x, t, zs, :] = new if t < 2 else jnp.where(keep, new, 0.0)
        return 0

    def coarse(a, _):
        for k in range(CZ // 8):
            at = ZP + 8 * k
            parts = vector_piece(
                lambda i, r, t, dz: V[a * 3 + i, r, t, at + dz : at + dz + 8, :], (1,), 2,
                lambda r, t: 0.25, lambda r, t: 0.25, 2.0, lane,
            )
            for (i, r, t), (c2, lap, gd) in parts.items():
                zs = slice(8 * k, 8 * k + 8)
                old = co[pl.ds((a * 3 + i) * CZ + 8 * k, 8), :] if t == 0 else coh[a * 3 + i, zs, :]
                new = c2 - old + cv[0, t, zs, :] * lap + cv[1, t, zs, :] * gd
                c1[a * 3 + i, t, zs, :] = new if t == 0 else jnp.where(keep, new, 0.0)
        return 0

    lax.fori_loop(0, 2, fine, 0)
    lax.fori_loop(0, 2, coarse, 0)
    tmp[...] = jnp.zeros_like(tmp)
    for f in range(F):
        for t in range(3):
            tmp[f : f + 1, t * L : (t + 1) * L] = f1[f * 2, t, FZ - 1 : FZ, :] + f1[f * 2 + 1, t, FZ - 1 : FZ, :]
    rg1[...] = exact_dot(tmp[...], pool[...])
    group = lane40 >> 2
    low = jnp.zeros((FZ, L), F32)
    for f in range(F):
        for half in range(2):
            g = 6 + 2 * f + half
            low = jnp.where(group == g, pltpu.roll(c1[f, 1, half * 40 : half * 40 + 40, :], 2 + 4 * g, 1), low)
    for out, row in ((mxa, 1 - px), (mxb, px)):
        acc = low
        for f in range(F):
            for t in range(2):
                out[f * 80 + t * 40 : f * 80 + t * 40 + 40, :] = f1[f * 2 + row, t]
            out[480 + f * CZ : 480 + (f + 1) * CZ, :] = c1[f, 0]
            acc = jnp.where(group == f, pltpu.roll(f1[f * 2 + row, 2], 2 + 4 * f, 1), acc)
        out[RIDGE_AT : RIDGE_AT + 8, :] = rg1[:, 0:L]
        out[BULK : BULK + 40, :] = acc


def step_two(fn, cn, f1, c1, rg1, rxa, rxb, jv, cf, cv, spread, fout, cout, fk, ck, U, V, cc):
    px = lax.rem(lax.axis_index("gx"), 2)
    edges = edges_here()
    lane = lanes((8, L))
    lane40 = lanes((FZ, L))
    near40 = ((lane40 + 2) & 127) < 4

    def corner(rx, g):
        return jnp.where(near40, pltpu.roll(rx[BULK : BULK + 40, :], (2 * L - 2 - 4 * g) % L, 1), 0.0)

    cc[...] = jnp.zeros_like(cc)
    body = slice(ZP, ZP + FZ)
    for f in range(F):
        for x in range(2):
            for t in range(3):
                U[f, 1 + x, t, body, :] = f1[f * 2 + x, t]
        for t in range(2):
            V[f, 1, t, ZP : ZP + CZ, :] = c1[f, t]
            V[f, 1, t, ZP - 1 : ZP, :] = rg1[f : f + 1, t * L : (t + 1) * L]
    for rx, fr, cr in ((rxa, 3 * (1 - px), 2 * (1 - px)), (rxb, 3 * px, 2 * px)):
        for f in range(F):
            for t in range(2):
                U[f, fr, t, body, :] = rx[f * 80 + t * 40 : f * 80 + t * 40 + 40, :]
            U[f, fr, 2, body, :] = corner(rx, f)
            V[f, cr, 0, ZP : ZP + CZ, :] = rx[480 + f * CZ : 480 + (f + 1) * CZ, :]
            for half in range(2):
                V[f, cr, 1, ZP + half * 40 : ZP + half * 40 + 40, :] = corner(rx, 6 + f * 2 + half)
            V[f, cr, 0, ZP - 1 : ZP, :] = rx[RIDGE_AT + f : RIDGE_AT + f + 1, :]
            V[f, cr, 1, ZP - 1 : ZP, :] = jnp.zeros((1, L), F32)
    fill_ghosts(U, V, cc, spread, edges)

    def fine(a, _):
        for k in range(FZ // 8):
            at = ZP + 8 * k
            parts = vector_piece(
                lambda i, r, t, dz: U[a * 3 + i, r, t, at + dz : at + dz + 8, :], (1, 2), 3,
                lambda r, t: jv[0, r, t], lambda r, t: jv[1, r, t], 1.0, lane,
            )
            for (i, r, t), (c2, lap, gd) in parts.items():
                if t < 2:
                    x = r - 1
                    zs = slice(8 * k, 8 * k + 8)
                    rows = fine_rows(a * 3 + i, t, x, 8 * k, 8)
                    fout[rows, :] = c2 - fn[rows, :] + cf[0, x, t, zs, :] * lap + cf[1, x, t, zs, :] * gd
        return 0

    def coarse(a, _):
        for k in range(CZ // 8):
            at = ZP + 8 * k
            parts = vector_piece(
                lambda i, r, t, dz: V[a * 3 + i, r, t, at + dz : at + dz + 8, :], (1,), 2,
                lambda r, t: 0.25, lambda r, t: 0.25, 2.0, lane,
            )
            for (i, r, t), (c2, lap, gd) in parts.items():
                if t == 0:
                    zs = slice(8 * k, 8 * k + 8)
                    rows = pl.ds((a * 3 + i) * CZ + 8 * k, 8)
                    cout[rows, :] = c2 - cn[rows, :] + cv[0, t, zs, :] * lap + cv[1, t, zs, :] * gd
        return 0

    lax.fori_loop(0, 2, fine, 0)
    lax.fori_loop(0, 2, coarse, 0)
    for x in range(2):
        for t in range(2):
            total = jnp.zeros((FZ, L), F32)
            for i in range(3):
                total = total + f1[i * 2 + x, t] * f1[(3 + i) * 2 + x, t]
            for i in range(3):
                total = total + fout[fine_rows(i, t, x), :] * fout[fine_rows(3 + i, t, x), :]
            fk[coef_rows(t, x), :] = total
    total = jnp.zeros((CZ, L), F32)
    for i in range(3):
        total = total + c1[i, 0] * c1[3 + i, 0]
    for i in range(3):
        total = total + cout[i * CZ : (i + 1) * CZ, :] * cout[(3 + i) * CZ : (4 + i) * CZ, :]
    ck[...] = total


def call(kernel, args, outs, scratch):
    shapes = tuple(jax.ShapeDtypeStruct(s, F32) for s in outs)
    return pl.pallas_call(
        kernel,
        out_shape=shapes,
        in_specs=[VM] * len(args),
        out_specs=(VM,) * len(outs),
        scratch_shapes=[pltpu.VMEM(s, F32) for s in scratch],
        compiler_params=PARAMS,
    )(*args)


def swap(cells, axis, first):
    count = lax.axis_size(axis)
    return lax.ppermute(cells, axis, [p for i in range(first, count - 1, 2) for p in ((i, i + 1), (i + 1, i))])


def rows_of(array):
    lead = array.size // 512
    return array.reshape(lead, 2, 2, L).transpose(0, 2, 1, 3).reshape(lead * 4, L)


def fine_of(rows, shape):
    return rows.reshape(-1, 2, 2, L).transpose(0, 2, 1, 3).reshape(shape)


def on_device(fine_old, fine_now, coarse_old, coarse_now, shear_fine, lame_fine, shear_coarse, lame_coarse, topography):
    fo, fn, sf, lf = rows_of(fine_old), rows_of(fine_now), rows_of(shear_fine), rows_of(lame_fine)
    tp = rows_of(topography)
    co, cn = coarse_old.reshape(-1, L), coarse_now.reshape(-1, L)
    sc, lc = shear_coarse.reshape(-1, L), lame_coarse.reshape(-1, L)
    pool, spread = jnp.asarray(POOL), jnp.asarray(SPREAD)
    mxa, mxb, mya, myb = call(first_pack, (fn, fo, cn, co, sf, lf, sc, lc, tp, pool), ((BULK, L), (BULK, L), (80, L), (80, L)), ((8, 256),))
    rxb = swap(mxb, "gx", 1)
    ryb = swap(myb, "gy", 1)
    rya = swap(mya, "gy", 0)
    rxa = swap(mxa, "gx", 0)
    fh, foh, sh, th, ch, coh, sch, rg, mca, mcb = call(
        open_y,
        (rya, ryb, fn, pool),
        ((12, FZ, L), (12, FZ, L), (4, FZ, L), (2, 8, L), (F, CZ, L), (F, CZ, L), (2, CZ, L), (8, 256), (80, L), (80, L)),
        ((8, 384),),
    )
    rcb = swap(mcb, "gx", 1)
    rca = swap(mca, "gx", 0)
    field = ((F, 4, 3, 56, L), (F, 3, 2, 96, L), (3, 8, 256))
    f1, c1, rg1, mxa, mxb, jv, cf, cv = call(
        step_one,
        (fn, fo, cn, co, sf, lf, sc, lc, tp, fh, foh, sh, th, ch, coh, sch, rg, rxa, rxb, rca, rcb, spread, pool),
        ((12, 3, FZ, L), (F, 2, CZ, L), (8, 256), (BULK + 40, L), (BULK + 40, L), (2, 4, 3, 8, L), (2, 2, 3, FZ, L), (2, 2, CZ, L)),
        field + ((8, 384),),
    )
    rxb = swap(mxb, "gx", 1)
    rxa = swap(mxa, "gx", 0)
    fout, cout, fk, ck = call(
        step_two,
        (fn, cn, f1, c1, rg1, rxa, rxb, jv, cf, cv, spread),
        ((FINE_ROWS, L), (COARSE_ROWS, L), (4 * FZ, L), (CZ, L)),
        field,
    )
    return (
        fine_of(fout, fine_now.shape),
        cout.reshape(coarse_now.shape),
        fine_of(fk, shear_fine.shape),
        ck.reshape(shear_coarse.shape),
    )


def solution(mesh):
    fields = P(None, None, None, "gx", "gy")
    cells = P(None, "gx", "gy")
    return jax.shard_map(
        on_device,
        mesh=mesh,
        in_specs=(fields, fields, fields, fields, cells, cells, cells, cells, P("gx", "gy")),
        out_specs=(fields, fields, cells, cells),
        check_vma=False,
    )
```

time: 188 us -> 63.3 us (0.34)
  the two profiles are of different devices: /device:TPU:127 before, /device:TPU:153 now
where the time goes in v1:
time: 63.3 us; the launch traced here: 62.6 us
  waiting for transfers between devices  27.2 us (43%)
  starting transfers between devices  16.7 us (26%)
  local copies, waits for them, and re-layouts  10 us (16%)
  Pallas kernels  7.87 us (12%)
  between operations  0.79 us (1%)
    ppermute x8, waiting for transfers between devices, swap(): lax.ppermute(cells, axis, [p for i in range(first, count - 1, 2) for p in...  27.2 us
    ppermute x8, starting transfers between devices, swap(): lax.ppermute(cells, axis, [p for i in range(first, count - 1, 2) for p in...  16.7 us
    unnamed x36, local copies, waits for them, and re-layouts  10 us
    pallas_call x4, Pallas kernels, call(): pl.pallas_call(kernel, out_shape=shapes, in_specs=[VM] * len(args), out_s...  7.87 us
  transfers between devices with their start and end apart: 8, of which 4 were waited for; matrix products, arithmetic and copies ran while one was open for 0% of the time, Pallas kernels for 1%

profile of v1, /device:TPU:153, one launch (start us, length us, event | category | flops | bytes accessed | tf_op | source)
XLA Modules:
  0.0 62.6 jit_solution(829591791575154551)
XLA Ops:
  0.6 0.0 copy-start.17
  0.6 0.7 %copy-done.17 = s32[2,256]{1,0:T(2,128)S(1)} copy-done((s32[2,256]{1,0:T(2,128)S(1)}, s32[2,256]{1,0:T(2,128)}, u32[]{:S(2)}) %copy-start.17) | copy-done | bytes 2072
  1.3 0.0 copy-start
  1.3 1.0 %copy-done = f32[2,3,40,2,256]{4,3,2,1,0:T(2,128)S(1)} copy-done((f32[2,3,40,2,256]{4,3,2,1,0:T(2,128)S(1)}, f32[2,3,40,2,256]{4,3,2,1,0:T(2,128)}, u32[]{:S(2)}) %copy-start) | copy-done | bytes 491544
  2.3 0.0 copy-start.1
  2.3 0.9 %copy-done.1 = f32[2,3,80,1,128]{4,3,2,1,0:T(1,128)S(1)} copy-done((f32[2,3,80,1,128]{4,3,2,1,0:T(1,128)S(1)}, f32[2,3,80,1,128]{4,3,2,1,0:T(1,128)}, u32[]{:S(2)}) %copy-start.1) | copy-done | bytes 245784
  3.3 0.0 copy-start.3
  3.3 1.0 %copy-done.3 = f32[2,3,40,2,256]{4,3,2,1,0:T(2,128)S(1)} copy-done((f32[2,3,40,2,256]{4,3,2,1,0:T(2,128)S(1)}, f32[2,3,40,2,256]{4,3,2,1,0:T(2,128)}, u32[]{:S(2)}) %copy-start.3) | copy-done | bytes 491544
  4.3 0.0 copy-start.5
  4.3 0.9 %copy-done.5 = bf16[384,256]{1,0:T(8,128)(2,1)S(1)} copy-done((bf16[384,256]{1,0:T(8,128)(2,1)S(1)}, bf16[384,256]{1,0:T(8,128)(2,1)}, u32[]{:S(2)}) %copy-start.5) | copy-done | bytes 196632
  5.2 0.0 copy-start.7
  5.3 0.9 %copy-done.7 = f32[2,3,80,1,128]{4,3,2,1,0:T(1,128)S(1)} copy-done((f32[2,3,80,1,128]{4,3,2,1,0:T(1,128)S(1)}, f32[2,3,80,1,128]{4,3,2,1,0:T(1,128)}, u32[]{:S(2)}) %copy-start.7) | copy-done | bytes 245784
  6.2 0.0 copy-start.11
  6.2 0.9 %copy-done.11 = f32[40,2,256]{2,1,0:T(2,128)S(1)} copy-done((f32[40,2,256]{2,1,0:T(2,128)S(1)}, f32[40,2,256]{2,1,0:T(2,128)}, u32[]{:S(2)}) %copy-start.11) | copy-done | bytes 81944
  7.1 0.0 copy-start.13
  7.1 0.9 %copy-done.13 = f32[40,2,256]{2,1,0:T(2,128)S(1)} copy-done((f32[40,2,256]{2,1,0:T(2,128)S(1)}, f32[40,2,256]{2,1,0:T(2,128)}, u32[]{:S(2)}) %copy-start.13) | copy-done | bytes 81944
  8.0 0.0 copy-start.15
  8.0 0.8 %copy-done.15 = f32[80,1,128]{2,1,0:T(1,128)S(1)} copy-done((f32[80,1,128]{2,1,0:T(1,128)S(1)}, f32[80,1,128]{2,1,0:T(1,128)}, u32[]{:S(2)}) %copy-start.15) | copy-done | bytes 40984
  8.7 0.0 copy-start.16
  8.8 0.8 %copy-done.16 = f32[80,1,128]{2,1,0:T(1,128)S(1)} copy-done((f32[80,1,128]{2,1,0:T(1,128)S(1)}, f32[80,1,128]{2,1,0:T(1,128)}, u32[]{:S(2)}) %copy-start.16) | copy-done | bytes 40984
  9.5 0.0 copy-start.6
  9.5 0.0 copy-start.8
  9.5 0.0 copy-start.9
  9.5 0.0 copy-start.12
  9.5 0.0 copy-start.14
  9.5 0.7 %shard_map.138 = (f32[968,128]{1,0:T(8,128)S(1)}, f32[968,128]{1,0:T(8,128)S(1)}, f32[80,128]{1,0:T(8,128)S(1)}, f32[80,128]{1,0:T(8,128)S(1)}) custom-call(f32[960,128]{1,0:T(8,128)S(1)} %bitcast.45, f32[960,128]{1,0:T(8,128)S(1)} %bitcast.52, f32[480,128]{1,0:T(8,128)S(1)} %bitcast.49, f32[480,128]{1,0:T(8,128)S(1)} %bitcast.54, f32[160,128]{1,0:T(8,128)S(1)} %bitcast.56, ...), custom_call_target="tpu_custom_call" | custom-call | tf_op jit(solution)/shard_map/pallas_call | solution.py:455
  10.3 0.0 copy-start.4
  10.3 0.8 %collective-permute-start.2 = (f32[968,128]{1,0:T(8,128)S(1)}, f32[968,128]{1,0:T(8,128)S(1)}, u32[]{:S(2)}, u32[]{:S(2)}) collective-permute-start(f32[968,128]{1,0:T(8,128)S(1)} %get-tuple-element.40), channel_id=1, source_target_pairs={{0,8},{8,0},{16,24},{24,16},{32,40},{40,32},{48,56},{56,48},{64,72... | collective-permute-start | bytes 1486856 | tf_op jit(solution)/shard_map/ppermute | solution.py:467
  11.1 3.1 %collective-permute-start.3 = (f32[968,128]{1,0:T(8,128)S(1)}, f32[968,128]{1,0:T(8,128)S(1)}, u32[]{:S(2)}, u32[]{:S(2)}) collective-permute-start(f32[968,128]{1,0:T(8,128)S(1)} %get-tuple-element.41), channel_id=1, source_target_pairs={{8,16},{16,8},{24,32},{32,24},{40,48},{48,40},{56,64},{64,56},{72,... | collective-permute-start | bytes 1486856 | tf_op jit(solution)/shard_map/ppermute | solution.py:467
  14.2 2.5 %collective-permute-start = (f32[80,128]{1,0:T(8,128)S(1)}, f32[80,128]{1,0:T(8,128)S(1)}, u32[]{:S(2)}, u32[]{:S(2)}) collective-permute-start(f32[80,128]{1,0:T(8,128)S(1)} %get-tuple-element.30), channel_id=1, source_target_pairs={{0,1},{1,0},{2,3},{3,2},{4,5},{5,4},{6,7},{7,6},{8,9},{9,8},{10,11... | collective-permute-start | bytes 122888 | tf_op jit(solution)/shard_map/ppermute | solution.py:467
  16.7 0.0 copy-start.2
  16.8 2.7 %collective-permute-start.1 = (f32[80,128]{1,0:T(8,128)S(1)}, f32[80,128]{1,0:T(8,128)S(1)}, u32[]{:S(2)}, u32[]{:S(2)}) collective-permute-start(f32[80,128]{1,0:T(8,128)S(1)} %get-tuple-element.31), channel_id=1, source_target_pairs={{1,2},{2,1},{3,4},{4,3},{5,6},{6,5},{9,10},{10,9},{11,12},{12,11},... | collective-permute-start | bytes 122888 | tf_op jit(solution)/shard_map/ppermute | solution.py:467
  19.5 9.6 %collective-permute-done.rya = f32[80,128]{1,0:T(8,128)S(1)} collective-permute-done((f32[80,128]{1,0:T(8,128)S(1)}, f32[80,128]{1,0:T(8,128)S(1)}, u32[]{:S(2)}, u32[]{:S(2)}) %collective-permute-start) | collective-permute-done | bytes 40992 | tf_op jit(solution)/shard_map/ppermute | solution.py:467
  29.1 1.1 %collective-permute-done.1.ryb = f32[80,128]{1,0:T(8,128)S(1)} collective-permute-done((f32[80,128]{1,0:T(8,128)S(1)}, f32[80,128]{1,0:T(8,128)S(1)}, u32[]{:S(2)}, u32[]{:S(2)}) %collective-permute-start.1) | collective-permute-done | bytes 40992 | tf_op jit(solution)/shard_map/ppermute | solution.py:467
  30.1 0.0 copy-done.6
  30.1 0.8 %shard_map.139 = (f32[12,40,128]{2,1,0:T(8,128)S(1)}, f32[12,40,128]{2,1,0:T(8,128)S(1)}, f32[4,40,128]{2,1,0:T(8,128)S(1)}, f32[2,8,128]{2,1,0:T(8,128)S(1)}, f...) custom-call(f32[80,128]{1,0:T(8,128)S(1)} %collective-permute-done.r, ...), custom_call_target="tpu_custom_call" | custom-call | tf_op jit(solution)/shard_map/pallas_call | solution.py:455
  31.0 0.1 collective-permute-start.4
  31.1 3.0 %collective-permute-start.5 = (f32[80,128]{1,0:T(8,128)S(1)}, f32[80,128]{1,0:T(8,128)S(1)}, u32[]{:S(2)}, u32[]{:S(2)}) collective-permute-start(f32[80,128]{1,0:T(8,128)S(1)} %get-tuple-element.43), channel_id=1, source_target_pairs={{8,16},{16,8},{24,32},{32,24},{40,48},{48,40},{56,64},{64,56},{72,... | collective-permute-start | bytes 122888 | tf_op jit(solution)/shard_map/ppermute | solution.py:467
  34.0 0.0 collective-permute-done.4.rca
  34.1 2.3 %collective-permute-done.5.rcb = f32[80,128]{1,0:T(8,128)S(1)} collective-permute-done((f32[80,128]{1,0:T(8,128)S(1)}, f32[80,128]{1,0:T(8,128)S(1)}, u32[]{:S(2)}, u32[]{:S(2)}) %collective-permute-start.5) | collective-permute-done | bytes 40992 | tf_op jit(solution)/shard_map/ppermute | solution.py:467
  36.4 0.0 collective-permute-done.2.rxa
  36.4 0.0 collective-permute-done.3.rxb
  36.4 0.0 copy-done.8
  36.4 0.0 copy-done.9
  36.4 0.0 copy-done.12
  36.4 0.0 copy-done.14
  36.4 0.0 copy-done.4
  36.4 0.0 copy-done.2
  36.5 3.4 %shard_map.140 = (f32[12,3,40,128]{3,2,1,0:T(8,128)}, f32[6,2,80,128]{3,2,1,0:T(8,128)S(1)}, f32[8,256]{1,0:T(8,128)S(1)}, f32[1008,128]{1,0:T(8,128)S(1)}, f32[...) custom-call(f32[960,128]{1,0:T(8,128)S(1)} %bitcast.47, ...), custom_call_target="tpu_custom_call" | custom-call | tf_op jit(solution)/shard_map/pallas_call | solution.py:455
  39.9 2.6 %collective-permute-start.6 = (f32[1008,128]{1,0:T(8,128)S(1)}, f32[1008,128]{1,0:T(8,128)S(1)}, u32[]{:S(2)}, u32[]{:S(2)}) collective-permute-start(f32[1008,128]{1,0:T(8,128)S(1)} %get-tuple-element.47), channel_id=1, source_target_pairs={{0,8},{8,0},{16,24},{24,16},{32,40},{40,32},{48,56},{56,48},{64,72... | collective-permute-start | bytes 1548296 | tf_op jit(solution)/shard_map/ppermute | solution.py:467
  42.5 1.9 %collective-permute-start.7 = (f32[1008,128]{1,0:T(8,128)}, f32[1008,128]{1,0:T(8,128)S(1)}, u32[]{:S(2)}, u32[]{:S(2)}) collective-permute-start(f32[1008,128]{1,0:T(8,128)} %get-tuple-element.48), channel_id=1, source_target_pairs={{8,16},{16,8},{24,32},{32,24},{40,48},{48,40},{56,64},{64,56},{72,... | collective-permute-start | bytes 1548296 | tf_op jit(solution)/shard_map/ppermute | solution.py:467
  44.4 0.0 collective-permute-done.6.rxa
  44.4 14.2 %collective-permute-done.7.rxb = f32[1008,128]{1,0:T(8,128)S(1)} collective-permute-done((f32[1008,128]{1,0:T(8,128)}, f32[1008,128]{1,0:T(8,128)S(1)}, u32[]{:S(2)}, u32[]{:S(2)}) %collective-permute-start.7) | collective-permute-done | bytes 516128 | tf_op jit(solution)/shard_map/ppermute | solution.py:467
  58.6 0.0 copy-start.10
  58.6 1.1 %copy-done.10 = f32[12,3,40,128]{3,2,1,0:T(8,128)S(1)} copy-done((f32[12,3,40,128]{3,2,1,0:T(8,128)S(1)}, f32[12,3,40,128]{3,2,1,0:T(8,128)}, u32[]{:S(2)}) %copy-start.10) | copy-done | bytes 737304
  59.7 2.9 %shard_map.141 = (f32[960,128]{1,0:T(8,128)}, f32[480,128]{1,0:T(8,128)}, f32[160,128]{1,0:T(8,128)}, f32[80,128]{1,0:T(8,128)}) custom-call(f32[960,128]{1,0:T(8,128)S(1)} %bitcast.48, f32[480,128]{1,0:T(8,128)S(1)} %bitcast.51, f32[12,3,40,128]{3,2,1,0:T(8,128)S(1)} %copy-done.10, f32[6,2,80,128]{3,2,1,0:T(8,128)S(1)} %get-tuple-element.45.c1, ...), custom_call_target="tpu_custom_call" | custom-call | tf_op jit(solution)/shard_map/pallas_call | solution.py:455
Async XLA Ops:
  0.6 0.7 %copy-start.17 = (s32[2,256]{1,0:T(2,128)S(1)}, s32[2,256]{1,0:T(2,128)}, u32[]{:S(2)}) copy-start(s32[2,256]{1,0:T(2,128)} %param.19) | copy-start | bytes 6148
  1.3 1.0 %copy-start = (f32[2,3,40,2,256]{4,3,2,1,0:T(2,128)S(1)}, f32[2,3,40,2,256]{4,3,2,1,0:T(2,128)}, u32[]{:S(2)}) copy-start(f32[2,3,40,2,256]{4,3,2,1,0:T(2,128)} %param.12) | copy-start | bytes 1474564
  2.3 0.9 %copy-start.1 = (f32[2,3,80,1,128]{4,3,2,1,0:T(1,128)S(1)}, f32[2,3,80,1,128]{4,3,2,1,0:T(1,128)}, u32[]{:S(2)}) copy-start(f32[2,3,80,1,128]{4,3,2,1,0:T(1,128)} %param.14) | copy-start | bytes 737284
  3.3 1.0 %copy-start.3 = (f32[2,3,40,2,256]{4,3,2,1,0:T(2,128)S(1)}, f32[2,3,40,2,256]{4,3,2,1,0:T(2,128)}, u32[]{:S(2)}) copy-start(f32[2,3,40,2,256]{4,3,2,1,0:T(2,128)} %param.11) | copy-start | bytes 1474564
  4.3 0.9 %copy-start.5 = (bf16[384,256]{1,0:T(8,128)(2,1)S(1)}, bf16[384,256]{1,0:T(8,128)(2,1)}, u32[]{:S(2)}) copy-start(bf16[384,256]{1,0:T(8,128)(2,1)} %constant.4.clone.pool) | copy-start | bytes 589828
  5.2 0.9 %copy-start.7 = (f32[2,3,80,1,128]{4,3,2,1,0:T(1,128)S(1)}, f32[2,3,80,1,128]{4,3,2,1,0:T(1,128)}, u32[]{:S(2)}) copy-start(f32[2,3,80,1,128]{4,3,2,1,0:T(1,128)} %param.13) | copy-start | bytes 737284
  6.2 0.9 %copy-start.11 = (f32[40,2,256]{2,1,0:T(2,128)S(1)}, f32[40,2,256]{2,1,0:T(2,128)}, u32[]{:S(2)}) copy-start(f32[40,2,256]{2,1,0:T(2,128)} %param.15) | copy-start | bytes 245764
  7.1 0.9 %copy-start.13 = (f32[40,2,256]{2,1,0:T(2,128)S(1)}, f32[40,2,256]{2,1,0:T(2,128)}, u32[]{:S(2)}) copy-start(f32[40,2,256]{2,1,0:T(2,128)} %param.16) | copy-start | bytes 245764
  8.0 0.8 %copy-start.15 = (f32[80,1,128]{2,1,0:T(1,128)S(1)}, f32[80,1,128]{2,1,0:T(1,128)}, u32[]{:S(2)}) copy-start(f32[80,1,128]{2,1,0:T(1,128)} %param.17) | copy-start | bytes 122884
  8.7 0.8 %copy-start.16 = (f32[80,1,128]{2,1,0:T(1,128)S(1)}, f32[80,1,128]{2,1,0:T(1,128)}, u32[]{:S(2)}) copy-start(f32[80,1,128]{2,1,0:T(1,128)} %param.18) | copy-start | bytes 122884
  9.5 20.6 %copy-start.6 = (bf16[384,256]{1,0:T(8,128)(2,1)S(1)}, bf16[384,256]{1,0:T(8,128)(2,1)}, u32[]{:S(2)}) copy-start(bf16[384,256]{1,0:T(8,128)(2,1)} %constant.4.clone.pool) | copy-start | bytes 589828
  9.5 26.9 %copy-start.8 = (f32[2,3,80,1,128]{4,3,2,1,0:T(1,128)S(1)}, f32[2,3,80,1,128]{4,3,2,1,0:T(1,128)}, u32[]{:S(2)}) copy-start(f32[2,3,80,1,128]{4,3,2,1,0:T(1,128)} %param.13) | copy-start | bytes 737284
  9.5 26.9 %copy-start.9 = (bf16[256,384]{1,0:T(8,128)(2,1)S(1)}, bf16[256,384]{1,0:T(8,128)(2,1)}, u32[]{:S(2)}) copy-start(bf16[256,384]{1,0:T(8,128)(2,1)} %constant.5.clone.spread) | copy-start | bytes 589828
  9.5 26.9 %copy-start.12 = (f32[40,2,256]{2,1,0:T(2,128)S(1)}, f32[40,2,256]{2,1,0:T(2,128)}, u32[]{:S(2)}) copy-start(f32[40,2,256]{2,1,0:T(2,128)} %param.15) | copy-start | bytes 245764
  9.5 26.9 %copy-start.14 = (f32[40,2,256]{2,1,0:T(2,128)S(1)}, f32[40,2,256]{2,1,0:T(2,128)}, u32[]{:S(2)}) copy-start(f32[40,2,256]{2,1,0:T(2,128)} %param.16) | copy-start | bytes 245764
  10.3 26.2 %copy-start.4 = (f32[2,3,40,2,256]{4,3,2,1,0:T(2,128)S(1)}, f32[2,3,40,2,256]{4,3,2,1,0:T(2,128)}, u32[]{:S(2)}) copy-start(f32[2,3,40,2,256]{4,3,2,1,0:T(2,128)} %param.11) | copy-start | bytes 1474564
  10.3 26.1 %collective-permute-start.2 = (f32[968,128]{1,0:T(8,128)S(1)}, f32[968,128]{1,0:T(8,128)S(1)}, u32[]{:S(2)}, u32[]{:S(2)}) collective-permute-start(f32[968,128]{1,0:T(8,128)S(1)} %get-tuple-element.40), channel_id=1, source_target_pairs={{0,8},{8,0},{16,24},{24,16},{32,40},{40,32},{48,56},{56,48},{64,72... | collective-permute-start | bytes 1486856 | tf_op jit(solution)/shard_map/ppermute | solution.py:467
  11.1 25.3 %collective-permute-start.3 = (f32[968,128]{1,0:T(8,128)S(1)}, f32[968,128]{1,0:T(8,128)S(1)}, u32[]{:S(2)}, u32[]{:S(2)}) collective-permute-start(f32[968,128]{1,0:T(8,128)S(1)} %get-tuple-element.41), channel_id=1, source_target_pairs={{8,16},{16,8},{24,32},{32,24},{40,48},{48,40},{56,64},{64,56},{72,... | collective-permute-start | bytes 1486856 | tf_op jit(solution)/shard_map/ppermute | solution.py:467
  14.2 14.9 %collective-permute-start = (f32[80,128]{1,0:T(8,128)S(1)}, f32[80,128]{1,0:T(8,128)S(1)}, u32[]{:S(2)}, u32[]{:S(2)}) collective-permute-start(f32[80,128]{1,0:T(8,128)S(1)} %get-tuple-element.30), channel_id=1, source_target_pairs={{0,1},{1,0},{2,3},{3,2},{4,5},{5,4},{6,7},{7,6},{8,9},{9,8},{10,11... | collective-permute-start | bytes 122888 | tf_op jit(solution)/shard_map/ppermute | solution.py:467
  16.7 19.7 %copy-start.2 = (f32[2,3,80,1,128]{4,3,2,1,0:T(1,128)S(1)}, f32[2,3,80,1,128]{4,3,2,1,0:T(1,128)}, u32[]{:S(2)}) copy-start(f32[2,3,80,1,128]{4,3,2,1,0:T(1,128)} %param.14) | copy-start | bytes 737284
  16.8 13.4 %collective-permute-start.1 = (f32[80,128]{1,0:T(8,128)S(1)}, f32[80,128]{1,0:T(8,128)S(1)}, u32[]{:S(2)}, u32[]{:S(2)}) collective-permute-start(f32[80,128]{1,0:T(8,128)S(1)} %get-tuple-element.31), channel_id=1, source_target_pairs={{1,2},{2,1},{3,4},{4,3},{5,6},{6,5},{9,10},{10,9},{11,12},{12,11},... | collective-permute-start | bytes 122888 | tf_op jit(solution)/shard_map/ppermute | solution.py:467
  31.0 3.1 %collective-permute-start.4 = (f32[80,128]{1,0:T(8,128)S(1)}, f32[80,128]{1,0:T(8,128)S(1)}, u32[]{:S(2)}, u32[]{:S(2)}) collective-permute-start(f32[80,128]{1,0:T(8,128)S(1)} %get-tuple-element.42), channel_id=1, source_target_pairs={{0,8},{8,0},{16,24},{24,16},{32,40},{40,32},{48,56},{56,48},{64,72... | collective-permute-start | bytes 122888 | tf_op jit(solution)/shard_map/ppermute | solution.py:467
  31.1 5.3 %collective-permute-start.5 = (f32[80,128]{1,0:T(8,128)S(1)}, f32[80,128]{1,0:T(8,128)S(1)}, u32[]{:S(2)}, u32[]{:S(2)}) collective-permute-start(f32[80,128]{1,0:T(8,128)S(1)} %get-tuple-element.43), channel_id=1, source_target_pairs={{8,16},{16,8},{24,32},{32,24},{40,48},{48,40},{56,64},{64,56},{72,... | collective-permute-start | bytes 122888 | tf_op jit(solution)/shard_map/ppermute | solution.py:467
  39.9 4.5 %collective-permute-start.6 = (f32[1008,128]{1,0:T(8,128)S(1)}, f32[1008,128]{1,0:T(8,128)S(1)}, u32[]{:S(2)}, u32[]{:S(2)}) collective-permute-start(f32[1008,128]{1,0:T(8,128)S(1)} %get-tuple-element.47), channel_id=1, source_target_pairs={{0,8},{8,0},{16,24},{24,16},{32,40},{40,32},{48,56},{56,48},{64,72... | collective-permute-start | bytes 1548296 | tf_op jit(solution)/shard_map/ppermute | solution.py:467
  42.5 16.1 %collective-permute-start.7 = (f32[1008,128]{1,0:T(8,128)}, f32[1008,128]{1,0:T(8,128)S(1)}, u32[]{:S(2)}, u32[]{:S(2)}) collective-permute-start(f32[1008,128]{1,0:T(8,128)} %get-tuple-element.48), channel_id=1, source_target_pairs={{8,16},{16,8},{24,32},{32,24},{40,48},{48,40},{56,64},{64,56},{72,... | collective-permute-start | bytes 1548296 | tf_op jit(solution)/shard_map/ppermute | solution.py:467
  58.6 1.1 %copy-start.10 = (f32[12,3,40,128]{3,2,1,0:T(8,128)S(1)}, f32[12,3,40,128]{3,2,1,0:T(8,128)}, u32[]{:S(2)}) copy-start(f32[12,3,40,128]{3,2,1,0:T(8,128)} %get-tuple-element.44.f1) | copy-start | bytes 2211844

commit v2 on v1

--- a/solution.py
+++ b/solution.py
@@ -17,11 +17,12 @@
 
 FINE_ROWS = F * FZ * 4
 COARSE_ROWS = F * CZ
-BULK = 2 * F * FZ + F * CZ + 8
-RIDGE_AT = 2 * F * FZ + F * CZ
+RIDGE_AT = 2 * F * FZ
 TOPO_AT = RIDGE_AT + F
+COARSE_AT = RIDGE_AT + 8
+NEAR = COARSE_AT
+BULK = COARSE_AT + COARSE_ROWS
 VM = pl.BlockSpec(memory_space=pltpu.VMEM)
-PARAMS = pltpu.CompilerParams(vmem_limit_bytes=48 * 1024 * 1024)
 
 
 def pool_weights():
@@ -70,22 +71,16 @@
     return pl.ds(start * 4 + lt * 2 + x, size, stride=4)
 
 
-def first_pack(fn, fo, cn, co, sf, lf, sc, lc, tp, pool, mxa, mxb, mya, myb, tmp):
-    px = lax.rem(lax.axis_index("gx"), 2)
+def load_and_pack_y(*refs):
+    n = 11
+    hbm, (fn, fo, cn, co, sf, lf, sc, lc, tp, pool, spread), (mxb, mya, myb, tmp, sems) = refs[:n], refs[n : 2 * n], refs[2 * n :]
+    copies = [pltpu.make_async_copy(src, dst, sems.at[q]) for q, (src, dst) in enumerate(zip(hbm, refs[n : 2 * n]))]
+    for copy in copies:
+        copy.start()
+    for copy in copies:
+        copy.wait()
+    pack_x(fn, cn, tp, pool, mxb, tmp)
     py = lax.rem(lax.axis_index("gy"), 2)
-    tmp[...] = jnp.zeros_like(tmp)
-    for f in range(F):
-        for lt in range(2):
-            tmp[f : f + 1, lt * L : (lt + 1) * L] = fn[pl.ds((f * FZ + FZ - 1) * 4 + lt * 2, 1), :] + fn[pl.ds((f * FZ + FZ - 1) * 4 + lt * 2 + 1, 1), :]
-    ridge = exact_dot(tmp[...], pool[0:256, 0:L])
-    for out, row in ((mxa, 1 - px), (mxb, px)):
-        for f in range(F):
-            for lt in range(2):
-                out[f * 80 + lt * 40 : f * 80 + lt * 40 + 40, :] = fn[fine_rows(f, lt, row), :]
-        out[480:960, :] = cn[...]
-        out[RIDGE_AT : RIDGE_AT + 8, :] = ridge
-        for lt in range(2):
-            out[TOPO_AT + lt : TOPO_AT + lt + 1, :] = tp[pl.ds(lt * 2 + row, 1), :].astype(F32)
     group = lanes((FZ, L)) >> 2
     for out, right in ((mya, 1 - py), (myb, py)):
         base = 4 * right
@@ -113,7 +108,31 @@
         out[40:80, :] = acc
 
 
-def open_y(rya, ryb, fn, pool, fh, foh, sh, th, ch, coh, sch, rg, mca, mcb, tmp):
+def bottom_sums(fn, tmp):
+    for f in range(F):
+        for lt in range(2):
+            at = (f * FZ + FZ - 1) * 4 + lt * 2
+            tmp[f : f + 1, lt * L : (lt + 1) * L] = fn[at : at + 1, :] + fn[at + 1 : at + 2, :]
+
+
+def near_row(fn, tp, row, ridge, out):
+    for f in range(F):
+        for lt in range(2):
+            out[f * 80 + lt * 40 : f * 80 + lt * 40 + 40, :] = fn[fine_rows(f, lt, row), :]
+    out[RIDGE_AT : RIDGE_AT + 8, :] = ridge
+    for lt in range(2):
+        out[TOPO_AT + lt : TOPO_AT + lt + 1, :] = tp[pl.ds(lt * 2 + row, 1), :].astype(F32)
+
+
+def pack_x(fn, cn, tp, pool, mxb, tmp):
+    px = lax.rem(lax.axis_index("gx"), 2)
+    tmp[...] = jnp.zeros_like(tmp)
+    bottom_sums(fn, tmp)
+    near_row(fn, tp, px, exact_dot(tmp[...], pool[0:256, 0:L]), mxb)
+    mxb[COARSE_AT : COARSE_AT + COARSE_ROWS, :] = cn[...]
+
+
+def open_y(rya, ryb, fn, tp, pool, fh, foh, sh, th, ch, coh, sch, rg, mxa, mcb, tmp):
     px = lax.rem(lax.axis_index("gx"), 2)
     py = lax.rem(lax.axis_index("gy"), 2)
     lane = lanes((FZ, L))
@@ -140,13 +159,13 @@
         for h in range(2):
             sch[q, h * 40 : h * 40 + 40, :] = halo(24 + q * 2 + h, 1)
     tmp[...] = jnp.zeros_like(tmp)
-    for f in range(F):
-        for lt in range(2):
-            tmp[f : f + 1, lt * L : (lt + 1) * L] = fn[pl.ds((f * FZ + FZ - 1) * 4 + lt * 2, 1), :] + fn[pl.ds((f * FZ + FZ - 1) * 4 + lt * 2 + 1, 1), :]
+    bottom_sums(fn, tmp)
+    for f in range(F):
         tmp[f : f + 1, 2 * L : 3 * L] = fh[f * 2, 39:40, :] + fh[f * 2 + 1, 39:40, :]
     rg[...] = exact_dot(tmp[...], pool[...])
     group = lane >> 3
-    for out, row in ((mca, 1 - px), (mcb, px)):
+    near_row(fn, tp, 1 - px, rg[:, 0:L], mxa)
+    for out, at, row in ((mxa, NEAR, 1 - px), (mcb, 0, px)):
         acc = jnp.zeros((FZ, L), F32)
         for f in range(F):
             acc = jnp.where(group == f, pltpu.roll(fh[f * 2 + row], 4 + 8 * f, 1), acc)
@@ -154,13 +173,13 @@
         for f in range(F):
             g = 7 + f
             acc = jnp.where(group == g, pltpu.roll(jnp.broadcast_to(rg[f : f + 1, L : 2 * L], (FZ, L)), 4 + 8 * g, 1), acc)
-        out[0:40, :] = acc
+        out[at : at + 40, :] = acc
     acc = jnp.zeros((FZ, L), F32)
     for f in range(F):
         for h in range(2):
             g = f * 2 + h
             acc = jnp.where(group == g, pltpu.roll(ch[f, h * 40 : h * 40 + 40, :], (4 + 8 * g) % L, 1), acc)
-    mca[40:80, :] = acc
+    mxa[NEAR + 40 : NEAR + 80, :] = acc
     mcb[40:80, :] = acc
 
 
@@ -260,7 +279,7 @@
 
 
 def step_one(
-    fn, fo, cn, co, sf, lf, sc, lc, tp, fh, foh, sh, th, ch, coh, sch, rg, rxa, rxb, rca, rcb, spread, pool,
+    fn, fo, cn, co, sf, lf, sc, lc, tp, fh, foh, sh, th, ch, coh, sch, rg, rxa, rac, rxb, rcb, spread, pool,
     f1, c1, rg1, mxa, mxb, jv, cf, cv, U, V, cc, tmp,
 ):
     px = lax.rem(lax.axis_index("gx"), 2)
@@ -270,7 +289,8 @@
     near40 = ((lane40 + 4) & 127) < 8
 
     def corner(rc, part, g):
-        return jnp.where(near40, pltpu.roll(rc[part * 40 : part * 40 + 40, :], (2 * L - 4 - 8 * g) % L, 1), 0.0)
+        rc, at = rc
+        return jnp.where(near40, pltpu.roll(rc[at + part * 40 : at + part * 40 + 40, :], (2 * L - 4 - 8 * g) % L, 1), 0.0)
 
     cc[...] = jnp.zeros_like(cc)
     body = slice(ZP, ZP + FZ)
@@ -283,12 +303,12 @@
         V[f, 1, 1, ZP : ZP + CZ, :] = ch[f]
         for t in range(2):
             V[f, 1, t, ZP - 1 : ZP, :] = rg[f : f + 1, t * L : (t + 1) * L]
-    for rx, rc, fr, cr in ((rxa, rca, 3 * (1 - px), 2 * (1 - px)), (rxb, rcb, 3 * px, 2 * px)):
+    for rx, rc, rz, zat, fr, cr in ((rxa, (rxa, NEAR), rac, 0, 3 * (1 - px), 2 * (1 - px)), (rxb, (rcb, 0), rxb, COARSE_AT, 3 * px, 2 * px)):
         for f in range(F):
             for t in range(2):
                 U[f, fr, t, body, :] = rx[f * 80 + t * 40 : f * 80 + t * 40 + 40, :]
             U[f, fr, 2, body, :] = corner(rc, 0, f)
-            V[f, cr, 0, ZP : ZP + CZ, :] = rx[480 + f * CZ : 480 + (f + 1) * CZ, :]
+            V[f, cr, 0, ZP : ZP + CZ, :] = rz[zat + f * CZ : zat + (f + 1) * CZ, :]
             for half in range(2):
                 V[f, cr, 1, ZP + half * 40 : ZP + half * 40 + 40, :] = corner(rc, 1, f * 2 + half)
             V[f, cr, 0, ZP - 1 : ZP, :] = rx[RIDGE_AT + f : RIDGE_AT + f + 1, :]
@@ -366,7 +386,7 @@
         for f in range(F):
             for t in range(2):
                 out[f * 80 + t * 40 : f * 80 + t * 40 + 40, :] = f1[f * 2 + row, t]
-            out[480 + f * CZ : 480 + (f + 1) * CZ, :] = c1[f, 0]
+            out[COARSE_AT + f * CZ : COARSE_AT + (f + 1) * CZ, :] = c1[f, 0]
             acc = jnp.where(group == f, pltpu.roll(f1[f * 2 + row, 2], 2 + 4 * f, 1), acc)
         out[RIDGE_AT : RIDGE_AT + 8, :] = rg1[:, 0:L]
         out[BULK : BULK + 40, :] = acc
@@ -396,7 +416,7 @@
             for t in range(2):
                 U[f, fr, t, body, :] = rx[f * 80 + t * 40 : f * 80 + t * 40 + 40, :]
             U[f, fr, 2, body, :] = corner(rx, f)
-            V[f, cr, 0, ZP : ZP + CZ, :] = rx[480 + f * CZ : 480 + (f + 1) * CZ, :]
+            V[f, cr, 0, ZP : ZP + CZ, :] = rx[COARSE_AT + f * CZ : COARSE_AT + (f + 1) * CZ, :]
             for half in range(2):
                 V[f, cr, 1, ZP + half * 40 : ZP + half * 40 + 40, :] = corner(rx, 6 + f * 2 + half)
             V[f, cr, 0, ZP - 1 : ZP, :] = rx[RIDGE_AT + f : RIDGE_AT + f + 1, :]
@@ -450,15 +470,15 @@
     ck[...] = total
 
 
-def call(kernel, args, outs, scratch):
-    shapes = tuple(jax.ShapeDtypeStruct(s, F32) for s in outs)
+def call(kernel, args, outs, scratch, space=VM, megabytes=12):
+    shapes = tuple(jax.ShapeDtypeStruct(s, F32) if isinstance(s, tuple) else s for s in outs)
     return pl.pallas_call(
         kernel,
         out_shape=shapes,
-        in_specs=[VM] * len(args),
+        in_specs=[space] * len(args),
         out_specs=(VM,) * len(outs),
-        scratch_shapes=[pltpu.VMEM(s, F32) for s in scratch],
-        compiler_params=PARAMS,
+        scratch_shapes=[pltpu.VMEM(s, F32) if isinstance(s, tuple) else s for s in scratch],
+        compiler_params=pltpu.CompilerParams(vmem_limit_bytes=megabytes * 1024 * 1024),
     )(*args)
 
 
@@ -482,23 +502,32 @@
     co, cn = coarse_old.reshape(-1, L), coarse_now.reshape(-1, L)
     sc, lc = shear_coarse.reshape(-1, L), lame_coarse.reshape(-1, L)
     pool, spread = jnp.asarray(POOL), jnp.asarray(SPREAD)
-    mxa, mxb, mya, myb = call(first_pack, (fn, fo, cn, co, sf, lf, sc, lc, tp, pool), ((BULK, L), (BULK, L), (80, L), (80, L)), ((8, 256),))
-    rxb = swap(mxb, "gx", 1)
+    raw = (fn, fo, cn, co, sf, lf, sc, lc, tp, pool, spread)
+    raw = tuple(pltpu.with_memory_space_constraint(v, pltpu.HBM) for v in raw)
+    local = call(
+        load_and_pack_y,
+        raw,
+        tuple(jax.ShapeDtypeStruct(v.shape, v.dtype) for v in raw) + ((BULK, L), (80, L), (80, L)),
+        ((8, 256), pltpu.SemaphoreType.DMA((len(raw),)),),
+        pl.BlockSpec(memory_space=pltpu.HBM),
+    )
+    fn, fo, cn, co, sf, lf, sc, lc, tp, pool, spread, mxb, mya, myb = local
     ryb = swap(myb, "gy", 1)
     rya = swap(mya, "gy", 0)
-    rxa = swap(mxa, "gx", 0)
-    fh, foh, sh, th, ch, coh, sch, rg, mca, mcb = call(
+    rxb = swap(mxb, "gx", 1)
+    fh, foh, sh, th, ch, coh, sch, rg, mxa, mcb = call(
         open_y,
-        (rya, ryb, fn, pool),
-        ((12, FZ, L), (12, FZ, L), (4, FZ, L), (2, 8, L), (F, CZ, L), (F, CZ, L), (2, CZ, L), (8, 256), (80, L), (80, L)),
+        (rya, ryb, fn, tp, pool),
+        ((12, FZ, L), (12, FZ, L), (4, FZ, L), (2, 8, L), (F, CZ, L), (F, CZ, L), (2, CZ, L), (8, 256), (NEAR + 80, L), (80, L)),
         ((8, 384),),
     )
     rcb = swap(mcb, "gx", 1)
-    rca = swap(mca, "gx", 0)
+    rxa = swap(mxa, "gx", 0)
+    rac = swap(cn, "gx", 0)
     field = ((F, 4, 3, 56, L), (F, 3, 2, 96, L), (3, 8, 256))
     f1, c1, rg1, mxa, mxb, jv, cf, cv = call(
         step_one,
-        (fn, fo, cn, co, sf, lf, sc, lc, tp, fh, foh, sh, th, ch, coh, sch, rg, rxa, rxb, rca, rcb, spread, pool),
+        (fn, fo, cn, co, sf, lf, sc, lc, tp, fh, foh, sh, th, ch, coh, sch, rg, rxa, rac, rxb, rcb, spread, pool),
         ((12, 3, FZ, L), (F, 2, CZ, L), (8, 256), (BULK + 40, L), (BULK + 40, L), (2, 4, 3, 8, L), (2, 2, 3, FZ, L), (2, 2, CZ, L)),
         field + ((8, 384),),
     )

time: 63.3 us -> 53.1 us (0.84)
  local copies, waits for them, and re-layouts: 10 us -> 0 us
  starting transfers between devices: 16.7 us -> 16 us
    unnamed x36 -> x0, local copies, waits for them, and re-layouts: 10 us -> none
    ppermute x8, starting transfers between devices: 16.7 us -> 16 us  [swap(): lax.ppermute(cells, axis, [p for i in range(first, count - 1, 2) for p in...]
  transfers between devices with their start and end apart: 8 -> 8, of which waited for: 4 -> 4; matrix products, arithmetic and copies ran while one was open for 0% -> 0% of each run, Pallas kernels for 1% -> 2%
where the time goes in v2:
time: 53.1 us; the launch traced here: 52.9 us
  waiting for transfers between devices  27.7 us (52%)
  starting transfers between devices  16 us (30%)
  Pallas kernels  8.47 us (16%)
  between operations  0.7 us (1%)
    ppermute x8, waiting for transfers between devices, swap(): lax.ppermute(cells, axis, [p for i in range(first, count - 1, 2) for p in...  27.7 us
    ppermute x8, starting transfers between devices, swap(): lax.ppermute(cells, axis, [p for i in range(first, count - 1, 2) for p in...  16 us
    pallas_call x4, Pallas kernels, call(): pl.pallas_call(kernel, out_shape=shapes, in_specs=[space] * len(args), ou...  8.47 us
  transfers between devices with their start and end apart: 8, of which 4 were waited for; matrix products, arithmetic and copies ran while one was open for 0% of the time, Pallas kernels for 2%

profile of v2, /device:TPU:153, one launch (start us, length us, event | category | flops | bytes accessed | tf_op | source)
XLA Modules:
  0.0 52.9 jit_solution(9453801230062503837)
XLA Ops:
  0.6 2.3 %shard_map.138 = (f32[960,128]{1,0:T(8,128)S(1)}, f32[960,128]{1,0:T(8,128)S(1)}, f32[480,128]{1,0:T(8,128)S(1)}, f32[480,128]{1,0:T(8,128)S(1)}, f32[160,128]{1...) custom-call(f32[960,128]{1,0:T(8,128)} %bitcast.45, ...), custom_call_target="tpu_custom_call" | custom-call | tf_op jit(solution)/shard_map/pallas_call | solution.py:475
  3.0 3.7 %collective-permute-start.4 = (f32[968,128]{1,0:T(8,128)S(1)}, f32[968,128]{1,0:T(8,128)S(1)}, u32[]{:S(2)}, u32[]{:S(2)}) collective-permute-start(f32[968,128]{1,0:T(8,128)S(1)} %get-tuple-element.61), channel_id=1, source_target_pairs={{8,16},{16,8},{24,32},{32,24},{40,48},{48,40},{56,64},{64,56},{72,... | collective-permute-start | bytes 1486856 | tf_op jit(solution)/shard_map/ppermute | solution.py:487
  6.7 2.5 %collective-permute-start = (f32[80,128]{1,0:T(8,128)S(1)}, f32[80,128]{1,0:T(8,128)S(1)}, u32[]{:S(2)}, u32[]{:S(2)}) collective-permute-start(f32[80,128]{1,0:T(8,128)S(1)} %get-tuple-element.49), channel_id=1, source_target_pairs={{0,1},{1,0},{2,3},{3,2},{4,5},{5,4},{6,7},{7,6},{8,9},{9,8},{10,11... | collective-permute-start | bytes 122888 | tf_op jit(solution)/shard_map/ppermute | solution.py:487
  9.2 2.6 %collective-permute-start.1 = (f32[80,128]{1,0:T(8,128)S(1)}, f32[80,128]{1,0:T(8,128)S(1)}, u32[]{:S(2)}, u32[]{:S(2)}) collective-permute-start(f32[80,128]{1,0:T(8,128)S(1)} %get-tuple-element.50), channel_id=1, source_target_pairs={{1,2},{2,1},{3,4},{4,3},{5,6},{6,5},{9,10},{10,9},{11,12},{12,11},... | collective-permute-start | bytes 122888 | tf_op jit(solution)/shard_map/ppermute | solution.py:487
  11.8 9.7 %collective-permute-done.rya = f32[80,128]{1,0:T(8,128)S(1)} collective-permute-done((f32[80,128]{1,0:T(8,128)S(1)}, f32[80,128]{1,0:T(8,128)S(1)}, u32[]{:S(2)}, u32[]{:S(2)}) %collective-permute-start) | collective-permute-done | bytes 40992 | tf_op jit(solution)/shard_map/ppermute | solution.py:487
  21.5 1.1 %collective-permute-done.1.ryb = f32[80,128]{1,0:T(8,128)S(1)} collective-permute-done((f32[80,128]{1,0:T(8,128)S(1)}, f32[80,128]{1,0:T(8,128)S(1)}, u32[]{:S(2)}, u32[]{:S(2)}) %collective-permute-start.1) | collective-permute-done | bytes 40992 | tf_op jit(solution)/shard_map/ppermute | solution.py:487
  22.6 0.8 %shard_map.139 = (f32[12,40,128]{2,1,0:T(8,128)S(1)}, f32[12,40,128]{2,1,0:T(8,128)S(1)}, f32[4,40,128]{2,1,0:T(8,128)S(1)}, f32[2,8,128]{2,1,0:T(8,128)S(1)}, f...) custom-call(f32[80,128]{1,0:T(8,128)S(1)} %collective-permute-done.r, ...), custom_call_target="tpu_custom_call" | custom-call | tf_op jit(solution)/shard_map/pallas_call | solution.py:475
  23.4 0.1 collective-permute-start.2
  23.5 0.5 collective-permute-start.3
  24.0 2.4 %collective-permute-start.5 = (f32[80,128]{1,0:T(8,128)S(1)}, f32[80,128]{1,0:T(8,128)S(1)}, u32[]{:S(2)}, u32[]{:S(2)}) collective-permute-start(f32[80,128]{1,0:T(8,128)S(1)} %get-tuple-element.62), channel_id=1, source_target_pairs={{8,16},{16,8},{24,32},{32,24},{40,48},{48,40},{56,64},{64,56},{72,... | collective-permute-start | bytes 122888 | tf_op jit(solution)/shard_map/ppermute | solution.py:487
  26.5 2.9 %collective-permute-done.5.rcb = f32[80,128]{1,0:T(8,128)S(1)} collective-permute-done((f32[80,128]{1,0:T(8,128)S(1)}, f32[80,128]{1,0:T(8,128)S(1)}, u32[]{:S(2)}, u32[]{:S(2)}) %collective-permute-start.5) | collective-permute-done | bytes 40992 | tf_op jit(solution)/shard_map/ppermute | solution.py:487
  29.3 0.0 collective-permute-done.3.rac
  29.3 0.0 collective-permute-done.2.rxa
  29.3 0.0 collective-permute-done.4.rxb
  29.3 2.4 %shard_map.140 = (f32[12,3,40,128]{3,2,1,0:T(8,128)S(1)}, f32[6,2,80,128]{3,2,1,0:T(8,128)S(1)}, f32[8,256]{1,0:T(8,128)S(1)}, f32[1008,128]{1,0:T(8,128)S(1)}, ...) custom-call(f32[960,128]{1,0:T(8,128)S(1)} %get-tuple-element.40.fn,, ...), custom_call_target="tpu_custom_call" | custom-call | tf_op jit(solution)/shard_map/pallas_call | solution.py:475
  31.8 2.3 %collective-permute-start.6 = (f32[1008,128]{1,0:T(8,128)S(1)}, f32[1008,128]{1,0:T(8,128)S(1)}, u32[]{:S(2)}, u32[]{:S(2)}) collective-permute-start(f32[1008,128]{1,0:T(8,128)S(1)} %get-tuple-element.67), channel_id=1, source_target_pairs={{0,8},{8,0},{16,24},{24,16},{32,40},{40,32},{48,56},{56,48},{64,72... | collective-permute-start | bytes 1548296 | tf_op jit(solution)/shard_map/ppermute | solution.py:487
  34.0 1.9 %collective-permute-start.7 = (f32[1008,128]{1,0:T(8,128)S(1)}, f32[1008,128]{1,0:T(8,128)S(1)}, u32[]{:S(2)}, u32[]{:S(2)}) collective-permute-start(f32[1008,128]{1,0:T(8,128)S(1)} %get-tuple-element.68), channel_id=1, source_target_pairs={{8,16},{16,8},{24,32},{32,24},{40,48},{48,40},{56,64},{64,56},{72,... | collective-permute-start | bytes 1548296 | tf_op jit(solution)/shard_map/ppermute | solution.py:487
  36.0 0.0 collective-permute-done.6.rxa
  36.0 14.0 %collective-permute-done.7.rxb = f32[1008,128]{1,0:T(8,128)S(1)} collective-permute-done((f32[1008,128]{1,0:T(8,128)S(1)}, f32[1008,128]{1,0:T(8,128)S(1)}, u32[]{:S(2)}, u32[]{:S(2)}) %collective-permute-start.7) | collective-permute-done | bytes 516128 | tf_op jit(solution)/shard_map/ppermute | solution.py:487
  50.0 2.9 %shard_map.141 = (f32[960,128]{1,0:T(8,128)}, f32[480,128]{1,0:T(8,128)}, f32[160,128]{1,0:T(8,128)}, f32[80,128]{1,0:T(8,128)}) custom-call(f32[960,128]{1,0:T(8,128)S(1)} %get-tuple-element.40.fn, f32[480,128]{1,0:T(8,128)S(1)} %get-tuple-element.41.cn, f32[12,3,40,128]{3,2,1,0:T(8,128)S(1)} %get-tuple-element.64.f1, ...), custom_call_target="tpu_custom_call" | custom-call | tf_op jit(solution)/shard_map/pallas_call | solution.py:475
Async XLA Ops:
  3.0 26.4 %collective-permute-start.4 = (f32[968,128]{1,0:T(8,128)S(1)}, f32[968,128]{1,0:T(8,128)S(1)}, u32[]{:S(2)}, u32[]{:S(2)}) collective-permute-start(f32[968,128]{1,0:T(8,128)S(1)} %get-tuple-element.61), channel_id=1, source_target_pairs={{8,16},{16,8},{24,32},{32,24},{40,48},{48,40},{56,64},{64,56},{72,... | collective-permute-start | bytes 1486856 | tf_op jit(solution)/shard_map/ppermute | solution.py:487
  6.7 14.9 %collective-permute-start = (f32[80,128]{1,0:T(8,128)S(1)}, f32[80,128]{1,0:T(8,128)S(1)}, u32[]{:S(2)}, u32[]{:S(2)}) collective-permute-start(f32[80,128]{1,0:T(8,128)S(1)} %get-tuple-element.49), channel_id=1, source_target_pairs={{0,1},{1,0},{2,3},{3,2},{4,5},{5,4},{6,7},{7,6},{8,9},{9,8},{10,11... | collective-permute-start | bytes 122888 | tf_op jit(solution)/shard_map/ppermute | solution.py:487
  9.2 13.4 %collective-permute-start.1 = (f32[80,128]{1,0:T(8,128)S(1)}, f32[80,128]{1,0:T(8,128)S(1)}, u32[]{:S(2)}, u32[]{:S(2)}) collective-permute-start(f32[80,128]{1,0:T(8,128)S(1)} %get-tuple-element.50), channel_id=1, source_target_pairs={{1,2},{2,1},{3,4},{4,3},{5,6},{6,5},{9,10},{10,9},{11,12},{12,11},... | collective-permute-start | bytes 122888 | tf_op jit(solution)/shard_map/ppermute | solution.py:487
  23.4 5.9 %collective-permute-start.2 = (f32[568,128]{1,0:T(8,128)S(1)}, f32[568,128]{1,0:T(8,128)S(1)}, u32[]{:S(2)}, u32[]{:S(2)}) collective-permute-start(f32[568,128]{1,0:T(8,128)S(1)} %get-tuple-element.60), channel_id=1, source_target_pairs={{0,8},{8,0},{16,24},{24,16},{32,40},{40,32},{48,56},{56,48},{64,72... | collective-permute-start | bytes 872456 | tf_op jit(solution)/shard_map/ppermute | solution.py:487
  23.5 5.8 %collective-permute-start.3 = (f32[480,128]{1,0:T(8,128)S(1)}, f32[480,128]{1,0:T(8,128)S(1)}, u32[]{:S(2)}, u32[]{:S(2)}) collective-permute-start(f32[480,128]{1,0:T(8,128)S(1)} %get-tuple-element.41.cn), channel_id=1, source_target_pairs={{0,8},{8,0},{16,24},{24,16},{32,40},{40,32},{48,56},{56,48},{64,72... | collective-permute-start | bytes 737288 | tf_op jit(solution)/shard_map/ppermute | solution.py:487
  24.0 5.3 %collective-permute-start.5 = (f32[80,128]{1,0:T(8,128)S(1)}, f32[80,128]{1,0:T(8,128)S(1)}, u32[]{:S(2)}, u32[]{:S(2)}) collective-permute-start(f32[80,128]{1,0:T(8,128)S(1)} %get-tuple-element.62), channel_id=1, source_target_pairs={{8,16},{16,8},{24,32},{32,24},{40,48},{48,40},{56,64},{64,56},{72,... | collective-permute-start | bytes 122888 | tf_op jit(solution)/shard_map/ppermute | solution.py:487
  31.8 4.2 %collective-permute-start.6 = (f32[1008,128]{1,0:T(8,128)S(1)}, f32[1008,128]{1,0:T(8,128)S(1)}, u32[]{:S(2)}, u32[]{:S(2)}) collective-permute-start(f32[1008,128]{1,0:T(8,128)S(1)} %get-tuple-element.67), channel_id=1, source_target_pairs={{0,8},{8,0},{16,24},{24,16},{32,40},{40,32},{48,56},{56,48},{64,72... | collective-permute-start | bytes 1548296 | tf_op jit(solution)/shard_map/ppermute | solution.py:487
  34.0 15.9 %collective-permute-start.7 = (f32[1008,128]{1,0:T(8,128)S(1)}, f32[1008,128]{1,0:T(8,128)S(1)}, u32[]{:S(2)}, u32[]{:S(2)}) collective-permute-start(f32[1008,128]{1,0:T(8,128)S(1)} %get-tuple-element.68), channel_id=1, source_target_pairs={{8,16},{16,8},{24,32},{32,24},{40,48},{48,40},{56,64},{64,56},{72,... | collective-permute-start | bytes 1548296 | tf_op jit(solution)/shard_map/ppermute | solution.py:487

commit v3 on v2

--- a/solution.py
+++ b/solution.py
@@ -22,6 +22,7 @@
 COARSE_AT = RIDGE_AT + 8
 NEAR = COARSE_AT
 BULK = COARSE_AT + COARSE_ROWS
+LATER_COARSE = NEAR + 40
 VM = pl.BlockSpec(memory_space=pltpu.VMEM)
 
 
@@ -132,7 +133,7 @@
     mxb[COARSE_AT : COARSE_AT + COARSE_ROWS, :] = cn[...]
 
 
-def open_y(rya, ryb, fn, tp, pool, fh, foh, sh, th, ch, coh, sch, rg, mxa, mcb, tmp):
+def open_y(ryb, rya, fn, tp, pool, fh, foh, sh, th, ch, coh, sch, rg, mxa, mcb, tmp):
     px = lax.rem(lax.axis_index("gx"), 2)
     py = lax.rem(lax.axis_index("gy"), 2)
     lane = lanes((FZ, L))
@@ -280,7 +281,7 @@
 
 def step_one(
     fn, fo, cn, co, sf, lf, sc, lc, tp, fh, foh, sh, th, ch, coh, sch, rg, rxa, rac, rxb, rcb, spread, pool,
-    f1, c1, rg1, mxa, mxb, jv, cf, cv, U, V, cc, tmp,
+    f1, c1, c1h, rg1, mxa, mxb, jv, cf, cv, U, V, cc, tmp,
 ):
     px = lax.rem(lax.axis_index("gx"), 2)
     edges = edges_here()
@@ -365,7 +366,10 @@
                 zs = slice(8 * k, 8 * k + 8)
                 old = co[pl.ds((a * 3 + i) * CZ + 8 * k, 8), :] if t == 0 else coh[a * 3 + i, zs, :]
                 new = c2 - old + cv[0, t, zs, :] * lap + cv[1, t, zs, :] * gd
-                c1[a * 3 + i, t, zs, :] = new if t == 0 else jnp.where(keep, new, 0.0)
+                if t == 0:
+                    c1[pl.ds((a * 3 + i) * CZ + 8 * k, 8), :] = new
+                else:
+                    c1h[a * 3 + i, zs, :] = jnp.where(keep, new, 0.0)
         return 0
 
     lax.fori_loop(0, 2, fine, 0)
@@ -380,19 +384,19 @@
     for f in range(F):
         for half in range(2):
             g = 6 + 2 * f + half
-            low = jnp.where(group == g, pltpu.roll(c1[f, 1, half * 40 : half * 40 + 40, :], 2 + 4 * g, 1), low)
+            low = jnp.where(group == g, pltpu.roll(c1h[f, half * 40 : half * 40 + 40, :], 2 + 4 * g, 1), low)
     for out, row in ((mxa, 1 - px), (mxb, px)):
         acc = low
         for f in range(F):
             for t in range(2):
                 out[f * 80 + t * 40 : f * 80 + t * 40 + 40, :] = f1[f * 2 + row, t]
-            out[COARSE_AT + f * CZ : COARSE_AT + (f + 1) * CZ, :] = c1[f, 0]
             acc = jnp.where(group == f, pltpu.roll(f1[f * 2 + row, 2], 2 + 4 * f, 1), acc)
         out[RIDGE_AT : RIDGE_AT + 8, :] = rg1[:, 0:L]
-        out[BULK : BULK + 40, :] = acc
-
-
-def step_two(fn, cn, f1, c1, rg1, rxa, rxb, jv, cf, cv, spread, fout, cout, fk, ck, U, V, cc):
+        out[NEAR : NEAR + 40, :] = acc
+    mxb[LATER_COARSE : LATER_COARSE + COARSE_ROWS, :] = c1[...]
+
+
+def step_two(fn, cn, f1, c1, c1h, rg1, rxa, rac, rxb, jv, cf, cv, spread, fout, cout, fk, ck, U, V, cc):
     px = lax.rem(lax.axis_index("gx"), 2)
     edges = edges_here()
     lane = lanes((8, L))
@@ -400,7 +404,7 @@
     near40 = ((lane40 + 2) & 127) < 4
 
     def corner(rx, g):
-        return jnp.where(near40, pltpu.roll(rx[BULK : BULK + 40, :], (2 * L - 2 - 4 * g) % L, 1), 0.0)
+        return jnp.where(near40, pltpu.roll(rx[NEAR : NEAR + 40, :], (2 * L - 2 - 4 * g) % L, 1), 0.0)
 
     cc[...] = jnp.zeros_like(cc)
     body = slice(ZP, ZP + FZ)
@@ -408,15 +412,16 @@
         for x in range(2):
             for t in range(3):
                 U[f, 1 + x, t, body, :] = f1[f * 2 + x, t]
+        V[f, 1, 0, ZP : ZP + CZ, :] = c1[f * CZ : (f + 1) * CZ, :]
+        V[f, 1, 1, ZP : ZP + CZ, :] = c1h[f]
         for t in range(2):
-            V[f, 1, t, ZP : ZP + CZ, :] = c1[f, t]
             V[f, 1, t, ZP - 1 : ZP, :] = rg1[f : f + 1, t * L : (t + 1) * L]
-    for rx, fr, cr in ((rxa, 3 * (1 - px), 2 * (1 - px)), (rxb, 3 * px, 2 * px)):
+    for rx, rz, zat, fr, cr in ((rxa, rac, 0, 3 * (1 - px), 2 * (1 - px)), (rxb, rxb, LATER_COARSE, 3 * px, 2 * px)):
         for f in range(F):
             for t in range(2):
                 U[f, fr, t, body, :] = rx[f * 80 + t * 40 : f * 80 + t * 40 + 40, :]
             U[f, fr, 2, body, :] = corner(rx, f)
-            V[f, cr, 0, ZP : ZP + CZ, :] = rx[COARSE_AT + f * CZ : COARSE_AT + (f + 1) * CZ, :]
+            V[f, cr, 0, ZP : ZP + CZ, :] = rz[zat + f * CZ : zat + (f + 1) * CZ, :]
             for half in range(2):
                 V[f, cr, 1, ZP + half * 40 : ZP + half * 40 + 40, :] = corner(rx, 6 + f * 2 + half)
             V[f, cr, 0, ZP - 1 : ZP, :] = rx[RIDGE_AT + f : RIDGE_AT + f + 1, :]
@@ -464,13 +469,13 @@
             fk[coef_rows(t, x), :] = total
     total = jnp.zeros((CZ, L), F32)
     for i in range(3):
-        total = total + c1[i, 0] * c1[3 + i, 0]
+        total = total + c1[i * CZ : (i + 1) * CZ, :] * c1[(3 + i) * CZ : (4 + i) * CZ, :]
     for i in range(3):
         total = total + cout[i * CZ : (i + 1) * CZ, :] * cout[(3 + i) * CZ : (4 + i) * CZ, :]
     ck[...] = total
 
 
-def call(kernel, args, outs, scratch, space=VM, megabytes=12):
+def call(kernel, args, outs, scratch, space=VM, megabytes=12, flops=0):
     shapes = tuple(jax.ShapeDtypeStruct(s, F32) if isinstance(s, tuple) else s for s in outs)
     return pl.pallas_call(
         kernel,
@@ -478,6 +483,7 @@
         in_specs=[space] * len(args),
         out_specs=(VM,) * len(outs),
         scratch_shapes=[pltpu.VMEM(s, F32) if isinstance(s, tuple) else s for s in scratch],
+        cost_estimate=pl.CostEstimate(flops=flops, transcendentals=0, bytes_accessed=1024) if flops else None,
         compiler_params=pltpu.CompilerParams(vmem_limit_bytes=megabytes * 1024 * 1024),
     )(*args)
 
@@ -517,25 +523,27 @@
     rxb = swap(mxb, "gx", 1)
     fh, foh, sh, th, ch, coh, sch, rg, mxa, mcb = call(
         open_y,
-        (rya, ryb, fn, tp, pool),
+        (ryb, rya, fn, tp, pool),
         ((12, FZ, L), (12, FZ, L), (4, FZ, L), (2, 8, L), (F, CZ, L), (F, CZ, L), (2, CZ, L), (8, 256), (NEAR + 80, L), (80, L)),
         ((8, 384),),
+        flops=5 * 10**9,
     )
     rcb = swap(mcb, "gx", 1)
     rxa = swap(mxa, "gx", 0)
     rac = swap(cn, "gx", 0)
     field = ((F, 4, 3, 56, L), (F, 3, 2, 96, L), (3, 8, 256))
-    f1, c1, rg1, mxa, mxb, jv, cf, cv = call(
+    f1, c1, c1h, rg1, mxa, mxb, jv, cf, cv = call(
         step_one,
         (fn, fo, cn, co, sf, lf, sc, lc, tp, fh, foh, sh, th, ch, coh, sch, rg, rxa, rac, rxb, rcb, spread, pool),
-        ((12, 3, FZ, L), (F, 2, CZ, L), (8, 256), (BULK + 40, L), (BULK + 40, L), (2, 4, 3, 8, L), (2, 2, 3, FZ, L), (2, 2, CZ, L)),
+        ((12, 3, FZ, L), (COARSE_ROWS, L), (F, CZ, L), (8, 256), (NEAR + 40, L), (BULK + 40, L), (2, 4, 3, 8, L), (2, 2, 3, FZ, L), (2, 2, CZ, L)),
         field + ((8, 384),),
     )
     rxb = swap(mxb, "gx", 1)
     rxa = swap(mxa, "gx", 0)
+    rac = swap(c1, "gx", 0)
     fout, cout, fk, ck = call(
         step_two,
-        (fn, cn, f1, c1, rg1, rxa, rxb, jv, cf, cv, spread),
+        (fn, cn, f1, c1, c1h, rg1, rxa, rac, rxb, jv, cf, cv, spread),
         ((FINE_ROWS, L), (COARSE_ROWS, L), (4 * FZ, L), (CZ, L)),
         field,
     )

time: 53.1 us -> 47.4 us (0.89)
  the two profiles are of different devices: /device:TPU:153 before, /device:TPU:106 now
where the time goes in v3:
time: 47.4 us; the launch traced here: 47.2 us
  waiting for transfers between devices  22.8 us (48%)
  starting transfers between devices  15.2 us (32%)
  Pallas kernels  8.49 us (18%)
  between operations  0.71 us (1%)
    ppermute x9, waiting for transfers between devices, swap(): lax.ppermute(cells, axis, [p for i in range(first, count - 1, 2) for p in...  22.8 us
    ppermute x9, starting transfers between devices, swap(): lax.ppermute(cells, axis, [p for i in range(first, count - 1, 2) for p in...  15.2 us
    pallas_call x4, Pallas kernels, call(): pl.pallas_call(kernel, out_shape=shapes, in_specs=[space] * len(args), ou...  8.49 us
  transfers between devices with their start and end apart: 9, of which 4 were waited for; matrix products, arithmetic and copies ran while one was open for 0% of the time, Pallas kernels for 2%

profile of v3, /device:TPU:106, one launch (start us, length us, event | category | flops | bytes accessed | tf_op | source)
XLA Modules:
  0.0 47.2 jit_solution(4647539654684376580)
XLA Ops:
  0.6 2.3 %shard_map.138 = (f32[960,128]{1,0:T(8,128)S(1)}, f32[960,128]{1,0:T(8,128)S(1)}, f32[480,128]{1,0:T(8,128)S(1)}, f32[480,128]{1,0:T(8,128)S(1)}, f32[160,128]{1...) custom-call(f32[960,128]{1,0:T(8,128)} %bitcast.45, ...), custom_call_target="tpu_custom_call" | custom-call | tf_op jit(solution)/shard_map/pallas_call | solution.py:480
  3.0 3.9 %collective-permute-start = (f32[80,128]{1,0:T(8,128)S(1)}, f32[80,128]{1,0:T(8,128)S(1)}, u32[]{:S(2)}, u32[]{:S(2)}) collective-permute-start(f32[80,128]{1,0:T(8,128)S(1)} %get-tuple-element.50), channel_id=1, source_target_pairs={{1,2},{2,1},{3,4},{4,3},{5,6},{6,5},{9,10},{10,9},{11,12},{12,11},... | collective-permute-start | bytes 122888 | tf_op jit(solution)/shard_map/ppermute | solution.py:493
  6.9 2.6 %collective-permute-start.1 = (f32[80,128]{1,0:T(8,128)S(1)}, f32[80,128]{1,0:T(8,128)S(1)}, u32[]{:S(2)}, u32[]{:S(2)}) collective-permute-start(f32[80,128]{1,0:T(8,128)S(1)} %get-tuple-element.51), channel_id=1, source_target_pairs={{0,1},{1,0},{2,3},{3,2},{4,5},{5,4},{6,7},{7,6},{8,9},{9,8},{10,11... | collective-permute-start | bytes 122888 | tf_op jit(solution)/shard_map/ppermute | solution.py:493
  9.5 1.9 %collective-permute-start.4 = (f32[968,128]{1,0:T(8,128)S(1)}, f32[968,128]{1,0:T(8,128)S(1)}, u32[]{:S(2)}, u32[]{:S(2)}) collective-permute-start(f32[968,128]{1,0:T(8,128)S(1)} %get-tuple-element.62), channel_id=1, source_target_pairs={{8,16},{16,8},{24,32},{32,24},{40,48},{48,40},{56,64},{64,56},{72,... | collective-permute-start | bytes 1486856 | tf_op jit(solution)/shard_map/ppermute | solution.py:493
  11.4 0.0 collective-permute-done.ryb
  11.4 1.0 %collective-permute-done.1.rya = f32[80,128]{1,0:T(8,128)S(1)} collective-permute-done((f32[80,128]{1,0:T(8,128)S(1)}, f32[80,128]{1,0:T(8,128)S(1)}, u32[]{:S(2)}, u32[]{:S(2)}) %collective-permute-start.1) | collective-permute-done | bytes 40992 | tf_op jit(solution)/shard_map/ppermute | solution.py:493
  12.5 0.8 %shard_map.139 = (f32[12,40,128]{2,1,0:T(8,128)S(1)}, f32[12,40,128]{2,1,0:T(8,128)S(1)}, f32[4,40,128]{2,1,0:T(8,128)S(1)}, f32[2,8,128]{2,1,0:T(8,128)S(1)}, f...) custom-call(f32[80,128]{1,0:T(8,128)S(1)} %collective-permute-done.r, ...), custom_call_target="tpu_custom_call" | custom-call | flops 5000000000 | bytes 1024 | tf_op jit(solution)/shard_map/pallas_call | solution.py:480
  13.3 2.3 %collective-permute-start.2 = (f32[568,128]{1,0:T(8,128)S(1)}, f32[568,128]{1,0:T(8,128)S(1)}, u32[]{:S(2)}, u32[]{:S(2)}) collective-permute-start(f32[568,128]{1,0:T(8,128)S(1)} %get-tuple-element.61), channel_id=1, source_target_pairs={{0,8},{8,0},{16,24},{24,16},{32,40},{40,32},{48,56},{56,48},{64,72... | collective-permute-start | bytes 872456 | tf_op jit(solution)/shard_map/ppermute | solution.py:493
  15.6 0.1 collective-permute-start.3
  15.7 1.9 %collective-permute-start.5 = (f32[80,128]{1,0:T(8,128)S(1)}, f32[80,128]{1,0:T(8,128)S(1)}, u32[]{:S(2)}, u32[]{:S(2)}) collective-permute-start(f32[80,128]{1,0:T(8,128)S(1)} %get-tuple-element.63), channel_id=1, source_target_pairs={{8,16},{16,8},{24,32},{32,24},{40,48},{48,40},{56,64},{64,56},{72,... | collective-permute-start | bytes 122888 | tf_op jit(solution)/shard_map/ppermute | solution.py:493
  17.6 8.3 %collective-permute-done.5.rcb = f32[80,128]{1,0:T(8,128)S(1)} collective-permute-done((f32[80,128]{1,0:T(8,128)S(1)}, f32[80,128]{1,0:T(8,128)S(1)}, u32[]{:S(2)}, u32[]{:S(2)}) %collective-permute-start.5) | collective-permute-done | bytes 40992 | tf_op jit(solution)/shard_map/ppermute | solution.py:493
  25.9 0.0 collective-permute-done.3.rac
  25.9 0.0 collective-permute-done.2.rxa
  25.9 0.0 collective-permute-done.4.rxb
  25.9 2.4 %shard_map.140 = (f32[12,3,40,128]{3,2,1,0:T(8,128)S(1)}, f32[480,128]{1,0:T(8,128)S(1)}, f32[6,80,128]{2,1,0:T(8,128)S(1)}, f32[8,256]{1,0:T(8,128)S(1)}, f32[5...) custom-call(f32[960,128]{1,0:T(8,128)S(1)} %get-tuple-element.41.fn,, ...), custom_call_target="tpu_custom_call" | custom-call | tf_op jit(solution)/shard_map/pallas_call | solution.py:480
  28.3 1.9 %collective-permute-start.8 = (f32[1008,128]{1,0:T(8,128)S(1)}, f32[1008,128]{1,0:T(8,128)S(1)}, u32[]{:S(2)}, u32[]{:S(2)}) collective-permute-start(f32[1008,128]{1,0:T(8,128)S(1)} %get-tuple-element.70), channel_id=1, source_target_pairs={{8,16},{16,8},{24,32},{32,24},{40,48},{48,40},{56,64},{64,56},{72,... | collective-permute-start | bytes 1548296 | tf_op jit(solution)/shard_map/ppermute | solution.py:493
  30.3 0.1 collective-permute-start.6
  30.4 0.5 %collective-permute-start.7 = (f32[480,128]{1,0:T(8,128)S(1)}, f32[480,128]{1,0:T(8,128)S(1)}, u32[]{:S(2)}, u32[]{:S(2)}) collective-permute-start(f32[480,128]{1,0:T(8,128)S(1)} %get-tuple-element.66.c1), channel_id=1, source_target_pairs={{0,8},{8,0},{16,24},{24,16},{32,40},{40,32},{48,56},{56,48},{64,72... | collective-permute-start | bytes 737288 | tf_op jit(solution)/shard_map/ppermute | solution.py:493
  30.9 1.4 %collective-permute-done.7.rac = f32[480,128]{1,0:T(8,128)S(1)} collective-permute-done((f32[480,128]{1,0:T(8,128)S(1)}, f32[480,128]{1,0:T(8,128)S(1)}, u32[]{:S(2)}, u32[]{:S(2)}) %collective-permute-start.7) | collective-permute-done | bytes 245792 | tf_op jit(solution)/shard_map/ppermute | solution.py:493
  32.2 0.0 collective-permute-done.6.rxa
  32.3 12.0 %collective-permute-done.8.rxb = f32[1008,128]{1,0:T(8,128)S(1)} collective-permute-done((f32[1008,128]{1,0:T(8,128)S(1)}, f32[1008,128]{1,0:T(8,128)S(1)}, u32[]{:S(2)}, u32[]{:S(2)}) %collective-permute-start.8) | collective-permute-done | bytes 516128 | tf_op jit(solution)/shard_map/ppermute | solution.py:493
  44.3 2.9 %shard_map.141 = (f32[960,128]{1,0:T(8,128)}, f32[480,128]{1,0:T(8,128)}, f32[160,128]{1,0:T(8,128)}, f32[80,128]{1,0:T(8,128)}) custom-call(f32[960,128]{1,0:T(8,128)S(1)} %get-tuple-element.41.fn, f32[480,128]{1,0:T(8,128)S(1)} %get-tuple-element.42.cn, f32[12,3,40,128]{3,2,1,0:T(8,128)S(1)} %get-tuple-element.65.f1, f32[480,128]{1,0:T(8,128)S(1)} %get-tuple-element.66.c1, ...), custom_call_target="tpu_custom_call" | custom-call | tf_op jit(solution)/shard_map/pallas_call | solution.py:480
Async XLA Ops:
  3.0 8.5 %collective-permute-start = (f32[80,128]{1,0:T(8,128)S(1)}, f32[80,128]{1,0:T(8,128)S(1)}, u32[]{:S(2)}, u32[]{:S(2)}) collective-permute-start(f32[80,128]{1,0:T(8,128)S(1)} %get-tuple-element.50), channel_id=1, source_target_pairs={{1,2},{2,1},{3,4},{4,3},{5,6},{6,5},{9,10},{10,9},{11,12},{12,11},... | collective-permute-start | bytes 122888 | tf_op jit(solution)/shard_map/ppermute | solution.py:493
  6.9 5.6 %collective-permute-start.1 = (f32[80,128]{1,0:T(8,128)S(1)}, f32[80,128]{1,0:T(8,128)S(1)}, u32[]{:S(2)}, u32[]{:S(2)}) collective-permute-start(f32[80,128]{1,0:T(8,128)S(1)} %get-tuple-element.51), channel_id=1, source_target_pairs={{0,1},{1,0},{2,3},{3,2},{4,5},{5,4},{6,7},{7,6},{8,9},{9,8},{10,11... | collective-permute-start | bytes 122888 | tf_op jit(solution)/shard_map/ppermute | solution.py:493
  9.5 16.4 %collective-permute-start.4 = (f32[968,128]{1,0:T(8,128)S(1)}, f32[968,128]{1,0:T(8,128)S(1)}, u32[]{:S(2)}, u32[]{:S(2)}) collective-permute-start(f32[968,128]{1,0:T(8,128)S(1)} %get-tuple-element.62), channel_id=1, source_target_pairs={{8,16},{16,8},{24,32},{32,24},{40,48},{48,40},{56,64},{64,56},{72,... | collective-permute-start | bytes 1486856 | tf_op jit(solution)/shard_map/ppermute | solution.py:493
  13.3 12.6 %collective-permute-start.2 = (f32[568,128]{1,0:T(8,128)S(1)}, f32[568,128]{1,0:T(8,128)S(1)}, u32[]{:S(2)}, u32[]{:S(2)}) collective-permute-start(f32[568,128]{1,0:T(8,128)S(1)} %get-tuple-element.61), channel_id=1, source_target_pairs={{0,8},{8,0},{16,24},{24,16},{32,40},{40,32},{48,56},{56,48},{64,72... | collective-permute-start | bytes 872456 | tf_op jit(solution)/shard_map/ppermute | solution.py:493
  15.6 10.3 %collective-permute-start.3 = (f32[480,128]{1,0:T(8,128)S(1)}, f32[480,128]{1,0:T(8,128)S(1)}, u32[]{:S(2)}, u32[]{:S(2)}) collective-permute-start(f32[480,128]{1,0:T(8,128)S(1)} %get-tuple-element.42.cn), channel_id=1, source_target_pairs={{0,8},{8,0},{16,24},{24,16},{32,40},{40,32},{48,56},{56,48},{64,72... | collective-permute-start | bytes 737288 | tf_op jit(solution)/shard_map/ppermute | solution.py:493
  15.7 10.2 %collective-permute-start.5 = (f32[80,128]{1,0:T(8,128)S(1)}, f32[80,128]{1,0:T(8,128)S(1)}, u32[]{:S(2)}, u32[]{:S(2)}) collective-permute-start(f32[80,128]{1,0:T(8,128)S(1)} %get-tuple-element.63), channel_id=1, source_target_pairs={{8,16},{16,8},{24,32},{32,24},{40,48},{48,40},{56,64},{64,56},{72,... | collective-permute-start | bytes 122888 | tf_op jit(solution)/shard_map/ppermute | solution.py:493
  28.3 15.9 %collective-permute-start.8 = (f32[1008,128]{1,0:T(8,128)S(1)}, f32[1008,128]{1,0:T(8,128)S(1)}, u32[]{:S(2)}, u32[]{:S(2)}) collective-permute-start(f32[1008,128]{1,0:T(8,128)S(1)} %get-tuple-element.70), channel_id=1, source_target_pairs={{8,16},{16,8},{24,32},{32,24},{40,48},{48,40},{56,64},{64,56},{72,... | collective-permute-start | bytes 1548296 | tf_op jit(solution)/shard_map/ppermute | solution.py:493
  30.3 2.0 %collective-permute-start.6 = (f32[528,128]{1,0:T(8,128)S(1)}, f32[528,128]{1,0:T(8,128)S(1)}, u32[]{:S(2)}, u32[]{:S(2)}) collective-permute-start(f32[528,128]{1,0:T(8,128)S(1)} %get-tuple-element.69), channel_id=1, source_target_pairs={{0,8},{8,0},{16,24},{24,16},{32,40},{40,32},{48,56},{56,48},{64,72... | collective-permute-start | bytes 811016 | tf_op jit(solution)/shard_map/ppermute | solution.py:493
  30.4 1.9 %collective-permute-start.7 = (f32[480,128]{1,0:T(8,128)S(1)}, f32[480,128]{1,0:T(8,128)S(1)}, u32[]{:S(2)}, u32[]{:S(2)}) collective-permute-start(f32[480,128]{1,0:T(8,128)S(1)} %get-tuple-element.66.c1), channel_id=1, source_target_pairs={{0,8},{8,0},{16,24},{24,16},{32,40},{40,32},{48,56},{56,48},{64,72... | collective-permute-start | bytes 737288 | tf_op jit(solution)/shard_map/ppermute | solution.py:493

commit v4 on v2

v4 whole, which is shorter than its diff:
```python
import jax
import jax.numpy as jnp
import ml_dtypes
import numpy as np
from jax import lax
from jax.experimental import pallas as pl
from jax.experimental.pallas import tpu as pltpu
from jax.sharding import PartitionSpec as P

F = 6
FZ = 40
CZ = 80
L = 128
ZP = 8
DT2 = 0.04
F32 = jnp.float32

FINE_ROWS = F * FZ * 4
COARSE_ROWS = F * CZ
HFINE = 3 * 2 * FZ
HTOPO = HFINE + 3
HCOARSE = HFINE + 8
HALF = HCOARSE + 3 * CZ
HLATER = HCOARSE + 40
C_OPEN = 5*10**9
C_ONE = (5*10**9, 10**9)
C_TWO = 1
VM = pl.BlockSpec(memory_space=pltpu.VMEM)


def pool_weights():
    w = np.zeros((384, 256), np.float32)
    for n in range(384):
        if n < 256:
            w[n, n // 2] = 0.25
        else:
            k = n - 256
            w[n, 128 + (k // 2 if k < 64 else 64 + k // 2)] = 0.25
    return w.astype(ml_dtypes.bfloat16)


def spread_weights():
    w = np.zeros((256, 384), np.float32)
    for n in range(384):
        col = n if n < 320 else n - 384
        j = col // 2
        w[j % 256, n] += 0.75
        w[(j + (1 if col % 2 else -1)) % 256, n] += 0.25
    return w.astype(ml_dtypes.bfloat16)


POOL = pool_weights()
SPREAD = spread_weights()


def exact_dot(rows, weights):
    hi = rows.astype(jnp.bfloat16)
    rest = rows - hi.astype(F32)
    mid = rest.astype(jnp.bfloat16)
    low = (rest - mid.astype(F32)).astype(jnp.bfloat16)
    dot = lambda part: jnp.dot(part, weights, preferred_element_type=F32)
    return dot(hi) + (dot(mid) + dot(low))


def lanes(shape):
    return lax.broadcasted_iota(jnp.int32, shape, len(shape) - 1)


def fine_rows(f, lt, x, start=0, size=FZ):
    return pl.ds((f * FZ + start) * 4 + lt * 2 + x, size, stride=4)


def coef_rows(lt, x, start=0, size=FZ):
    return pl.ds(start * 4 + lt * 2 + x, size, stride=4)


def load_and_pack_y(*refs):
    n = 11
    hbm, (fn, fo, cn, co, sf, lf, sc, lc, tp, pool, spread), (ma, mbf, mbg, mya, myb, tmp, sems) = refs[:n], refs[n : 2 * n], refs[2 * n :]
    copies = [pltpu.make_async_copy(src, dst, sems.at[q]) for q, (src, dst) in enumerate(zip(hbm, refs[n : 2 * n]))]
    for copy in copies:
        copy.start()
    for copy in copies:
        copy.wait()
    pack_x(fn, cn, tp, pool, (ma, mbf, mbg), tmp)
    py = lax.rem(lax.axis_index("gy"), 2)
    group = lanes((FZ, L)) >> 2
    for out, right in ((mya, 1 - py), (myb, py)):
        base = 4 * right
        acc = jnp.zeros((FZ, L), F32)
        for arr, at in ((fn, 0), (fo, 12)):
            for f in range(F):
                for x in range(2):
                    g = at + f * 2 + x
                    acc = jnp.where(group == g, pltpu.roll(arr[fine_rows(f, right, x), :], lax.rem(base + 4 * g, L), 1), acc)
        for arr, at in ((sf, 24), (lf, 26)):
            for x in range(2):
                g = at + x
                acc = jnp.where(group == g, pltpu.roll(arr[coef_rows(right, x), :], lax.rem(base + 4 * g, L), 1), acc)
        for x in range(2):
            g = 28 + x
            plane = jnp.broadcast_to(tp[pl.ds(right * 2 + x, 1), :].astype(F32), (FZ, L))
            acc = jnp.where(group == g, pltpu.roll(plane, lax.rem(base + 4 * g, L), 1), acc)
        out[0:40, :] = acc
        acc = jnp.zeros((FZ, L), F32)
        for arr, at, count in ((cn, 0, F), (co, 12, F), (sc, 24, 1), (lc, 26, 1)):
            for f in range(count):
                for h in range(2):
                    g = at + f * 2 + h
                    acc = jnp.where(group == g, pltpu.roll(arr[f * CZ + h * 40 : f * CZ + h * 40 + 40, :], lax.rem(base + 4 * g, L), 1), acc)
        out[40:80, :] = acc


def bottom_sums(fn, tmp):
    for f in range(F):
        for lt in range(2):
            at = (f * FZ + FZ - 1) * 4 + lt * 2
            tmp[f : f + 1, lt * L : (lt + 1) * L] = fn[at : at + 1, :] + fn[at + 1 : at + 2, :]


def pack_x(fn, cn, tp, pool, outs, tmp):
    px = lax.rem(lax.axis_index("gx"), 2)
    tmp[...] = jnp.zeros_like(tmp)
    bottom_sums(fn, tmp)
    ridge = exact_dot(tmp[...], pool[0:256, 0:L])
    ma, mbf, mbg = outs
    in_chip = (ma.at[0:HALF, :], ma.at[HALF : 2 * HALF, :])
    for out, a, row in zip((*in_chip, mbf, mbg), (0, 1, 0, 1), (1 - px, 1 - px, px, px)):
        for i in range(3):
            for lt in range(2):
                out[i * 80 + lt * 40 : i * 80 + lt * 40 + 40, :] = fn[fine_rows(a * 3 + i, lt, row), :]
        out[HFINE : HFINE + 3, :] = ridge[a * 3 : a * 3 + 3, :]
        for lt in range(2):
            out[HTOPO + lt : HTOPO + lt + 1, :] = tp[pl.ds(lt * 2 + row, 1), :].astype(F32)
        out[HTOPO + 2 : HCOARSE, :] = jnp.zeros((3, L), F32)
        out[HCOARSE : HCOARSE + 3 * CZ, :] = cn[a * 3 * CZ : (a + 1) * 3 * CZ, :]
        if out.shape[0] > HALF:
            out[HALF : HALF + 8, :] = jnp.zeros((8, L), F32)


def open_y(ryb, rya, fn, pool, fh, foh, sh, th, ch, coh, sch, rg, mca, mcb, tmp):
    px = lax.rem(lax.axis_index("gx"), 2)
    py = lax.rem(lax.axis_index("gy"), 2)
    lane = lanes((FZ, L))
    in_a = ((lane + 4 * py) & 127) < 4
    in_b = ((lane + 4 * (1 - py)) & 127) < 4

    def halo(g, part):
        a = pltpu.roll(rya[part * 40 : part * 40 + 40, :], lax.rem(256 - 4 * g - 4 * py, L), 1)
        b = pltpu.roll(ryb[part * 40 : part * 40 + 40, :], lax.rem(256 - 4 * g - 4 * (1 - py), L), 1)
        return jnp.where(in_a, a, jnp.where(in_b, b, 0.0))

    for q in range(12):
        fh[q] = halo(q, 0)
        foh[q] = halo(12 + q, 0)
    for q in range(4):
        sh[q] = halo(24 + q, 0)
    for x in range(2):
        th[x] = halo(28 + x, 0)[0:8, :]
    for f in range(F):
        for h in range(2):
            ch[f, h * 40 : h * 40 + 40, :] = halo(f * 2 + h, 1)
            coh[f, h * 40 : h * 40 + 40, :] = halo(12 + f * 2 + h, 1)
    for q in range(2):
        for h in range(2):
            sch[q, h * 40 : h * 40 + 40, :] = halo(24 + q * 2 + h, 1)
    tmp[...] = jnp.zeros_like(tmp)
    bottom_sums(fn, tmp)
    for f in range(F):
        tmp[f : f + 1, 2 * L : 3 * L] = fh[f * 2, 39:40, :] + fh[f * 2 + 1, 39:40, :]
    rg[...] = exact_dot(tmp[...], pool[...])
    group = lane >> 3
    for out, row in ((mca, 1 - px), (mcb, px)):
        acc = jnp.zeros((FZ, L), F32)
        for f in range(F):
            acc = jnp.where(group == f, pltpu.roll(fh[f * 2 + row], 4 + 8 * f, 1), acc)
        acc = jnp.where(group == 6, pltpu.roll(jnp.broadcast_to(th[row, 0:1, :], (FZ, L)), 4 + 8 * 6, 1), acc)
        for f in range(F):
            g = 7 + f
            acc = jnp.where(group == g, pltpu.roll(jnp.broadcast_to(rg[f : f + 1, L : 2 * L], (FZ, L)), 4 + 8 * g, 1), acc)
        out[0:40, :] = acc
    acc = jnp.zeros((FZ, L), F32)
    for f in range(F):
        for h in range(2):
            g = f * 2 + h
            acc = jnp.where(group == g, pltpu.roll(ch[f, h * 40 : h * 40 + 40, :], (4 + 8 * g) % L, 1), acc)
    mca[40:80, :] = acc
    mcb[40:80, :] = acc


def ring_sum_diff(tiles_sum, tiles_diff, lane):
    def shifted(tiles):
        up = [pltpu.roll(t, L - 1, 1) for t in tiles]
        down = [pltpu.roll(t, 1, 1) for t in tiles]
        n = len(tiles)
        up = [jnp.where(lane < L - 1, up[t], up[(t + 1) % n]) for t in range(n)]
        down = [jnp.where(lane > 0, down[t], down[(t - 1) % n]) for t in range(n)]
        return up, down

    a, b = shifted(tiles_sum)
    c, d = shifted(tiles_diff)
    return [p + q for p, q in zip(a, b)], [p - q for p, q in zip(c, d)]


def vector_piece(load, own, nt, inv2j, invjj, h, lane):
    ia = 1.0 / (h * h)
    q = 0.25 * ia
    s = 0.5 / h
    cache = {}

    def u(i, r, t, dz=0):
        key = (i, r, t, dz)
        if key not in cache:
            cache[key] = load(i, r, t, dz)
        return cache[key]

    grads = {}

    def g(i, r, t):
        key = (i, r, t)
        if key not in grads:
            grads[key] = (u(i, r, t, 1) - u(i, r, t, -1)) * (inv2j(r, t) * s)
        return grads[key]

    out = {}
    ts = range(nt)
    for r in own:
        inner = (
            [q * (u(1, r + 1, t) - u(1, r - 1, t)) for t in ts],
            [q * (u(0, r + 1, t) - u(0, r - 1, t)) + g(2, r, t) for t in ts],
            [g(1, r, t) for t in ts],
        )
        for i in range(3):
            side, mixed = ring_sum_diff([u(i, r, t) for t in ts], inner[i], lane)
            for t in ts:
                c = u(i, r, t)
                c2 = c + c
                xx = (u(i, r + 1, t) + u(i, r - 1, t) - c2) * ia
                yy = (side[t] - c2) * ia
                zz = (u(i, r, t, 1) + u(i, r, t, -1) - c2) * invjj(r, t)
                cross = mixed[t]
                if i == 0:
                    cross = cross + (g(2, r + 1, t) - g(2, r - 1, t))
                if i == 2:
                    cross = cross + (g(0, r + 1, t) - g(0, r - 1, t))
                out[i, r, t] = (c2, xx + yy + zz, (xx, yy, zz)[i] + cross)
    return out


def interpolate(cc, spread, edges, lane8):
    left, right, low, high = edges
    a, b, c = cc[0], cc[1], cc[2]
    zero = jnp.zeros_like(a)
    mixes = [
        jnp.where(left, 0.75 * a + 0.25 * b, zero),
        0.75 * b + 0.25 * a,
        0.75 * b + 0.25 * c,
        jnp.where(right, 0.75 * c + 0.25 * b, zero),
    ]
    plane = exact_dot(jnp.concatenate(mixes, axis=0), spread[...])
    keep = (lane8 < 2 * L) | ((lane8 < 2 * L + 64) & high) | ((lane8 >= 2 * L + 64) & low)
    return jnp.where(keep, plane, 0.0)


def edges_here():
    x, y = lax.axis_index("gx"), lax.axis_index("gy")
    return x > 0, x < lax.axis_size("gx") - 1, y > 0, y < lax.axis_size("gy") - 1


def fill_ghosts(U, V, cc, spread, edges):
    for f in range(3):
        for r in range(3):
            for t in range(2):
                cc[r, f : f + 1, t * L : (t + 1) * L] = V[f, r, t, ZP : ZP + 1, :]
    plane = interpolate(cc, spread, edges, lanes((32, 384)))
    for f in range(3):
        for r in range(4):
            for t in range(3):
                U[f, r, t, ZP + FZ : ZP + FZ + 1, :] = plane[r * 8 + f : r * 8 + f + 1, t * L : (t + 1) * L]
                U[f, r, t, ZP - 1 : ZP, :] = U[f, r, t, ZP : ZP + 1, :]
        for r in range(3):
            for t in range(2):
                V[f, r, t, ZP + CZ : ZP + CZ + 1, :] = jnp.zeros((1, L), F32)


def one_field(kernel, a):
    def body(*refs):
        kernel(a, *refs)

    body.__name__ = kernel.__name__
    return body


def fine_pieces(U, jv, lane):
    for k in range(FZ // 8):
        at = ZP + 8 * k
        parts = vector_piece(
            lambda i, r, t, dz: U[i, r, t, at + dz : at + dz + 8, :], (1, 2), 3,
            lambda r, t: jv[0, r, t], lambda r, t: jv[1, r, t], 1.0, lane,
        )
        for (i, r, t), values in parts.items():
            yield k, i, r - 1, t, values


def coarse_pieces(V, lane):
    for k in range(CZ // 8):
        at = ZP + 8 * k
        parts = vector_piece(
            lambda i, r, t, dz: V[i, r, t, at + dz : at + dz + 8, :], (1,), 2,
            lambda r, t: 0.25, lambda r, t: 0.25, 2.0, lane,
        )
        for (i, r, t), values in parts.items():
            yield k, i, t, values


def step_one(
    a, fn, fo, cn, co, sf, lf, sc, lc, tp, fh, foh, sh, th, ch, coh, sch, rg, rxa, rxb, rca, rcb, spread, pool,
    f1, c1, c1h, rg1, mxa, mxb, jv, cf, cv, U, V, cc, tmp,
):
    px = lax.rem(lax.axis_index("gx"), 2)
    edges = edges_here()
    lane = lanes((8, L))
    lane40 = lanes((FZ, L))
    near40 = ((lane40 + 4) & 127) < 8

    def corner(rc, part, g):
        return jnp.where(near40, pltpu.roll(rc[part * 40 : part * 40 + 40, :], (2 * L - 4 - 8 * g) % L, 1), 0.0)

    cc[...] = jnp.zeros_like(cc)
    body = slice(ZP, ZP + FZ)
    for i in range(3):
        f = 3 * a + i
        for x in range(2):
            for t in range(2):
                U[i, 1 + x, t, body, :] = fn[fine_rows(f, t, x), :]
            U[i, 1 + x, 2, body, :] = fh[f * 2 + x]
        V[i, 1, 0, ZP : ZP + CZ, :] = cn[f * CZ : (f + 1) * CZ, :]
        V[i, 1, 1, ZP : ZP + CZ, :] = ch[f]
        for t in range(2):
            V[i, 1, t, ZP - 1 : ZP, :] = rg[f : f + 1, t * L : (t + 1) * L]
    for rx, rc, fr, cr in ((rxa.at[a * HALF : (a + 1) * HALF, :], rca, 3 * (1 - px), 2 * (1 - px)), (rxb, rcb, 3 * px, 2 * px)):
        for i in range(3):
            f = 3 * a + i
            for t in range(2):
                U[i, fr, t, body, :] = rx[i * 80 + t * 40 : i * 80 + t * 40 + 40, :]
            U[i, fr, 2, body, :] = corner(rc, 0, f)
            V[i, cr, 0, ZP : ZP + CZ, :] = rx[HCOARSE + i * CZ : HCOARSE + (i + 1) * CZ, :]
            for half in range(2):
                V[i, cr, 1, ZP + half * 40 : ZP + half * 40 + 40, :] = corner(rc, 1, f * 2 + half)
            V[i, cr, 0, ZP - 1 : ZP, :] = rx[HFINE + i : HFINE + i + 1, :]
            V[i, cr, 1, ZP - 1 : ZP, :] = corner(rc, 0, 7 + f)[0:1, :]
        for t in range(2):
            jv[0, fr, t] = jnp.broadcast_to(rx[HTOPO + t : HTOPO + t + 1, :], (8, L))
        jv[0, fr, 2] = corner(rc, 0, 6)[0:8, :]
    for x in range(2):
        for t in range(2):
            jv[0, 1 + x, t] = jnp.broadcast_to(tp[t * 2 + x : t * 2 + x + 1, :].astype(F32), (8, L))
        jv[0, 1 + x, 2] = th[x]
    for r in range(4):
        for t in range(3):
            spacing = 1.0 + jv[0, r, t] * (1.0 / 1024.0)
            jv[0, r, t] = 1.0 / (2.0 * spacing)
            jv[1, r, t] = 1.0 / (spacing * spacing)
    for x in range(2):
        for t in range(3):
            shear = sf[coef_rows(t, x), :] if t < 2 else sh[x]
            lame = lf[coef_rows(t, x), :] if t < 2 else sh[2 + x]
            cf[0, x, t] = DT2 * shear
            cf[1, x, t] = DT2 * (lame + shear)
    for t in range(2):
        shear = sc[...] if t == 0 else sch[0]
        lame = lc[...] if t == 0 else sch[1]
        cv[0, t] = DT2 * shear
        cv[1, t] = DT2 * (lame + shear)
    fill_ghosts(U, V, cc, spread, edges)
    keep = ((lane < 64) & edges[3]) | ((lane >= 64) & edges[2])
    for k, i, x, t, (c2, lap, gd) in fine_pieces(U, jv, lane):
        f = 3 * a + i
        zs = slice(8 * k, 8 * k + 8)
        old = fo[fine_rows(f, t, x, 8 * k, 8), :] if t < 2 else foh[f * 2 + x, zs, :]
        new = c2 - old + cf[0, x, t, zs, :] * lap + cf[1, x, t, zs, :] * gd
        f1[i * 2 + x, t, zs, :] = new if t < 2 else jnp.where(keep, new, 0.0)
    for k, i, t, (c2, lap, gd) in coarse_pieces(V, lane):
        f = 3 * a + i
        zs = slice(8 * k, 8 * k + 8)
        old = co[f * CZ + 8 * k : f * CZ + 8 * k + 8, :] if t == 0 else coh[f, zs, :]
        new = c2 - old + cv[0, t, zs, :] * lap + cv[1, t, zs, :] * gd
        if t == 0:
            c1[i * CZ + 8 * k : i * CZ + 8 * k + 8, :] = new
        else:
            c1h[i, zs, :] = jnp.where(keep, new, 0.0)
    tmp[...] = jnp.zeros_like(tmp)
    for i in range(3):
        for t in range(3):
            tmp[i : i + 1, t * L : (t + 1) * L] = f1[i * 2, t, FZ - 1 : FZ, :] + f1[i * 2 + 1, t, FZ - 1 : FZ, :]
    rg1[...] = exact_dot(tmp[...], pool[...])
    for out, row in ((mxb, px), (mxa, 1 - px)):
        for i in range(3):
            for t in range(2):
                out[i * 80 + t * 40 : i * 80 + t * 40 + 40, :] = f1[i * 2 + row, t]
        out[HFINE:HCOARSE, :] = rg1[:, 0:L]
        out[HCOARSE:HLATER, :] = later_corners(f1, c1h, row, lane40)
        out[HLATER : HLATER + 3 * CZ, :] = c1[...]
    mxb[HALF + 40 : HALF + 48, :] = jnp.zeros((8, L), F32)


def later_corners(f1, c1h, row, lane40):
    group = lane40 >> 2
    acc = jnp.zeros((FZ, L), F32)
    for i in range(3):
        acc = jnp.where(group == i, pltpu.roll(f1[i * 2 + row, 2], 2 + 4 * i, 1), acc)
        for half in range(2):
            g = 3 + 2 * i + half
            acc = jnp.where(group == g, pltpu.roll(c1h[i, half * 40 : half * 40 + 40, :], 2 + 4 * g, 1), acc)
    return acc


def step_two(a, fn, cn, f1, c1, c1h, rg1, rxa, rxb, jv, cf, cv, spread, fout, cout, U, V, cc, after_fine=None):
    px = lax.rem(lax.axis_index("gx"), 2)
    edges = edges_here()
    lane = lanes((8, L))
    near40 = ((lanes((FZ, L)) + 2) & 127) < 4

    def corner(rx, g):
        return jnp.where(near40, pltpu.roll(rx[HCOARSE:HLATER, :], (2 * L - 2 - 4 * g) % L, 1), 0.0)

    cc[...] = jnp.zeros_like(cc)
    body = slice(ZP, ZP + FZ)
    for i in range(3):
        for x in range(2):
            for t in range(3):
                U[i, 1 + x, t, body, :] = f1[i * 2 + x, t]
        V[i, 1, 0, ZP : ZP + CZ, :] = c1[i * CZ : (i + 1) * CZ, :]
        V[i, 1, 1, ZP : ZP + CZ, :] = c1h[i]
        for t in range(2):
            V[i, 1, t, ZP - 1 : ZP, :] = rg1[i : i + 1, t * L : (t + 1) * L]
    for rx, fr, cr in ((rxa, 3 * (1 - px), 2 * (1 - px)), (rxb, 3 * px, 2 * px)):
        for i in range(3):
            for t in range(2):
                U[i, fr, t, body, :] = rx[i * 80 + t * 40 : i * 80 + t * 40 + 40, :]
            U[i, fr, 2, body, :] = corner(rx, i)
            V[i, cr, 0, ZP : ZP + CZ, :] = rx[HLATER + i * CZ : HLATER + (i + 1) * CZ, :]
            for half in range(2):
                V[i, cr, 1, ZP + half * 40 : ZP + half * 40 + 40, :] = corner(rx, 3 + i * 2 + half)
            V[i, cr, 0, ZP - 1 : ZP, :] = rx[HFINE + i : HFINE + i + 1, :]
            V[i, cr, 1, ZP - 1 : ZP, :] = jnp.zeros((1, L), F32)
    fill_ghosts(U, V, cc, spread, edges)
    for k, i, x, t, (c2, lap, gd) in fine_pieces(U, jv, lane):
        if t < 2:
            zs = slice(8 * k, 8 * k + 8)
            old = fn[fine_rows(3 * a + i, t, x, 8 * k, 8), :]
            fout[fine_rows(i, t, x, 8 * k, 8), :] = c2 - old + cf[0, x, t, zs, :] * lap + cf[1, x, t, zs, :] * gd
    if after_fine is not None:
        after_fine()
    for k, i, t, (c2, lap, gd) in coarse_pieces(V, lane):
        if t == 0:
            zs = slice(8 * k, 8 * k + 8)
            f = 3 * a + i
            old = cn[f * CZ + 8 * k : f * CZ + 8 * k + 8, :]
            cout[i * CZ + 8 * k : i * CZ + 8 * k + 8, :] = c2 - old + cv[0, t, zs, :] * lap + cv[1, t, zs, :] * gd


def step_two_first(fn, cn, f1, c1, c1h, rg1, rxa, rxb, jv, cf, cv, spread, f1g, c1g, fout, cout, fk1, ck1, U, V, cc):
    step_two(0, fn, cn, f1, c1, c1h, rg1, rxa, rxb, jv, cf, cv, spread, fout, cout, U, V, cc)
    for q in range(4):
        x, t = q // 2, q % 2
        total = jnp.zeros((FZ, L), F32)
        for i in range(3):
            total = total + f1[i * 2 + x, t] * f1g[i * 2 + x, t]
        fk1[q] = total
    total = jnp.zeros((CZ, L), F32)
    for i in range(3):
        total = total + c1[i * CZ : (i + 1) * CZ, :] * c1g[i * CZ : (i + 1) * CZ, :]
    ck1[...] = total


def step_two_last(
    fn, cn, f1, c1, c1h, rg1, rxa, rxb, jv, cf, cv, spread, fof, cof, fk1, ck1,
    fout, cout, fk, ck, U, V, cc, fog, cog, fks, cks, sems,
):
    half_f, half_c = 3 * FZ * 4, 3 * CZ
    copies = [
        pltpu.make_async_copy(fof, fout.at[0:half_f, :], sems.at[0]),
        pltpu.make_async_copy(cof, cout.at[0:half_c, :], sems.at[1]),
        pltpu.make_async_copy(fog, fout.at[half_f : 2 * half_f, :], sems.at[2]),
        pltpu.make_async_copy(cog, cout.at[half_c : 2 * half_c, :], sems.at[3]),
        pltpu.make_async_copy(fks, fk, sems.at[4]),
        pltpu.make_async_copy(cks, ck, sems.at[5]),
    ]
    copies[0].start()
    copies[1].start()

    def fine_done():
        copies[2].start()

    step_two(1, fn, cn, f1, c1, c1h, rg1, rxa, rxb, jv, cf, cv, spread, fog, cog, U, V, cc, fine_done)
    copies[3].start()
    total = ck1[...]
    for i in range(3):
        total = total + cof[i * CZ : (i + 1) * CZ, :] * cog[i * CZ : (i + 1) * CZ, :]
    cks[...] = total
    copies[5].start()
    for x in range(2):
        for t in range(2):
            total = fk1[x * 2 + t]
            for i in range(3):
                total = total + fof[fine_rows(i, t, x), :] * fog[fine_rows(i, t, x), :]
            fks[coef_rows(t, x), :] = total
    copies[4].start()
    for copy in copies:
        copy.wait()


def call(kernel, args, outs, scratch, space=VM, megabytes=12, flops=0, out_space=VM):
    shapes = tuple(jax.ShapeDtypeStruct(s, F32) if isinstance(s, tuple) else s for s in outs)
    return pl.pallas_call(
        kernel,
        out_shape=shapes,
        in_specs=[space] * len(args),
        out_specs=(out_space,) * len(outs),
        scratch_shapes=[pltpu.VMEM(s, F32) if isinstance(s, tuple) else s for s in scratch],
        cost_estimate=pl.CostEstimate(flops=flops, transcendentals=0, bytes_accessed=1024) if flops else None,
        compiler_params=pltpu.CompilerParams(vmem_limit_bytes=megabytes * 1024 * 1024),
    )(*args)


def swap(cells, axis, first):
    count = lax.axis_size(axis)
    return lax.ppermute(cells, axis, [p for i in range(first, count - 1, 2) for p in ((i, i + 1), (i + 1, i))])


def rows_of(array):
    lead = array.size // 512
    return array.reshape(lead, 2, 2, L).transpose(0, 2, 1, 3).reshape(lead * 4, L)


def fine_of(rows, shape):
    return rows.reshape(-1, 2, 2, L).transpose(0, 2, 1, 3).reshape(shape)


def on_device(fine_old, fine_now, coarse_old, coarse_now, shear_fine, lame_fine, shear_coarse, lame_coarse, topography):
    fo, fn, sf, lf = rows_of(fine_old), rows_of(fine_now), rows_of(shear_fine), rows_of(lame_fine)
    tp = rows_of(topography)
    co, cn = coarse_old.reshape(-1, L), coarse_now.reshape(-1, L)
    sc, lc = shear_coarse.reshape(-1, L), lame_coarse.reshape(-1, L)
    pool, spread = jnp.asarray(POOL), jnp.asarray(SPREAD)
    raw = (fn, fo, cn, co, sf, lf, sc, lc, tp, pool, spread)
    raw = tuple(pltpu.with_memory_space_constraint(v, pltpu.HBM) for v in raw)
    local = call(
        load_and_pack_y,
        raw,
        tuple(jax.ShapeDtypeStruct(v.shape, v.dtype) for v in raw) + ((2 * HALF, L), (HALF + 8, L), (HALF + 8, L), (80, L), (80, L)),
        ((8, 256), pltpu.SemaphoreType.DMA((len(raw),)),),
        pl.BlockSpec(memory_space=pltpu.HBM),
    )
    fn, fo, cn, co, sf, lf, sc, lc, tp, pool, spread, ma, mbf, mbg, mya, myb = local
    ryb = swap(myb, "gy", 1)
    rya = swap(mya, "gy", 0)
    by_link = [swap(m, "gx", 1) for m in (mbf, mbg)]
    in_chip = swap(ma, "gx", 0)
    fh, foh, sh, th, ch, coh, sch, rg, mca, mcb = call(
        open_y,
        (ryb, rya, fn, pool),
        ((12, FZ, L), (12, FZ, L), (4, FZ, L), (2, 8, L), (F, CZ, L), (F, CZ, L), (2, CZ, L), (8, 256), (80, L), (80, L)),
        ((8, 384),),
        flops=C_OPEN,
    )
    rcb = swap(mcb, "gx", 1)
    rca = swap(mca, "gx", 0)
    field = ((3, 4, 3, 56, L), (3, 3, 2, 96, L), (3, 8, 256))
    firsts, far, near = [], [], []
    for a in range(2):
        *results, mxa, mxb, jv, cf, cv = call(
            one_field(step_one, a),
            (fn, fo, cn, co, sf, lf, sc, lc, tp, fh, foh, sh, th, ch, coh, sch, rg, in_chip, by_link[a], rca, rcb, spread, pool),
            ((6, 3, FZ, L), (3 * CZ, L), (3, CZ, L), (8, 256), (HALF + 40, L), (HALF + 48, L), (2, 4, 3, 8, L), (2, 2, 3, FZ, L), (2, 2, CZ, L)),
            field + ((8, 384),),
            flops=C_ONE[a],
        )
        firsts.append(results)
        far.append(swap(mxb, "gx", 1))
        near.append(swap(mxa, "gx", 0))
    fof, cof, fk1, ck1 = call(
        step_two_first,
        (fn, cn, *firsts[0], near[0], far[0], jv, cf, cv, spread, *firsts[1][:2]),
        ((3 * FZ * 4, L), (3 * CZ, L), (4, FZ, L), (CZ, L)),
        field,
        flops=C_TWO,
    )
    fout, cout, fk, ck = call(
        step_two_last,
        (fn, cn, *firsts[1], near[1], far[1], jv, cf, cv, spread, fof, cof, fk1, ck1),
        ((FINE_ROWS, L), (COARSE_ROWS, L), (4 * FZ, L), (CZ, L)),
        field + ((3 * FZ * 4, L), (3 * CZ, L), (4 * FZ, L), (CZ, L), pltpu.SemaphoreType.DMA((6,))),
        out_space=pl.BlockSpec(memory_space=pltpu.HBM),
    )
    return (
        fine_of(fout, fine_now.shape),
        cout.reshape(coarse_now.shape),
        fine_of(fk, shear_fine.shape),
        ck.reshape(shear_coarse.shape),
    )


def solution(mesh):
    fields = P(None, None, None, "gx", "gy")
    cells = P(None, "gx", "gy")
    return jax.shard_map(
        on_device,
        mesh=mesh,
        in_specs=(fields, fields, fields, fields, cells, cells, cells, cells, P("gx", "gy")),
        out_specs=(fields, fields, cells, cells),
        check_vma=False,
    )
```

time: 53.1 us -> 43.4 us (0.82)
  the two profiles are of different devices: /device:TPU:153 before, /device:TPU:106 now
where the time goes in v4:
time: 43.4 us; the launch traced here: 43.1 us
  starting transfers between devices  25.9 us (60%)
  Pallas kernels  9.25 us (21%)
  waiting for transfers between devices  7.21 us (17%)
  between operations  0.76 us (2%)
    ppermute x11, starting transfers between devices, swap(): lax.ppermute(cells, axis, [p for i in range(first, count - 1, 2) for p in...  25.9 us
    pallas_call x6, Pallas kernels, call(): pl.pallas_call(kernel, out_shape=shapes, in_specs=[space] * len(args), ou...  9.25 us
    ppermute x11, waiting for transfers between devices, swap(): lax.ppermute(cells, axis, [p for i in range(first, count - 1, 2) for p in...  7.21 us
  transfers between devices with their start and end apart: 11, of which 4 were waited for; matrix products, arithmetic and copies ran while one was open for 0% of the time, Pallas kernels for 12%

profile of v4, /device:TPU:106, one launch (start us, length us, event | category | flops | bytes accessed | tf_op | source)
XLA Modules:
  0.0 43.1 jit_solution(13717191520295620214)
XLA Ops:
  0.6 2.4 %shard_map.138 = (f32[960,128]{1,0:T(8,128)S(1)}, f32[960,128]{1,0:T(8,128)S(1)}, f32[480,128]{1,0:T(8,128)S(1)}, f32[480,128]{1,0:T(8,128)S(1)}, f32[160,128]{1...) custom-call(f32[960,128]{1,0:T(8,128)} %bitcast.45, ...), custom_call_target="tpu_custom_call" | custom-call | tf_op jit(solution)/shard_map/pallas_call | solution.py:516
  3.0 3.9 %collective-permute-start = (f32[80,128]{1,0:T(8,128)S(1)}, f32[80,128]{1,0:T(8,128)S(1)}, u32[]{:S(2)}, u32[]{:S(2)}) collective-permute-start(f32[80,128]{1,0:T(8,128)S(1)} %get-tuple-element.62), channel_id=1, source_target_pairs={{1,2},{2,1},{3,4},{4,3},{5,6},{6,5},{9,10},{10,9},{11,12},{12,11},... | collective-permute-start | bytes 122888 | tf_op jit(solution)/shard_map/ppermute | solution.py:529
  6.9 2.6 %collective-permute-start.1 = (f32[80,128]{1,0:T(8,128)S(1)}, f32[80,128]{1,0:T(8,128)S(1)}, u32[]{:S(2)}, u32[]{:S(2)}) collective-permute-start(f32[80,128]{1,0:T(8,128)S(1)} %get-tuple-element.63), channel_id=1, source_target_pairs={{0,1},{1,0},{2,3},{3,2},{4,5},{5,4},{6,7},{7,6},{8,9},{9,8},{10,11... | collective-permute-start | bytes 122888 | tf_op jit(solution)/shard_map/ppermute | solution.py:529
  9.6 0.0 collective-permute-start.2
  9.6 2.5 %collective-permute-start.8 = (f32[496,128]{1,0:T(8,128)S(1)}, f32[496,128]{1,0:T(8,128)S(1)}, u32[]{:S(2)}, u32[]{:S(2)}) collective-permute-start(f32[496,128]{1,0:T(8,128)S(1)} %get-tuple-element.87), channel_id=1, source_target_pairs={{8,16},{16,8},{24,32},{32,24},{40,48},{48,40},{56,64},{64,56},{72,... | collective-permute-start | bytes 761864 | tf_op jit(solution)/shard_map/ppermute | solution.py:529
  12.1 0.0 collective-permute-done.ryb
  12.1 0.4 collective-permute-done.1.rya
  12.5 0.8 %shard_map.139 = (f32[12,40,128]{2,1,0:T(8,128)S(1)}, f32[12,40,128]{2,1,0:T(8,128)S(1)}, f32[4,40,128]{2,1,0:T(8,128)S(1)}, f32[2,8,128]{2,1,0:T(8,128)S(1)}, f...) custom-call(f32[80,128]{1,0:T(8,128)S(1)} %collective-permute-done.r, ...), custom_call_target="tpu_custom_call" | custom-call | flops 5000000000 | bytes 1024 | tf_op jit(solution)/shard_map/pallas_call | solution.py:516
  13.4 2.3 %collective-permute-start.4 = (f32[80,128]{1,0:T(8,128)S(1)}, f32[80,128]{1,0:T(8,128)S(1)}, u32[]{:S(2)}, u32[]{:S(2)}) collective-permute-start(f32[80,128]{1,0:T(8,128)S(1)} %get-tuple-element.75), channel_id=1, source_target_pairs={{0,8},{8,0},{16,24},{24,16},{32,40},{40,32},{48,56},{56,48},{64,72... | collective-permute-start | bytes 122888 | tf_op jit(solution)/shard_map/ppermute | solution.py:529
  15.6 1.9 %collective-permute-start.5 = (f32[80,128]{1,0:T(8,128)S(1)}, f32[80,128]{1,0:T(8,128)S(1)}, u32[]{:S(2)}, u32[]{:S(2)}) collective-permute-start(f32[80,128]{1,0:T(8,128)S(1)} %get-tuple-element.76), channel_id=1, source_target_pairs={{8,16},{16,8},{24,32},{32,24},{40,48},{48,40},{56,64},{64,56},{72,... | collective-permute-start | bytes 122888 | tf_op jit(solution)/shard_map/ppermute | solution.py:529
  17.6 3.6 %collective-permute-start.3 = (f32[496,128]{1,0:T(8,128)S(1)}, f32[496,128]{1,0:T(8,128)S(1)}, u32[]{:S(2)}, u32[]{:S(2)}) collective-permute-start(f32[496,128]{1,0:T(8,128)S(1)} %get-tuple-element.74), channel_id=1, source_target_pairs={{8,16},{16,8},{24,32},{32,24},{40,48},{48,40},{56,64},{64,56},{72,... | collective-permute-start | bytes 761864 | tf_op jit(solution)/shard_map/ppermute | solution.py:529
  21.2 0.0 collective-permute-done.4.refs_19_
  21.2 0.0 collective-permute-done.5.refs_20_
  21.2 0.0 collective-permute-done.8.refs_18_
  21.2 0.0 collective-permute-done.2.refs_17_
  21.2 2.0 %shard_map.141 = (f32[6,3,40,128]{3,2,1,0:T(8,128)S(1)}, f32[240,128]{1,0:T(8,128)S(1)}, f32[3,80,128]{2,1,0:T(8,128)S(1)}, f32[8,256]{1,0:T(8,128)S(1)}, f32[52...) custom-call(f32[960,128]{1,0:T(8,128)S(1)} %get-tuple-element.53.fn., ...), custom_call_target="tpu_custom_call" | custom-call | flops 5000000000 | bytes 1024 | tf_op jit(solution)/shard_map/pallas_call | solution.py:516
  23.2 2.0 %collective-permute-start.10 = (f32[536,128]{1,0:T(8,128)S(1)}, f32[536,128]{1,0:T(8,128)S(1)}, u32[]{:S(2)}, u32[]{:S(2)}) collective-permute-start(f32[536,128]{1,0:T(8,128)S(1)} %get-tuple-element.93), channel_id=1, source_target_pairs={{8,16},{16,8},{24,32},{32,24},{40,48},{48,40},{56,64},{64,56},{72,... | collective-permute-start | bytes 823304 | tf_op jit(solution)/shard_map/ppermute | solution.py:529
  25.2 1.0 %collective-permute-done.3.refs_18_ = f32[496,128]{1,0:T(8,128)S(1)} collective-permute-done((f32[496,128]{1,0:T(8,128)S(1)}, f32[496,128]{1,0:T(8,128)S(1)}, u32[]{:S(2)}, u32[]{:S(2)}) %collective-permute-start.3) | collective-permute-done | bytes 253984 | tf_op jit(solution)/shard_map/ppermute | solution.py:529
  26.3 1.3 %shard_map.140 = (f32[6,3,40,128]{3,2,1,0:T(8,128)S(1)}, f32[240,128]{1,0:T(8,128)S(1)}, f32[3,80,128]{2,1,0:T(8,128)S(1)}, f32[8,256]{1,0:T(8,128)S(1)}, f32[52...) custom-call(f32[960,128]{1,0:T(8,128)S(1)} %get-tuple-element.53.fn., ...), custom_call_target="tpu_custom_call" | custom-call | flops 1000000000 | bytes 1024 | tf_op jit(solution)/shard_map/pallas_call | solution.py:516
  27.6 3.8 %collective-permute-start.7 = (f32[536,128]{1,0:T(8,128)S(1)}, f32[536,128]{1,0:T(8,128)S(1)}, u32[]{:S(2)}, u32[]{:S(2)}) collective-permute-start(f32[536,128]{1,0:T(8,128)S(1)} %get-tuple-element.83), channel_id=1, source_target_pairs={{8,16},{16,8},{24,32},{32,24},{40,48},{48,40},{56,64},{64,56},{72,... | collective-permute-start | bytes 823304 | tf_op jit(solution)/shard_map/ppermute | solution.py:529
  31.4 3.0 %collective-permute-start.9 = (f32[528,128]{1,0:T(8,128)S(1)}, f32[528,128]{1,0:T(8,128)S(1)}, u32[]{:S(2)}, u32[]{:S(2)}) collective-permute-start(f32[528,128]{1,0:T(8,128)S(1)} %get-tuple-element.92), channel_id=1, source_target_pairs={{0,8},{8,0},{16,24},{24,16},{32,40},{40,32},{48,56},{56,48},{64,72... | collective-permute-start | bytes 811016 | tf_op jit(solution)/shard_map/ppermute | solution.py:529
  34.4 0.1 collective-permute-start.6
  34.5 1.1 %collective-permute-done.9.rxa = f32[528,128]{1,0:T(8,128)S(1)} collective-permute-done((f32[528,128]{1,0:T(8,128)S(1)}, f32[528,128]{1,0:T(8,128)S(1)}, u32[]{:S(2)}, u32[]{:S(2)}) %collective-permute-start.9) | collective-permute-done | bytes 270368 | tf_op jit(solution)/shard_map/ppermute | solution.py:529
  35.6 0.0 collective-permute-done.10.rxb
  35.6 1.0 %shard_map.142 = (f32[480,128]{1,0:T(8,128)S(1)}, f32[240,128]{1,0:T(8,128)S(1)}, f32[4,40,128]{2,1,0:T(8,128)S(1)}, f32[80,128]{1,0:T(8,128)S(1)}) custom-call(f32[960,128]{1,0:T(8,128)S(1)} %get-tuple-element.53.fn.refs_0_, f32[480,128]{1,0:T(8,128)S(1)} %get-tuple-element.54.refs_2_.cn, f32[6,3,40,128]{3,2,1,0:T(8,128)S(1)} %get-tuple-element.88.f1, ...), custom_call_target="tpu_custom_call" | custom-call | flops 1 | bytes 1024 | tf_op jit(solution)/shard_map/pallas_call | solution.py:516
  36.6 0.0 collective-permute-done.6.rxa
  36.7 4.7 %collective-permute-done.7.rxb = f32[536,128]{1,0:T(8,128)S(1)} collective-permute-done((f32[536,128]{1,0:T(8,128)S(1)}, f32[536,128]{1,0:T(8,128)S(1)}, u32[]{:S(2)}, u32[]{:S(2)}) %collective-permute-start.7) | collective-permute-done | bytes 274464 | tf_op jit(solution)/shard_map/ppermute | solution.py:529
  41.3 1.8 %shard_map.143 = (f32[960,128]{1,0:T(8,128)}, f32[480,128]{1,0:T(8,128)}, f32[160,128]{1,0:T(8,128)}, f32[80,128]{1,0:T(8,128)}) custom-call(f32[960,128]{1,0:T(8,128)S(1)} %get-tuple-element.53.fn.refs_0_, f32[480,128]{1,0:T(8,128)S(1)} %get-tuple-element.54.refs_2_.cn, f32[6,3,40,128]{3,2,1,0:T(8,128)S(1)} %get-tuple-element.78.f1g.f1, ...), custom_call_target="tpu_custom_call" | custom-call | tf_op jit(solution)/shard_map/pallas_call | solution.py:516
Async XLA Ops:
  3.0 9.1 %collective-permute-start = (f32[80,128]{1,0:T(8,128)S(1)}, f32[80,128]{1,0:T(8,128)S(1)}, u32[]{:S(2)}, u32[]{:S(2)}) collective-permute-start(f32[80,128]{1,0:T(8,128)S(1)} %get-tuple-element.62), channel_id=1, source_target_pairs={{1,2},{2,1},{3,4},{4,3},{5,6},{6,5},{9,10},{10,9},{11,12},{12,11},... | collective-permute-start | bytes 122888 | tf_op jit(solution)/shard_map/ppermute | solution.py:529
  6.9 5.6 %collective-permute-start.1 = (f32[80,128]{1,0:T(8,128)S(1)}, f32[80,128]{1,0:T(8,128)S(1)}, u32[]{:S(2)}, u32[]{:S(2)}) collective-permute-start(f32[80,128]{1,0:T(8,128)S(1)} %get-tuple-element.63), channel_id=1, source_target_pairs={{0,1},{1,0},{2,3},{3,2},{4,5},{5,4},{6,7},{7,6},{8,9},{9,8},{10,11... | collective-permute-start | bytes 122888 | tf_op jit(solution)/shard_map/ppermute | solution.py:529
  9.6 11.7 %collective-permute-start.2 = (f32[976,128]{1,0:T(8,128)S(1)}, f32[976,128]{1,0:T(8,128)S(1)}, u32[]{:S(2)}, u32[]{:S(2)}) collective-permute-start(f32[976,128]{1,0:T(8,128)S(1)} %get-tuple-element.73), channel_id=1, source_target_pairs={{0,8},{8,0},{16,24},{24,16},{32,40},{40,32},{48,56},{56,48},{64,72... | collective-permute-start | bytes 1499144 | tf_op jit(solution)/shard_map/ppermute | solution.py:529
  9.6 11.7 %collective-permute-start.8 = (f32[496,128]{1,0:T(8,128)S(1)}, f32[496,128]{1,0:T(8,128)S(1)}, u32[]{:S(2)}, u32[]{:S(2)}) collective-permute-start(f32[496,128]{1,0:T(8,128)S(1)} %get-tuple-element.87), channel_id=1, source_target_pairs={{8,16},{16,8},{24,32},{32,24},{40,48},{48,40},{56,64},{64,56},{72,... | collective-permute-start | bytes 761864 | tf_op jit(solution)/shard_map/ppermute | solution.py:529
  13.4 7.8 %collective-permute-start.4 = (f32[80,128]{1,0:T(8,128)S(1)}, f32[80,128]{1,0:T(8,128)S(1)}, u32[]{:S(2)}, u32[]{:S(2)}) collective-permute-start(f32[80,128]{1,0:T(8,128)S(1)} %get-tuple-element.75), channel_id=1, source_target_pairs={{0,8},{8,0},{16,24},{24,16},{32,40},{40,32},{48,56},{56,48},{64,72... | collective-permute-start | bytes 122888 | tf_op jit(solution)/shard_map/ppermute | solution.py:529
  15.6 5.6 %collective-permute-start.5 = (f32[80,128]{1,0:T(8,128)S(1)}, f32[80,128]{1,0:T(8,128)S(1)}, u32[]{:S(2)}, u32[]{:S(2)}) collective-permute-start(f32[80,128]{1,0:T(8,128)S(1)} %get-tuple-element.76), channel_id=1, source_target_pairs={{8,16},{16,8},{24,32},{32,24},{40,48},{48,40},{56,64},{64,56},{72,... | collective-permute-start | bytes 122888 | tf_op jit(solution)/shard_map/ppermute | solution.py:529
  17.6 8.7 %collective-permute-start.3 = (f32[496,128]{1,0:T(8,128)S(1)}, f32[496,128]{1,0:T(8,128)S(1)}, u32[]{:S(2)}, u32[]{:S(2)}) collective-permute-start(f32[496,128]{1,0:T(8,128)S(1)} %get-tuple-element.74), channel_id=1, source_target_pairs={{8,16},{16,8},{24,32},{32,24},{40,48},{48,40},{56,64},{64,56},{72,... | collective-permute-start | bytes 761864 | tf_op jit(solution)/shard_map/ppermute | solution.py:529
  23.2 12.4 %collective-permute-start.10 = (f32[536,128]{1,0:T(8,128)S(1)}, f32[536,128]{1,0:T(8,128)S(1)}, u32[]{:S(2)}, u32[]{:S(2)}) collective-permute-start(f32[536,128]{1,0:T(8,128)S(1)} %get-tuple-element.93), channel_id=1, source_target_pairs={{8,16},{16,8},{24,32},{32,24},{40,48},{48,40},{56,64},{64,56},{72,... | collective-permute-start | bytes 823304 | tf_op jit(solution)/shard_map/ppermute | solution.py:529
  27.6 13.7 %collective-permute-start.7 = (f32[536,128]{1,0:T(8,128)S(1)}, f32[536,128]{1,0:T(8,128)S(1)}, u32[]{:S(2)}, u32[]{:S(2)}) collective-permute-start(f32[536,128]{1,0:T(8,128)S(1)} %get-tuple-element.83), channel_id=1, source_target_pairs={{8,16},{16,8},{24,32},{32,24},{40,48},{48,40},{56,64},{64,56},{72,... | collective-permute-start | bytes 823304 | tf_op jit(solution)/shard_map/ppermute | solution.py:529
  31.4 4.2 %collective-permute-start.9 = (f32[528,128]{1,0:T(8,128)S(1)}, f32[528,128]{1,0:T(8,128)S(1)}, u32[]{:S(2)}, u32[]{:S(2)}) collective-permute-start(f32[528,128]{1,0:T(8,128)S(1)} %get-tuple-element.92), channel_id=1, source_target_pairs={{0,8},{8,0},{16,24},{24,16},{32,40},{40,32},{48,56},{56,48},{64,72... | collective-permute-start | bytes 811016 | tf_op jit(solution)/shard_map/ppermute | solution.py:529
  34.4 2.2 %collective-permute-start.6 = (f32[528,128]{1,0:T(8,128)S(1)}, f32[528,128]{1,0:T(8,128)S(1)}, u32[]{:S(2)}, u32[]{:S(2)}) collective-permute-start(f32[528,128]{1,0:T(8,128)S(1)} %get-tuple-element.82), channel_id=1, source_target_pairs={{0,8},{8,0},{16,24},{24,16},{32,40},{40,32},{48,56},{56,48},{64,72... | collective-permute-start | bytes 811016 | tf_op jit(solution)/shard_map/ppermute | solution.py:529

commit v5 on v4

--- a/solution.py
+++ b/solution.py
@@ -21,9 +21,10 @@
 HTOPO = HFINE + 3
 HCOARSE = HFINE + 8
 HALF = HCOARSE + 3 * CZ
-HLATER = HCOARSE + 40
-C_OPEN = 5*10**9
-C_ONE = (5*10**9, 10**9)
+CORNERS = 16
+HLATER = HCOARSE + CORNERS
+C_OPEN = 4*10**9
+C_ONE = (4*10**9, 10**9)
 C_TWO = 1
 VM = pl.BlockSpec(memory_space=pltpu.VMEM)
 
@@ -78,11 +79,15 @@
     n = 11
     hbm, (fn, fo, cn, co, sf, lf, sc, lc, tp, pool, spread), (ma, mbf, mbg, mya, myb, tmp, sems) = refs[:n], refs[n : 2 * n], refs[2 * n :]
     copies = [pltpu.make_async_copy(src, dst, sems.at[q]) for q, (src, dst) in enumerate(zip(hbm, refs[n : 2 * n]))]
-    for copy in copies:
-        copy.start()
-    for copy in copies:
-        copy.wait()
+    early = (0, 2, 8, 9)
+    late = [q for q in range(n) if q not in early]
+    for q in (*early, *late):
+        copies[q].start()
+    for q in early:
+        copies[q].wait()
     pack_x(fn, cn, tp, pool, (ma, mbf, mbg), tmp)
+    for q in late:
+        copies[q].wait()
     py = lax.rem(lax.axis_index("gy"), 2)
     group = lanes((FZ, L)) >> 2
     for out, right in ((mya, 1 - py), (myb, py)):
@@ -134,8 +139,6 @@
             out[HTOPO + lt : HTOPO + lt + 1, :] = tp[pl.ds(lt * 2 + row, 1), :].astype(F32)
         out[HTOPO + 2 : HCOARSE, :] = jnp.zeros((3, L), F32)
         out[HCOARSE : HCOARSE + 3 * CZ, :] = cn[a * 3 * CZ : (a + 1) * 3 * CZ, :]
-        if out.shape[0] > HALF:
-            out[HALF : HALF + 8, :] = jnp.zeros((8, L), F32)
 
 
 def open_y(ryb, rya, fn, pool, fh, foh, sh, th, ch, coh, sch, rg, mca, mcb, tmp):
@@ -313,6 +316,29 @@
             yield k, i, t, values
 
 
+def tables(tp, th, sf, lf, sc, lc, sh, sch, jv, cf, cv):
+    for x in range(2):
+        for t in range(2):
+            jv[0, 1 + x, t] = jnp.broadcast_to(tp[t * 2 + x : t * 2 + x + 1, :].astype(F32), (8, L))
+        jv[0, 1 + x, 2] = th[x]
+    for r in range(4):
+        for t in range(3):
+            spacing = 1.0 + jv[0, r, t] * (1.0 / 1024.0)
+            jv[0, r, t] = 1.0 / (2.0 * spacing)
+            jv[1, r, t] = 1.0 / (spacing * spacing)
+    for x in range(2):
+        for t in range(3):
+            shear = sf[coef_rows(t, x), :] if t < 2 else sh[x]
+            lame = lf[coef_rows(t, x), :] if t < 2 else sh[2 + x]
+            cf[0, x, t] = DT2 * shear
+            cf[1, x, t] = DT2 * (lame + shear)
+    for t in range(2):
+        shear = sc[...] if t == 0 else sch[0]
+        lame = lc[...] if t == 0 else sch[1]
+        cv[0, t] = DT2 * shear
+        cv[1, t] = DT2 * (lame + shear)
+
+
 def step_one(
     a, fn, fo, cn, co, sf, lf, sc, lc, tp, fh, foh, sh, th, ch, coh, sch, rg, rxa, rxb, rca, rcb, spread, pool,
     f1, c1, c1h, rg1, mxa, mxb, jv, cf, cv, U, V, cc, tmp,
@@ -349,29 +375,12 @@
                 V[i, cr, 1, ZP + half * 40 : ZP + half * 40 + 40, :] = corner(rc, 1, f * 2 + half)
             V[i, cr, 0, ZP - 1 : ZP, :] = rx[HFINE + i : HFINE + i + 1, :]
             V[i, cr, 1, ZP - 1 : ZP, :] = corner(rc, 0, 7 + f)[0:1, :]
-        for t in range(2):
-            jv[0, fr, t] = jnp.broadcast_to(rx[HTOPO + t : HTOPO + t + 1, :], (8, L))
-        jv[0, fr, 2] = corner(rc, 0, 6)[0:8, :]
-    for x in range(2):
-        for t in range(2):
-            jv[0, 1 + x, t] = jnp.broadcast_to(tp[t * 2 + x : t * 2 + x + 1, :].astype(F32), (8, L))
-        jv[0, 1 + x, 2] = th[x]
-    for r in range(4):
-        for t in range(3):
-            spacing = 1.0 + jv[0, r, t] * (1.0 / 1024.0)
-            jv[0, r, t] = 1.0 / (2.0 * spacing)
-            jv[1, r, t] = 1.0 / (spacing * spacing)
-    for x in range(2):
-        for t in range(3):
-            shear = sf[coef_rows(t, x), :] if t < 2 else sh[x]
-            lame = lf[coef_rows(t, x), :] if t < 2 else sh[2 + x]
-            cf[0, x, t] = DT2 * shear
-            cf[1, x, t] = DT2 * (lame + shear)
-    for t in range(2):
-        shear = sc[...] if t == 0 else sch[0]
-        lame = lc[...] if t == 0 else sch[1]
-        cv[0, t] = DT2 * shear
-        cv[1, t] = DT2 * (lame + shear)
+        if a == 0:
+            for t in range(2):
+                jv[0, fr, t] = jnp.broadcast_to(rx[HTOPO + t : HTOPO + t + 1, :], (8, L))
+            jv[0, fr, 2] = corner(rc, 0, 6)[0:8, :]
+    if a == 0:
+        tables(tp, th, sf, lf, sc, lc, sh, sch, jv, cf, cv)
     fill_ghosts(U, V, cc, spread, edges)
     keep = ((lane < 64) & edges[3]) | ((lane >= 64) & edges[2])
     for k, i, x, t, (c2, lap, gd) in fine_pieces(U, jv, lane):
@@ -401,28 +410,43 @@
         out[HFINE:HCOARSE, :] = rg1[:, 0:L]
         out[HCOARSE:HLATER, :] = later_corners(f1, c1h, row, lane40)
         out[HLATER : HLATER + 3 * CZ, :] = c1[...]
-    mxb[HALF + 40 : HALF + 48, :] = jnp.zeros((8, L), F32)
+    mxb[HALF + CORNERS : HALF + CORNERS + 8, :] = jnp.zeros((8, L), F32)
+
+
+def step_one_adjoint(*refs):
+    step_one(1, *refs[:23], *refs[26:32], *refs[23:26], *refs[32:])
+
+
+def corner_group(k, g):
+    return 4 * (9 * (k // 2) + g)
 
 
 def later_corners(f1, c1h, row, lane40):
-    group = lane40 >> 2
-    acc = jnp.zeros((FZ, L), F32)
-    for i in range(3):
-        acc = jnp.where(group == i, pltpu.roll(f1[i * 2 + row, 2], 2 + 4 * i, 1), acc)
-        for half in range(2):
-            g = 3 + 2 * i + half
-            acc = jnp.where(group == g, pltpu.roll(c1h[i, half * 40 : half * 40 + 40, :], 2 + 4 * g, 1), acc)
-    return acc
+    group = lanes((8, L)) >> 2
+    accs = [jnp.zeros((8, L), F32), jnp.zeros((8, L), F32)]
+    for k in range(FZ // 8):
+        zs = slice(8 * k, 8 * k + 8)
+        for i in range(3):
+            pieces = [(i, f1[i * 2 + row, 2, zs, :])]
+            pieces += [(3 + 2 * i + half, c1h[i, half * 40 + 8 * k : half * 40 + 8 * k + 8, :]) for half in range(2)]
+            for g, piece in pieces:
+                at = corner_group(k, g)
+                accs[k % 2] = jnp.where(group == at // 4, pltpu.roll(piece, (2 + at) % L, 1), accs[k % 2])
+    return jnp.concatenate(accs, axis=0)
 
 
 def step_two(a, fn, cn, f1, c1, c1h, rg1, rxa, rxb, jv, cf, cv, spread, fout, cout, U, V, cc, after_fine=None):
     px = lax.rem(lax.axis_index("gx"), 2)
     edges = edges_here()
     lane = lanes((8, L))
-    near40 = ((lanes((FZ, L)) + 2) & 127) < 4
+    near8 = ((lane + 2) & 127) < 4
 
     def corner(rx, g):
-        return jnp.where(near40, pltpu.roll(rx[HCOARSE:HLATER, :], (2 * L - 2 - 4 * g) % L, 1), 0.0)
+        pieces = []
+        for k in range(FZ // 8):
+            rows = rx[HCOARSE + 8 * (k % 2) : HCOARSE + 8 * (k % 2) + 8, :]
+            pieces.append(jnp.where(near8, pltpu.roll(rows, (2 * L - 2 - corner_group(k, g)) % L, 1), 0.0))
+        return jnp.concatenate(pieces, axis=0)
 
     cc[...] = jnp.zeros_like(cc)
     body = slice(ZP, ZP + FZ)
@@ -549,7 +573,7 @@
     local = call(
         load_and_pack_y,
         raw,
-        tuple(jax.ShapeDtypeStruct(v.shape, v.dtype) for v in raw) + ((2 * HALF, L), (HALF + 8, L), (HALF + 8, L), (80, L), (80, L)),
+        tuple(jax.ShapeDtypeStruct(v.shape, v.dtype) for v in raw) + ((2 * HALF, L), (HALF, L), (HALF, L), (80, L), (80, L)),
         ((8, 256), pltpu.SemaphoreType.DMA((len(raw),)),),
         pl.BlockSpec(memory_space=pltpu.HBM),
     )
@@ -570,13 +594,17 @@
     field = ((3, 4, 3, 56, L), (3, 3, 2, 96, L), (3, 8, 256))
     firsts, far, near = [], [], []
     for a in range(2):
-        *results, mxa, mxb, jv, cf, cv = call(
-            one_field(step_one, a),
-            (fn, fo, cn, co, sf, lf, sc, lc, tp, fh, foh, sh, th, ch, coh, sch, rg, in_chip, by_link[a], rca, rcb, spread, pool),
-            ((6, 3, FZ, L), (3 * CZ, L), (3, CZ, L), (8, 256), (HALF + 40, L), (HALF + 48, L), (2, 4, 3, 8, L), (2, 2, 3, FZ, L), (2, 2, CZ, L)),
-            field + ((8, 384),),
-            flops=C_ONE[a],
-        )
+        args = (fn, fo, cn, co, sf, lf, sc, lc, tp, fh, foh, sh, th, ch, coh, sch, rg, in_chip, by_link[a], rca, rcb, spread, pool)
+        outs = ((6, 3, FZ, L), (3 * CZ, L), (3, CZ, L), (8, 256), (HALF + CORNERS, L), (HALF + CORNERS + 8, L))
+        if a == 0:
+            kernel, outs = one_field(step_one, 0), outs + ((2, 4, 3, 8, L), (2, 2, 3, FZ, L), (2, 2, CZ, L))
+        else:
+            kernel, args = step_one_adjoint, args + (jv, cf, cv)
+        results = call(kernel, args, outs, field + ((8, 384),), flops=C_ONE[a])
+        if a == 0:
+            jv, cf, cv = results[6:]
+        mxa, mxb = results[4:6]
+        results = results[:4]
         firsts.append(results)
         far.append(swap(mxb, "gx", 1))
         near.append(swap(mxa, "gx", 0))

time: 43.4 us -> 43.3 us (level)
  waiting for transfers between devices: 7.21 us -> 8.01 us
  Pallas kernels: 9.25 us -> 8.61 us
    ppermute x11, waiting for transfers between devices: 7.21 us -> 8.01 us  [swap(): lax.ppermute(cells, axis, [p for i in range(first, count - 1, 2) for p in...]
    pallas_call x6, Pallas kernels: 9.25 us -> 8.61 us  [call(): pl.pallas_call(kernel, out_shape=shapes, in_specs=[space] * len(args), ou...]
  transfers between devices with their start and end apart: 11 -> 11, of which waited for: 4 -> 5; matrix products, arithmetic and copies ran while one was open for 0% -> 0% of each run, Pallas kernels for 12% -> 10%
where the time goes in v5:
time: 43.3 us; the launch traced here: 43.1 us
  starting transfers between devices  25.7 us (59%)
  Pallas kernels  8.61 us (20%)
  waiting for transfers between devices  8.01 us (18%)
  between operations  0.77 us (2%)
    ppermute x11, starting transfers between devices, swap(): lax.ppermute(cells, axis, [p for i in range(first, count - 1, 2) for p in...  25.7 us
    pallas_call x6, Pallas kernels, call(): pl.pallas_call(kernel, out_shape=shapes, in_specs=[space] * len(args), ou...  8.61 us
    ppermute x11, waiting for transfers between devices, swap(): lax.ppermute(cells, axis, [p for i in range(first, count - 1, 2) for p in...  8.01 us
  transfers between devices with their start and end apart: 11, of which 5 were waited for; matrix products, arithmetic and copies ran while one was open for 0% of the time, Pallas kernels for 10%

profile of v5, /device:TPU:106, one launch (start us, length us, event | category | flops | bytes accessed | tf_op | source)
XLA Modules:
  0.0 43.1 jit_solution(13787993989099059791)
XLA Ops:
  0.6 2.4 %shard_map.138 = (f32[960,128]{1,0:T(8,128)S(1)}, f32[960,128]{1,0:T(8,128)S(1)}, f32[480,128]{1,0:T(8,128)S(1)}, f32[480,128]{1,0:T(8,128)S(1)}, f32[160,128]{1...) custom-call(f32[960,128]{1,0:T(8,128)} %bitcast.45, ...), custom_call_target="tpu_custom_call" | custom-call | tf_op jit(solution)/shard_map/pallas_call | solution.py:540
  3.0 0.1 collective-permute-start.2
  3.1 3.9 %collective-permute-start = (f32[80,128]{1,0:T(8,128)S(1)}, f32[80,128]{1,0:T(8,128)S(1)}, u32[]{:S(2)}, u32[]{:S(2)}) collective-permute-start(f32[80,128]{1,0:T(8,128)S(1)} %get-tuple-element.62), channel_id=1, source_target_pairs={{1,2},{2,1},{3,4},{4,3},{5,6},{6,5},{9,10},{10,9},{11,12},{12,11},... | collective-permute-start | bytes 122888 | tf_op jit(solution)/shard_map/ppermute | solution.py:553
  7.0 2.6 %collective-permute-start.1 = (f32[80,128]{1,0:T(8,128)S(1)}, f32[80,128]{1,0:T(8,128)S(1)}, u32[]{:S(2)}, u32[]{:S(2)}) collective-permute-start(f32[80,128]{1,0:T(8,128)S(1)} %get-tuple-element.63), channel_id=1, source_target_pairs={{0,1},{1,0},{2,3},{3,2},{4,5},{5,4},{6,7},{7,6},{8,9},{9,8},{10,11... | collective-permute-start | bytes 122888 | tf_op jit(solution)/shard_map/ppermute | solution.py:553
  9.6 2.0 %collective-permute-start.6 = (f32[488,128]{1,0:T(8,128)S(1)}, f32[488,128]{1,0:T(8,128)S(1)}, u32[]{:S(2)}, u32[]{:S(2)}) collective-permute-start(f32[488,128]{1,0:T(8,128)S(1)} %get-tuple-element.78), channel_id=1, source_target_pairs={{8,16},{16,8},{24,32},{32,24},{40,48},{48,40},{56,64},{64,56},{72,... | collective-permute-start | bytes 749576 | tf_op jit(solution)/shard_map/ppermute | solution.py:553
  11.6 0.1 collective-permute-done.ryb
  11.8 0.9 %collective-permute-done.1.rya = f32[80,128]{1,0:T(8,128)S(1)} collective-permute-done((f32[80,128]{1,0:T(8,128)S(1)}, f32[80,128]{1,0:T(8,128)S(1)}, u32[]{:S(2)}, u32[]{:S(2)}) %collective-permute-start.1) | collective-permute-done | bytes 40992 | tf_op jit(solution)/shard_map/ppermute | solution.py:553
  12.6 0.8 %shard_map.139 = (f32[12,40,128]{2,1,0:T(8,128)S(1)}, f32[12,40,128]{2,1,0:T(8,128)S(1)}, f32[4,40,128]{2,1,0:T(8,128)S(1)}, f32[2,8,128]{2,1,0:T(8,128)S(1)}, f...) custom-call(f32[80,128]{1,0:T(8,128)S(1)} %collective-permute-done.r, ...), custom_call_target="tpu_custom_call" | custom-call | flops 4000000000 | bytes 1024 | tf_op jit(solution)/shard_map/pallas_call | solution.py:540
  13.5 2.3 %collective-permute-start.4 = (f32[80,128]{1,0:T(8,128)S(1)}, f32[80,128]{1,0:T(8,128)S(1)}, u32[]{:S(2)}, u32[]{:S(2)}) collective-permute-start(f32[80,128]{1,0:T(8,128)S(1)} %get-tuple-element.75), channel_id=1, source_target_pairs={{0,8},{8,0},{16,24},{24,16},{32,40},{40,32},{48,56},{56,48},{64,72... | collective-permute-start | bytes 122888 | tf_op jit(solution)/shard_map/ppermute | solution.py:553
  15.7 1.9 %collective-permute-start.5 = (f32[80,128]{1,0:T(8,128)S(1)}, f32[80,128]{1,0:T(8,128)S(1)}, u32[]{:S(2)}, u32[]{:S(2)}) collective-permute-start(f32[80,128]{1,0:T(8,128)S(1)} %get-tuple-element.76), channel_id=1, source_target_pairs={{8,16},{16,8},{24,32},{32,24},{40,48},{48,40},{56,64},{64,56},{72,... | collective-permute-start | bytes 122888 | tf_op jit(solution)/shard_map/ppermute | solution.py:553
  17.6 3.6 %collective-permute-start.3 = (f32[488,128]{1,0:T(8,128)S(1)}, f32[488,128]{1,0:T(8,128)S(1)}, u32[]{:S(2)}, u32[]{:S(2)}) collective-permute-start(f32[488,128]{1,0:T(8,128)S(1)} %get-tuple-element.74), channel_id=1, source_target_pairs={{8,16},{16,8},{24,32},{32,24},{40,48},{48,40},{56,64},{64,56},{72,... | collective-permute-start | bytes 749576 | tf_op jit(solution)/shard_map/ppermute | solution.py:553
  21.3 0.0 collective-permute-done.4.refs_19_
  21.3 0.0 collective-permute-done.5.refs_20_
  21.3 0.0 collective-permute-done.6.refs_18_
  21.3 0.0 collective-permute-done.2.refs_17_
  21.3 1.3 %shard_map.140 = (f32[6,3,40,128]{3,2,1,0:T(8,128)S(1)}, f32[240,128]{1,0:T(8,128)S(1)}, f32[3,80,128]{2,1,0:T(8,128)S(1)}, f32[8,256]{1,0:T(8,128)S(1)}, f32[50...) custom-call(f32[960,128]{1,0:T(8,128)S(1)} %get-tuple-element.53.fn., ...), custom_call_target="tpu_custom_call" | custom-call | flops 4000000000 | bytes 1024 | tf_op jit(solution)/shard_map/pallas_call | solution.py:540
  22.7 1.9 %collective-permute-start.10 = (f32[512,128]{1,0:T(8,128)S(1)}, f32[512,128]{1,0:T(8,128)S(1)}, u32[]{:S(2)}, u32[]{:S(2)}) collective-permute-start(f32[512,128]{1,0:T(8,128)S(1)} %get-tuple-element.93), channel_id=1, source_target_pairs={{8,16},{16,8},{24,32},{32,24},{40,48},{48,40},{56,64},{64,56},{72,... | collective-permute-start | bytes 786440 | tf_op jit(solution)/shard_map/ppermute | solution.py:553
  24.6 1.8 %collective-permute-done.3.refs_18_ = f32[488,128]{1,0:T(8,128)S(1)} collective-permute-done((f32[488,128]{1,0:T(8,128)S(1)}, f32[488,128]{1,0:T(8,128)S(1)}, u32[]{:S(2)}, u32[]{:S(2)}) %collective-permute-start.3) | collective-permute-done | bytes 249888 | tf_op jit(solution)/shard_map/ppermute | solution.py:553
  26.4 1.3 %shard_map.141 = (f32[6,3,40,128]{3,2,1,0:T(8,128)S(1)}, f32[240,128]{1,0:T(8,128)S(1)}, f32[3,80,128]{2,1,0:T(8,128)S(1)}, f32[8,256]{1,0:T(8,128)S(1)}, f32[50...) custom-call(f32[960,128]{1,0:T(8,128)S(1)} %get-tuple-element.53.fn.refs_0_, f32[960,128]{1,0:T(8,128)S(1)} %get-tuple-element.55.refs_1_, ...), custom_call_target="tpu_custom_call" | custom-call | flops 1000000000 | bytes 1024 | tf_op jit(solution)/shard_map/pallas_call | solution.py:540
  27.7 6.8 %collective-permute-start.8 = (f32[512,128]{1,0:T(8,128)S(1)}, f32[512,128]{1,0:T(8,128)S(1)}, u32[]{:S(2)}, u32[]{:S(2)}) collective-permute-start(f32[512,128]{1,0:T(8,128)S(1)} %get-tuple-element.87), channel_id=1, source_target_pairs={{8,16},{16,8},{24,32},{32,24},{40,48},{48,40},{56,64},{64,56},{72,... | collective-permute-start | bytes 786440 | tf_op jit(solution)/shard_map/ppermute | solution.py:553
  34.4 0.1 collective-permute-start.9
  34.6 0.5 %collective-permute-start.7 = (f32[504,128]{1,0:T(8,128)S(1)}, f32[504,128]{1,0:T(8,128)S(1)}, u32[]{:S(2)}, u32[]{:S(2)}) collective-permute-start(f32[504,128]{1,0:T(8,128)S(1)} %get-tuple-element.86), channel_id=1, source_target_pairs={{0,8},{8,0},{16,24},{24,16},{32,40},{40,32},{48,56},{56,48},{64,72... | collective-permute-start | bytes 774152 | tf_op jit(solution)/shard_map/ppermute | solution.py:553
  35.0 1.0 %collective-permute-done.9.rxa = f32[504,128]{1,0:T(8,128)S(1)} collective-permute-done((f32[504,128]{1,0:T(8,128)S(1)}, f32[504,128]{1,0:T(8,128)S(1)}, u32[]{:S(2)}, u32[]{:S(2)}) %collective-permute-start.9) | collective-permute-done | bytes 258080 | tf_op jit(solution)/shard_map/ppermute | solution.py:553
  36.0 0.0 collective-permute-done.10.rxb
  36.0 1.0 %shard_map.142 = (f32[480,128]{1,0:T(8,128)S(1)}, f32[240,128]{1,0:T(8,128)S(1)}, f32[4,40,128]{2,1,0:T(8,128)S(1)}, f32[80,128]{1,0:T(8,128)S(1)}) custom-call(f32[960,128]{1,0:T(8,128)S(1)} %get-tuple-element.53.fn.refs_0_, f32[480,128]{1,0:T(8,128)S(1)} %get-tuple-element.54.refs_2_.cn, f32[6,3,40,128]{3,2,1,0:T(8,128)S(1)} %get-tuple-element.88.f1, ...), custom_call_target="tpu_custom_call" | custom-call | flops 1 | bytes 1024 | tf_op jit(solution)/shard_map/pallas_call | solution.py:540
  37.1 0.0 collective-permute-done.7.rxa
  37.1 4.2 %collective-permute-done.8.rxb = f32[512,128]{1,0:T(8,128)S(1)} collective-permute-done((f32[512,128]{1,0:T(8,128)S(1)}, f32[512,128]{1,0:T(8,128)S(1)}, u32[]{:S(2)}, u32[]{:S(2)}) %collective-permute-start.8) | collective-permute-done | bytes 262176 | tf_op jit(solution)/shard_map/ppermute | solution.py:553
  41.3 1.8 %shard_map.143 = (f32[960,128]{1,0:T(8,128)}, f32[480,128]{1,0:T(8,128)}, f32[160,128]{1,0:T(8,128)}, f32[80,128]{1,0:T(8,128)}) custom-call(f32[960,128]{1,0:T(8,128)S(1)} %get-tuple-element.53.fn.refs_0_, f32[480,128]{1,0:T(8,128)S(1)} %get-tuple-element.54.refs_2_.cn, f32[6,3,40,128]{3,2,1,0:T(8,128)S(1)} %get-tuple-element.82.f1g.f1, ...), custom_call_target="tpu_custom_call" | custom-call | tf_op jit(solution)/shard_map/pallas_call | solution.py:540
Async XLA Ops:
  3.0 18.3 %collective-permute-start.2 = (f32[976,128]{1,0:T(8,128)S(1)}, f32[976,128]{1,0:T(8,128)S(1)}, u32[]{:S(2)}, u32[]{:S(2)}) collective-permute-start(f32[976,128]{1,0:T(8,128)S(1)} %get-tuple-element.73), channel_id=1, source_target_pairs={{0,8},{8,0},{16,24},{24,16},{32,40},{40,32},{48,56},{56,48},{64,72... | collective-permute-start | bytes 1499144 | tf_op jit(solution)/shard_map/ppermute | solution.py:553
  3.1 8.7 %collective-permute-start = (f32[80,128]{1,0:T(8,128)S(1)}, f32[80,128]{1,0:T(8,128)S(1)}, u32[]{:S(2)}, u32[]{:S(2)}) collective-permute-start(f32[80,128]{1,0:T(8,128)S(1)} %get-tuple-element.62), channel_id=1, source_target_pairs={{1,2},{2,1},{3,4},{4,3},{5,6},{6,5},{9,10},{10,9},{11,12},{12,11},... | collective-permute-start | bytes 122888 | tf_op jit(solution)/shard_map/ppermute | solution.py:553
  7.0 5.6 %collective-permute-start.1 = (f32[80,128]{1,0:T(8,128)S(1)}, f32[80,128]{1,0:T(8,128)S(1)}, u32[]{:S(2)}, u32[]{:S(2)}) collective-permute-start(f32[80,128]{1,0:T(8,128)S(1)} %get-tuple-element.63), channel_id=1, source_target_pairs={{0,1},{1,0},{2,3},{3,2},{4,5},{5,4},{6,7},{7,6},{8,9},{9,8},{10,11... | collective-permute-start | bytes 122888 | tf_op jit(solution)/shard_map/ppermute | solution.py:553
  9.6 11.7 %collective-permute-start.6 = (f32[488,128]{1,0:T(8,128)S(1)}, f32[488,128]{1,0:T(8,128)S(1)}, u32[]{:S(2)}, u32[]{:S(2)}) collective-permute-start(f32[488,128]{1,0:T(8,128)S(1)} %get-tuple-element.78), channel_id=1, source_target_pairs={{8,16},{16,8},{24,32},{32,24},{40,48},{48,40},{56,64},{64,56},{72,... | collective-permute-start | bytes 749576 | tf_op jit(solution)/shard_map/ppermute | solution.py:553
  13.5 7.8 %collective-permute-start.4 = (f32[80,128]{1,0:T(8,128)S(1)}, f32[80,128]{1,0:T(8,128)S(1)}, u32[]{:S(2)}, u32[]{:S(2)}) collective-permute-start(f32[80,128]{1,0:T(8,128)S(1)} %get-tuple-element.75), channel_id=1, source_target_pairs={{0,8},{8,0},{16,24},{24,16},{32,40},{40,32},{48,56},{56,48},{64,72... | collective-permute-start | bytes 122888 | tf_op jit(solution)/shard_map/ppermute | solution.py:553
  15.7 5.6 %collective-permute-start.5 = (f32[80,128]{1,0:T(8,128)S(1)}, f32[80,128]{1,0:T(8,128)S(1)}, u32[]{:S(2)}, u32[]{:S(2)}) collective-permute-start(f32[80,128]{1,0:T(8,128)S(1)} %get-tuple-element.76), channel_id=1, source_target_pairs={{8,16},{16,8},{24,32},{32,24},{40,48},{48,40},{56,64},{64,56},{72,... | collective-permute-start | bytes 122888 | tf_op jit(solution)/shard_map/ppermute | solution.py:553
  17.6 8.7 %collective-permute-start.3 = (f32[488,128]{1,0:T(8,128)S(1)}, f32[488,128]{1,0:T(8,128)S(1)}, u32[]{:S(2)}, u32[]{:S(2)}) collective-permute-start(f32[488,128]{1,0:T(8,128)S(1)} %get-tuple-element.74), channel_id=1, source_target_pairs={{8,16},{16,8},{24,32},{32,24},{40,48},{48,40},{56,64},{64,56},{72,... | collective-permute-start | bytes 749576 | tf_op jit(solution)/shard_map/ppermute | solution.py:553
  22.7 13.4 %collective-permute-start.10 = (f32[512,128]{1,0:T(8,128)S(1)}, f32[512,128]{1,0:T(8,128)S(1)}, u32[]{:S(2)}, u32[]{:S(2)}) collective-permute-start(f32[512,128]{1,0:T(8,128)S(1)} %get-tuple-element.93), channel_id=1, source_target_pairs={{8,16},{16,8},{24,32},{32,24},{40,48},{48,40},{56,64},{64,56},{72,... | collective-permute-start | bytes 786440 | tf_op jit(solution)/shard_map/ppermute | solution.py:553
  27.7 13.6 %collective-permute-start.8 = (f32[512,128]{1,0:T(8,128)S(1)}, f32[512,128]{1,0:T(8,128)S(1)}, u32[]{:S(2)}, u32[]{:S(2)}) collective-permute-start(f32[512,128]{1,0:T(8,128)S(1)} %get-tuple-element.87), channel_id=1, source_target_pairs={{8,16},{16,8},{24,32},{32,24},{40,48},{48,40},{56,64},{64,56},{72,... | collective-permute-start | bytes 786440 | tf_op jit(solution)/shard_map/ppermute | solution.py:553
  34.4 1.6 %collective-permute-start.9 = (f32[504,128]{1,0:T(8,128)S(1)}, f32[504,128]{1,0:T(8,128)S(1)}, u32[]{:S(2)}, u32[]{:S(2)}) collective-permute-start(f32[504,128]{1,0:T(8,128)S(1)} %get-tuple-element.92), channel_id=1, source_target_pairs={{0,8},{8,0},{16,24},{24,16},{32,40},{40,32},{48,56},{56,48},{64,72... | collective-permute-start | bytes 774152 | tf_op jit(solution)/shard_map/ppermute | solution.py:553
  34.6 2.5 %collective-permute-start.7 = (f32[504,128]{1,0:T(8,128)S(1)}, f32[504,128]{1,0:T(8,128)S(1)}, u32[]{:S(2)}, u32[]{:S(2)}) collective-permute-start(f32[504,128]{1,0:T(8,128)S(1)} %get-tuple-element.86), channel_id=1, source_target_pairs={{0,8},{8,0},{16,24},{24,16},{32,40},{40,32},{48,56},{56,48},{64,72... | collective-permute-start | bytes 774152 | tf_op jit(solution)/shard_map/ppermute | solution.py:553

commit v6 on v4

--- a/solution.py
+++ b/solution.py
@@ -23,8 +23,9 @@
 HALF = HCOARSE + 3 * CZ
 HLATER = HCOARSE + 40
 C_OPEN = 5*10**9
-C_ONE = (5*10**9, 10**9)
+C_ONE = (5*10**9, 5*10**9)
 C_TWO = 1
+C_BOTH = 1
 VM = pl.BlockSpec(memory_space=pltpu.VMEM)
 
 
@@ -78,11 +79,15 @@
     n = 11
     hbm, (fn, fo, cn, co, sf, lf, sc, lc, tp, pool, spread), (ma, mbf, mbg, mya, myb, tmp, sems) = refs[:n], refs[n : 2 * n], refs[2 * n :]
     copies = [pltpu.make_async_copy(src, dst, sems.at[q]) for q, (src, dst) in enumerate(zip(hbm, refs[n : 2 * n]))]
-    for copy in copies:
-        copy.start()
-    for copy in copies:
-        copy.wait()
+    early = (0, 2, 8, 9)
+    late = [q for q in range(n) if q not in early]
+    for q in (*early, *late):
+        copies[q].start()
+    for q in early:
+        copies[q].wait()
     pack_x(fn, cn, tp, pool, (ma, mbf, mbg), tmp)
+    for q in late:
+        copies[q].wait()
     py = lax.rem(lax.axis_index("gy"), 2)
     group = lanes((FZ, L)) >> 2
     for out, right in ((mya, 1 - py), (myb, py)):
@@ -268,6 +273,7 @@
 
 
 def fill_ghosts(U, V, cc, spread, edges):
+    cc[...] = jnp.zeros_like(cc)
     for f in range(3):
         for r in range(3):
             for t in range(2):
@@ -313,20 +319,13 @@
             yield k, i, t, values
 
 
-def step_one(
-    a, fn, fo, cn, co, sf, lf, sc, lc, tp, fh, foh, sh, th, ch, coh, sch, rg, rxa, rxb, rca, rcb, spread, pool,
-    f1, c1, c1h, rg1, mxa, mxb, jv, cf, cv, U, V, cc, tmp,
-):
+def fill_one(a, fn, cn, tp, fh, th, ch, rg, rxa, rxb, rca, rcb, jv, U, V, heights):
     px = lax.rem(lax.axis_index("gx"), 2)
-    edges = edges_here()
-    lane = lanes((8, L))
-    lane40 = lanes((FZ, L))
-    near40 = ((lane40 + 4) & 127) < 8
+    near40 = ((lanes((FZ, L)) + 4) & 127) < 8
 
     def corner(rc, part, g):
         return jnp.where(near40, pltpu.roll(rc[part * 40 : part * 40 + 40, :], (2 * L - 4 - 8 * g) % L, 1), 0.0)
 
-    cc[...] = jnp.zeros_like(cc)
     body = slice(ZP, ZP + FZ)
     for i in range(3):
         f = 3 * a + i
@@ -349,18 +348,27 @@
                 V[i, cr, 1, ZP + half * 40 : ZP + half * 40 + 40, :] = corner(rc, 1, f * 2 + half)
             V[i, cr, 0, ZP - 1 : ZP, :] = rx[HFINE + i : HFINE + i + 1, :]
             V[i, cr, 1, ZP - 1 : ZP, :] = corner(rc, 0, 7 + f)[0:1, :]
-        for t in range(2):
-            jv[0, fr, t] = jnp.broadcast_to(rx[HTOPO + t : HTOPO + t + 1, :], (8, L))
-        jv[0, fr, 2] = corner(rc, 0, 6)[0:8, :]
-    for x in range(2):
-        for t in range(2):
-            jv[0, 1 + x, t] = jnp.broadcast_to(tp[t * 2 + x : t * 2 + x + 1, :].astype(F32), (8, L))
-        jv[0, 1 + x, 2] = th[x]
+        if heights:
+            for t in range(2):
+                jv[0, fr, t] = jnp.broadcast_to(rx[HTOPO + t : HTOPO + t + 1, :], (8, L))
+            jv[0, fr, 2] = corner(rc, 0, 6)[0:8, :]
+    if heights:
+        for x in range(2):
+            for t in range(2):
+                jv[0, 1 + x, t] = jnp.broadcast_to(tp[t * 2 + x : t * 2 + x + 1, :].astype(F32), (8, L))
+            jv[0, 1 + x, 2] = th[x]
+
+
+def spacings(jv):
     for r in range(4):
         for t in range(3):
             spacing = 1.0 + jv[0, r, t] * (1.0 / 1024.0)
             jv[0, r, t] = 1.0 / (2.0 * spacing)
             jv[1, r, t] = 1.0 / (spacing * spacing)
+
+
+def tables(sf, lf, sc, lc, sh, sch, jv, cf, cv):
+    spacings(jv)
     for x in range(2):
         for t in range(3):
             shear = sf[coef_rows(t, x), :] if t < 2 else sh[x]
@@ -372,6 +380,19 @@
         lame = lc[...] if t == 0 else sch[1]
         cv[0, t] = DT2 * shear
         cv[1, t] = DT2 * (lame + shear)
+
+
+def step_one(
+    a, fn, fo, cn, co, sf, lf, sc, lc, tp, fh, foh, sh, th, ch, coh, sch, rg, rxa, rxb, rca, rcb, spread, pool,
+    f1, c1, c1h, rg1, mxa, jv, cf, cv, U, V, cc, tmp,
+):
+    px = lax.rem(lax.axis_index("gx"), 2)
+    edges = edges_here()
+    lane = lanes((8, L))
+    lane40 = lanes((FZ, L))
+    fill_one(a, fn, cn, tp, fh, th, ch, rg, rxa, rxb, rca, rcb, jv, U, V, a == 0)
+    if a == 0:
+        tables(sf, lf, sc, lc, sh, sch, jv, cf, cv)
     fill_ghosts(U, V, cc, spread, edges)
     keep = ((lane < 64) & edges[3]) | ((lane >= 64) & edges[2])
     for k, i, x, t, (c2, lap, gd) in fine_pieces(U, jv, lane):
@@ -394,28 +415,91 @@
         for t in range(3):
             tmp[i : i + 1, t * L : (t + 1) * L] = f1[i * 2, t, FZ - 1 : FZ, :] + f1[i * 2 + 1, t, FZ - 1 : FZ, :]
     rg1[...] = exact_dot(tmp[...], pool[...])
-    for out, row in ((mxb, px), (mxa, 1 - px)):
-        for i in range(3):
-            for t in range(2):
-                out[i * 80 + t * 40 : i * 80 + t * 40 + 40, :] = f1[i * 2 + row, t]
-        out[HFINE:HCOARSE, :] = rg1[:, 0:L]
-        out[HCOARSE:HLATER, :] = later_corners(f1, c1h, row, lane40)
-        out[HLATER : HLATER + 3 * CZ, :] = c1[...]
-    mxb[HALF + 40 : HALF + 48, :] = jnp.zeros((8, L), F32)
-
-
-def later_corners(f1, c1h, row, lane40):
+    row = 1 - px
+    for i in range(3):
+        for t in range(2):
+            mxa[i * 80 + t * 40 : i * 80 + t * 40 + 40, :] = f1[i * 2 + row, t]
+    mxa[HFINE:HCOARSE, :] = rg1[:, 0:L]
+    mxa[HCOARSE:HLATER, :] = later_corners([f1[i * 2 + row, 2] for i in range(3)], c1h, lane40)
+
+
+def step_one_both(
+    fn, fo, cn, co, sf, lf, sc, lc, tp, fh, foh, sh, th, ch, coh, sch, rg, rxa, rxf, rxg, rca, rcb, spread, pool,
+    f1f, c1f, c1hf, rgf, f1g, c1g, c1hg, rgg, mxf, mxg, jv, cf, cv, U, V, cc, tmp,
+):
+    fields = ((f1f, c1f, c1hf, rgf), (f1g, c1g, c1hg, rgg))
+    for a, rxb in enumerate((rxf, rxg)):
+        step_one(
+            a, fn, fo, cn, co, sf, lf, sc, lc, tp, fh, foh, sh, th, ch, coh, sch, rg, rxa, rxb, rca, rcb, spread, pool,
+            *fields[a], (mxf, mxg)[a], jv, cf, cv, U, V, cc, tmp,
+        )
+
+
+def rush(
+    a, fn, fo, cn, co, sf, lf, sc, lc, tp, fh, foh, sh, th, ch, coh, sch, rg, rxa, rxb, rca, rcb, spread, pool,
+    mxb, jv, U, V, cc, tmp, beside_fine, beside_coarse, bottoms,
+):
+    px = lax.rem(lax.axis_index("gx"), 2)
+    edges = edges_here()
+    lane = lanes((8, L))
+    lane40 = lanes((FZ, L))
+    keep = ((lane < 64) & edges[3]) | ((lane >= 64) & edges[2])
+    bottoms[...] = jnp.zeros_like(bottoms)
+    fill_one(a, fn, cn, tp, fh, th, ch, rg, rxa, rxb, rca, rcb, jv, U, V, True)
+    spacings(jv)
+    fill_ghosts(U, V, cc, spread, edges)
+
+    def stepped(c2, old, shear, lame, lap, gd):
+        return c2 - old + (DT2 * shear) * lap + (DT2 * (lame + shear)) * gd
+
+    for near, x, ks in ((0, px, range(FZ // 8)), (1, 1 - px, (FZ // 8 - 1,))):
+        for k in ks:
+            at = ZP + 8 * k
+            zs = slice(8 * k, 8 * k + 8)
+            parts = vector_piece(
+                lambda i, r, t, dz: U[i, x + r, t, at + dz : at + dz + 8, :], (1,), 3,
+                lambda r, t: jv[0, x + r, t], lambda r, t: jv[1, x + r, t], 1.0, lane,
+            )
+            for (i, r, t), (c2, lap, gd) in parts.items():
+                f = 3 * a + i
+                if t < 2:
+                    rows = coef_rows(t, x, 8 * k, 8)
+                    new = stepped(c2, fo[fine_rows(f, t, x, 8 * k, 8), :], sf[rows, :], lf[rows, :], lap, gd)
+                else:
+                    new = stepped(c2, foh[f * 2 + x, zs, :], sh[x, zs, :], sh[2 + x, zs, :], lap, gd)
+                    new = jnp.where(keep, new, 0.0)
+                if near == 0:
+                    if t < 2:
+                        mxb[i * 80 + t * 40 + 8 * k : i * 80 + t * 40 + 8 * k + 8, :] = new
+                    else:
+                        beside_fine[i, zs, :] = new
+                if k == FZ // 8 - 1:
+                    bottoms[near, i : i + 1, t * L : (t + 1) * L] = new[7:8, :]
+    for k, i, t, (c2, lap, gd) in coarse_pieces(V, lane):
+        zs = slice(8 * k, 8 * k + 8)
+        f = 3 * a + i
+        if t == 0:
+            new = stepped(c2, co[f * CZ + 8 * k : f * CZ + 8 * k + 8, :], sc[zs, :], lc[zs, :], lap, gd)
+            mxb[HLATER + i * CZ + 8 * k : HLATER + i * CZ + 8 * k + 8, :] = new
+        else:
+            new = stepped(c2, coh[f, zs, :], sch[0, zs, :], sch[1, zs, :], lap, gd)
+            beside_coarse[i, zs, :] = jnp.where(keep, new, 0.0)
+    mxb[HFINE:HCOARSE, :] = exact_dot(bottoms[0] + bottoms[1], pool[:, 0:L])
+    mxb[HCOARSE:HLATER, :] = later_corners([beside_fine[i] for i in range(3)], beside_coarse, lane40)
+
+
+def later_corners(beside, c1h, lane40):
     group = lane40 >> 2
     acc = jnp.zeros((FZ, L), F32)
     for i in range(3):
-        acc = jnp.where(group == i, pltpu.roll(f1[i * 2 + row, 2], 2 + 4 * i, 1), acc)
+        acc = jnp.where(group == i, pltpu.roll(beside[i], 2 + 4 * i, 1), acc)
         for half in range(2):
             g = 3 + 2 * i + half
             acc = jnp.where(group == g, pltpu.roll(c1h[i, half * 40 : half * 40 + 40, :], 2 + 4 * g, 1), acc)
     return acc
 
 
-def step_two(a, fn, cn, f1, c1, c1h, rg1, rxa, rxb, jv, cf, cv, spread, fout, cout, U, V, cc, after_fine=None):
+def step_two(a, fn, cn, f1, c1, c1h, rg1, rxa, rac, rxb, jv, cf, cv, spread, fout, cout, U, V, cc, after_fine=None):
     px = lax.rem(lax.axis_index("gx"), 2)
     edges = edges_here()
     lane = lanes((8, L))
@@ -434,12 +518,12 @@
         V[i, 1, 1, ZP : ZP + CZ, :] = c1h[i]
         for t in range(2):
             V[i, 1, t, ZP - 1 : ZP, :] = rg1[i : i + 1, t * L : (t + 1) * L]
-    for rx, fr, cr in ((rxa, 3 * (1 - px), 2 * (1 - px)), (rxb, 3 * px, 2 * px)):
+    for rx, rz, zat, fr, cr in ((rxa, rac, 0, 3 * (1 - px), 2 * (1 - px)), (rxb, rxb, HLATER, 3 * px, 2 * px)):
         for i in range(3):
             for t in range(2):
                 U[i, fr, t, body, :] = rx[i * 80 + t * 40 : i * 80 + t * 40 + 40, :]
             U[i, fr, 2, body, :] = corner(rx, i)
-            V[i, cr, 0, ZP : ZP + CZ, :] = rx[HLATER + i * CZ : HLATER + (i + 1) * CZ, :]
+            V[i, cr, 0, ZP : ZP + CZ, :] = rz[zat + i * CZ : zat + (i + 1) * CZ, :]
             for half in range(2):
                 V[i, cr, 1, ZP + half * 40 : ZP + half * 40 + 40, :] = corner(rx, 3 + i * 2 + half)
             V[i, cr, 0, ZP - 1 : ZP, :] = rx[HFINE + i : HFINE + i + 1, :]
@@ -460,8 +544,8 @@
             cout[i * CZ + 8 * k : i * CZ + 8 * k + 8, :] = c2 - old + cv[0, t, zs, :] * lap + cv[1, t, zs, :] * gd
 
 
-def step_two_first(fn, cn, f1, c1, c1h, rg1, rxa, rxb, jv, cf, cv, spread, f1g, c1g, fout, cout, fk1, ck1, U, V, cc):
-    step_two(0, fn, cn, f1, c1, c1h, rg1, rxa, rxb, jv, cf, cv, spread, fout, cout, U, V, cc)
+def step_two_first(fn, cn, f1, c1, c1h, rg1, rxa, rac, rxb, jv, cf, cv, spread, f1g, c1g, fout, cout, fk1, ck1, U, V, cc):
+    step_two(0, fn, cn, f1, c1, c1h, rg1, rxa, rac, rxb, jv, cf, cv, spread, fout, cout, U, V, cc)
     for q in range(4):
         x, t = q // 2, q % 2
         total = jnp.zeros((FZ, L), F32)
@@ -475,7 +559,7 @@
 
 
 def step_two_last(
-    fn, cn, f1, c1, c1h, rg1, rxa, rxb, jv, cf, cv, spread, fof, cof, fk1, ck1,
+    fn, cn, f1, c1, c1h, rg1, rxa, rac, rxb, jv, cf, cv, spread, fof, cof, fk1, ck1,
     fout, cout, fk, ck, U, V, cc, fog, cog, fks, cks, sems,
 ):
     half_f, half_c = 3 * FZ * 4, 3 * CZ
@@ -493,7 +577,7 @@
     def fine_done():
         copies[2].start()
 
-    step_two(1, fn, cn, f1, c1, c1h, rg1, rxa, rxb, jv, cf, cv, spread, fog, cog, U, V, cc, fine_done)
+    step_two(1, fn, cn, f1, c1, c1h, rg1, rxa, rac, rxb, jv, cf, cv, spread, fog, cog, U, V, cc, fine_done)
     copies[3].start()
     total = ck1[...]
     for i in range(3):
@@ -568,28 +652,36 @@
     rcb = swap(mcb, "gx", 1)
     rca = swap(mca, "gx", 0)
     field = ((3, 4, 3, 56, L), (3, 3, 2, 96, L), (3, 8, 256))
-    firsts, far, near = [], [], []
+    far = []
     for a in range(2):
-        *results, mxa, mxb, jv, cf, cv = call(
-            one_field(step_one, a),
+        (mxb,) = call(
+            one_field(rush, a),
             (fn, fo, cn, co, sf, lf, sc, lc, tp, fh, foh, sh, th, ch, coh, sch, rg, in_chip, by_link[a], rca, rcb, spread, pool),
-            ((6, 3, FZ, L), (3 * CZ, L), (3, CZ, L), (8, 256), (HALF + 40, L), (HALF + 48, L), (2, 4, 3, 8, L), (2, 2, 3, FZ, L), (2, 2, CZ, L)),
-            field + ((8, 384),),
+            ((HALF + 40, L),),
+            ((2, 4, 3, 8, L), *field, (8, 384), (3, FZ, L), (3, CZ, L), (2, 8, 384)),
             flops=C_ONE[a],
         )
-        firsts.append(results)
         far.append(swap(mxb, "gx", 1))
-        near.append(swap(mxa, "gx", 0))
+    first = ((6, 3, FZ, L), (3 * CZ, L), (3, CZ, L), (8, 256))
+    *results, mxf, mxg, jv, cf, cv = call(
+        step_one_both,
+        (fn, fo, cn, co, sf, lf, sc, lc, tp, fh, foh, sh, th, ch, coh, sch, rg, in_chip, *by_link, rca, rcb, spread, pool),
+        first + first + ((HLATER, L), (HLATER, L), (2, 4, 3, 8, L), (2, 2, 3, FZ, L), (2, 2, CZ, L)),
+        field + ((8, 384),),
+        flops=C_BOTH,
+    )
+    firsts = (results[:4], results[4:])
+    near = [(swap(m, "gx", 0), swap(r[1], "gx", 0)) for m, r in zip((mxf, mxg), firsts)]
     fof, cof, fk1, ck1 = call(
         step_two_first,
-        (fn, cn, *firsts[0], near[0], far[0], jv, cf, cv, spread, *firsts[1][:2]),
+        (fn, cn, *firsts[0], *near[0], far[0], jv, cf, cv, spread, *firsts[1][:2]),
         ((3 * FZ * 4, L), (3 * CZ, L), (4, FZ, L), (CZ, L)),
         field,
         flops=C_TWO,
     )
     fout, cout, fk, ck = call(
         step_two_last,
-        (fn, cn, *firsts[1], near[1], far[1], jv, cf, cv, spread, fof, cof, fk1, ck1),
+        (fn, cn, *firsts[1], *near[1], far[1], jv, cf, cv, spread, fof, cof, fk1, ck1),
         ((FINE_ROWS, L), (COARSE_ROWS, L), (4 * FZ, L), (CZ, L)),
         field + ((3 * FZ * 4, L), (3 * CZ, L), (4 * FZ, L), (CZ, L), pltpu.SemaphoreType.DMA((6,))),
         out_space=pl.BlockSpec(memory_space=pltpu.HBM),

time: 43.4 us -> 43.2 us (level)
  starting transfers between devices: 25.9 us -> 23.6 us
  Pallas kernels: 9.25 us -> 10.8 us
  waiting for transfers between devices: 7.21 us -> 7.75 us
    ppermute x11 -> x13, starting transfers between devices: 25.9 us -> 23.6 us  [swap(): lax.ppermute(cells, axis, [p for i in range(first, count - 1, 2) for p in...]
    pallas_call x6 -> x7, Pallas kernels: 9.25 us -> 10.8 us  [call(): pl.pallas_call(kernel, out_shape=shapes, in_specs=[space] * len(args), ou...]
    ppermute x11 -> x13, waiting for transfers between devices: 7.21 us -> 7.75 us  [swap(): lax.ppermute(cells, axis, [p for i in range(first, count - 1, 2) for p in...]
  transfers between devices with their start and end apart: 11 -> 13, of which waited for: 4 -> 6; matrix products, arithmetic and copies ran while one was open for 0% -> 0% of each run, Pallas kernels for 12% -> 16%
where the time goes in v6:
time: 43.2 us; the launch traced here: 43 us
  starting transfers between devices  23.6 us (55%)
  Pallas kernels  10.8 us (25%)
  waiting for transfers between devices  7.75 us (18%)
  between operations  0.77 us (2%)
    ppermute x13, starting transfers between devices, swap(): lax.ppermute(cells, axis, [p for i in range(first, count - 1, 2) for p in...  23.6 us
    pallas_call x7, Pallas kernels, call(): pl.pallas_call(kernel, out_shape=shapes, in_specs=[space] * len(args), ou...  10.8 us
    ppermute x13, waiting for transfers between devices, swap(): lax.ppermute(cells, axis, [p for i in range(first, count - 1, 2) for p in...  7.75 us
  transfers between devices with their start and end apart: 13, of which 6 were waited for; matrix products, arithmetic and copies ran while one was open for 0% of the time, Pallas kernels for 16%

profile of v6, /device:TPU:106, one launch (start us, length us, event | category | flops | bytes accessed | tf_op | source)
XLA Modules:
  0.0 43.0 jit_solution(11088186151515393391)
XLA Ops:
  0.6 2.4 %shard_map.138 = (f32[960,128]{1,0:T(8,128)S(1)}, f32[960,128]{1,0:T(8,128)S(1)}, f32[480,128]{1,0:T(8,128)S(1)}, f32[480,128]{1,0:T(8,128)S(1)}, f32[160,128]{1...) custom-call(f32[960,128]{1,0:T(8,128)} %bitcast.45, ...), custom_call_target="tpu_custom_call" | custom-call | tf_op jit(solution)/shard_map/pallas_call | solution.py:600
  3.0 3.9 %collective-permute-start = (f32[80,128]{1,0:T(8,128)S(1)}, f32[80,128]{1,0:T(8,128)S(1)}, u32[]{:S(2)}, u32[]{:S(2)}) collective-permute-start(f32[80,128]{1,0:T(8,128)S(1)} %get-tuple-element.60), channel_id=1, source_target_pairs={{1,2},{2,1},{3,4},{4,3},{5,6},{6,5},{9,10},{10,9},{11,12},{12,11},... | collective-permute-start | bytes 122888 | tf_op jit(solution)/shard_map/ppermute | solution.py:613
  6.9 2.6 %collective-permute-start.1 = (f32[80,128]{1,0:T(8,128)S(1)}, f32[80,128]{1,0:T(8,128)S(1)}, u32[]{:S(2)}, u32[]{:S(2)}) collective-permute-start(f32[80,128]{1,0:T(8,128)S(1)} %get-tuple-element.61), channel_id=1, source_target_pairs={{0,1},{1,0},{2,3},{3,2},{4,5},{5,4},{6,7},{7,6},{8,9},{9,8},{10,11... | collective-permute-start | bytes 122888 | tf_op jit(solution)/shard_map/ppermute | solution.py:613
  9.5 0.0 collective-permute-start.2
  9.6 2.5 %collective-permute-start.3 = (f32[496,128]{1,0:T(8,128)S(1)}, f32[496,128]{1,0:T(8,128)S(1)}, u32[]{:S(2)}, u32[]{:S(2)}) collective-permute-start(f32[496,128]{1,0:T(8,128)S(1)} %get-tuple-element.72), channel_id=1, source_target_pairs={{8,16},{16,8},{24,32},{32,24},{40,48},{48,40},{56,64},{64,56},{72,... | collective-permute-start | bytes 761864 | tf_op jit(solution)/shard_map/ppermute | solution.py:613
  12.1 0.0 collective-permute-done.ryb
  12.1 0.4 collective-permute-done.1.rya
  12.5 0.8 %shard_map.139 = (f32[12,40,128]{2,1,0:T(8,128)S(1)}, f32[12,40,128]{2,1,0:T(8,128)S(1)}, f32[4,40,128]{2,1,0:T(8,128)S(1)}, f32[2,8,128]{2,1,0:T(8,128)S(1)}, f...) custom-call(f32[80,128]{1,0:T(8,128)S(1)} %collective-permute-done.r, ...), custom_call_target="tpu_custom_call" | custom-call | flops 5000000000 | bytes 1024 | tf_op jit(solution)/shard_map/pallas_call | solution.py:600
  13.4 2.3 %collective-permute-start.5 = (f32[80,128]{1,0:T(8,128)S(1)}, f32[80,128]{1,0:T(8,128)S(1)}, u32[]{:S(2)}, u32[]{:S(2)}) collective-permute-start(f32[80,128]{1,0:T(8,128)S(1)} %get-tuple-element.74), channel_id=1, source_target_pairs={{0,8},{8,0},{16,24},{24,16},{32,40},{40,32},{48,56},{56,48},{64,72... | collective-permute-start | bytes 122888 | tf_op jit(solution)/shard_map/ppermute | solution.py:613
  15.6 1.9 %collective-permute-start.6 = (f32[80,128]{1,0:T(8,128)S(1)}, f32[80,128]{1,0:T(8,128)S(1)}, u32[]{:S(2)}, u32[]{:S(2)}) collective-permute-start(f32[80,128]{1,0:T(8,128)S(1)} %get-tuple-element.75), channel_id=1, source_target_pairs={{8,16},{16,8},{24,32},{32,24},{40,48},{48,40},{56,64},{64,56},{72,... | collective-permute-start | bytes 122888 | tf_op jit(solution)/shard_map/ppermute | solution.py:613
  17.5 3.6 %collective-permute-start.4 = (f32[496,128]{1,0:T(8,128)S(1)}, f32[496,128]{1,0:T(8,128)S(1)}, u32[]{:S(2)}, u32[]{:S(2)}) collective-permute-start(f32[496,128]{1,0:T(8,128)S(1)} %get-tuple-element.73), channel_id=1, source_target_pairs={{8,16},{16,8},{24,32},{32,24},{40,48},{48,40},{56,64},{64,56},{72,... | collective-permute-start | bytes 761864 | tf_op jit(solution)/shard_map/ppermute | solution.py:613
  21.2 0.0 collective-permute-done.5.rca.refs_19_
  21.2 0.0 collective-permute-done.6.rcb.refs_20_
  21.2 0.0 collective-permute-done.3.rxf.refs_18_
  21.2 0.0 collective-permute-done.2.rxa.refs_17_
  21.2 1.2 %shard_map.142 = f32[528,128]{1,0:T(8,128)S(1)} custom-call(f32[960,128]{1,0:T(8,128)S(1)} %get-tuple-element.51.fn.refs_0_, f32[960,128]{1,0:T(8,128)S(1)} %get-tuple-element.53.fo.refs_1_, f32[480,128]{1,0:T(8,128)S(1)} %get-tuple-element.52.cn.refs_2_, f32[480,128]{1,0:T(8,128)S(1)} %get-tuple-element.54.co.refs_3_, ...), custom_call_target="tpu_custom_call" | custom-call | flops 5000000000 | bytes 1024 | tf_op jit(solution)/shard_map/pallas_call | solution.py:600
  22.4 2.1 %collective-permute-start.12 = (f32[528,128]{1,0:T(8,128)S(1)}, f32[528,128]{1,0:T(8,128)S(1)}, u32[]{:S(2)}, u32[]{:S(2)}) collective-permute-start(f32[528,128]{1,0:T(8,128)S(1)} %shard_map.142), channel_id=1, source_target_pairs={{8,16},{16,8},{24,32},{32,24},{40,48},{48,40},{56,64},{64,56},{72,... | collective-permute-start | bytes 811016 | tf_op jit(solution)/shard_map/ppermute | solution.py:613
  24.5 4.7 %collective-permute-done.4.rxg.refs_18_ = f32[496,128]{1,0:T(8,128)S(1)} collective-permute-done((f32[496,128]{1,0:T(8,128)S(1)}, f32[496,128]{1,0:T(8,128)S(1)}, u32[]{:S(2)}, u32[]{:S(2)}) %collective-permute-start.4) | collective-permute-done | bytes 253984 | tf_op jit(solution)/shard_map/ppermute | solution.py:613
  29.2 1.2 %shard_map.141 = f32[528,128]{1,0:T(8,128)S(1)} custom-call(f32[960,128]{1,0:T(8,128)S(1)} %get-tuple-element.51.fn.refs_0_, f32[960,128]{1,0:T(8,128)S(1)} %get-tuple-element.53.fo.refs_1_, f32[480,128]{1,0:T(8,128)S(1)} %get-tuple-element.52.cn.refs_2_, f32[480,128]{1,0:T(8,128)S(1)} %get-tuple-element.54.co.refs_3_, ...), custom_call_target="tpu_custom_call" | custom-call | flops 5000000000 | bytes 1024 | tf_op jit(solution)/shard_map/pallas_call | solution.py:600
  30.4 3.8 %collective-permute-start.9 = (f32[528,128]{1,0:T(8,128)S(1)}, f32[528,128]{1,0:T(8,128)S(1)}, u32[]{:S(2)}, u32[]{:S(2)}) collective-permute-start(f32[528,128]{1,0:T(8,128)S(1)} %shard_map.141), channel_id=1, source_target_pairs={{8,16},{16,8},{24,32},{32,24},{40,48},{48,40},{56,64},{64,56},{72,... | collective-permute-start | bytes 811016 | tf_op jit(solution)/shard_map/ppermute | solution.py:613
  34.2 2.5 %shard_map.140 = (f32[6,3,40,128]{3,2,1,0:T(8,128)S(1)}, f32[240,128]{1,0:T(8,128)S(1)}, f32[3,80,128]{2,1,0:T(8,128)S(1)}, f32[8,256]{1,0:T(8,128)S(1)}, f32[6,...) custom-call(f32[960,128]{1,0:T(8,128)S(1)} %get-tuple-element.51.fn., ...), custom_call_target="tpu_custom_call" | custom-call | flops 1 | bytes 1024 | tf_op jit(solution)/shard_map/pallas_call | solution.py:600
  36.7 0.2 collective-permute-start.11
  36.9 0.4 collective-permute-start.10
  37.3 0.1 collective-permute-start.7
  37.4 0.7 %collective-permute-done.11.rac = f32[240,128]{1,0:T(8,128)S(1)} collective-permute-done((f32[240,128]{1,0:T(8,128)S(1)}, f32[240,128]{1,0:T(8,128)S(1)}, u32[]{:S(2)}, u32[]{:S(2)}) %collective-permute-start.11) | collective-permute-done | bytes 122912 | tf_op jit(solution)/shard_map/ppermute | solution.py:613
  38.1 0.1 collective-permute-start.8
  38.2 0.1 collective-permute-done.10.rxa
  38.3 0.0 collective-permute-done.12.rxb
  38.3 1.0 %shard_map.143 = (f32[480,128]{1,0:T(8,128)S(1)}, f32[240,128]{1,0:T(8,128)S(1)}, f32[4,40,128]{2,1,0:T(8,128)S(1)}, f32[80,128]{1,0:T(8,128)S(1)}) custom-call(f32[960,128]{1,0:T(8,128)S(1)} %get-tuple-element.51.fn.refs_0_, f32[480,128]{1,0:T(8,128)S(1)} %get-tuple-element.52.cn.refs_2_, f32[6,3,40,128]{3,2,1,0:T(8,128)S(1)} %get-tuple-element.85.f1, ...), custom_call_target="tpu_custom_call" | custom-call | flops 1 | bytes 1024 | tf_op jit(solution)/shard_map/pallas_call | solution.py:600
  39.3 0.1 collective-permute-done.8.rac
  39.4 0.0 collective-permute-done.7.rxa
  39.4 1.8 %collective-permute-done.9.rxb = f32[528,128]{1,0:T(8,128)S(1)} collective-permute-done((f32[528,128]{1,0:T(8,128)S(1)}, f32[528,128]{1,0:T(8,128)S(1)}, u32[]{:S(2)}, u32[]{:S(2)}) %collective-permute-start.9) | collective-permute-done | bytes 270368 | tf_op jit(solution)/shard_map/ppermute | solution.py:613
  41.2 1.8 %shard_map.144 = (f32[960,128]{1,0:T(8,128)}, f32[480,128]{1,0:T(8,128)}, f32[160,128]{1,0:T(8,128)}, f32[80,128]{1,0:T(8,128)}) custom-call(f32[960,128]{1,0:T(8,128)S(1)} %get-tuple-element.51.fn.refs_0_, f32[480,128]{1,0:T(8,128)S(1)} %get-tuple-element.52.cn.refs_2_, f32[6,3,40,128]{3,2,1,0:T(8,128)S(1)} %get-tuple-element.77.f1g.f1, ...), custom_call_target="tpu_custom_call" | custom-call | tf_op jit(solution)/shard_map/pallas_call | solution.py:600
Async XLA Ops:
  3.0 9.1 %collective-permute-start = (f32[80,128]{1,0:T(8,128)S(1)}, f32[80,128]{1,0:T(8,128)S(1)}, u32[]{:S(2)}, u32[]{:S(2)}) collective-permute-start(f32[80,128]{1,0:T(8,128)S(1)} %get-tuple-element.60), channel_id=1, source_target_pairs={{1,2},{2,1},{3,4},{4,3},{5,6},{6,5},{9,10},{10,9},{11,12},{12,11},... | collective-permute-start | bytes 122888 | tf_op jit(solution)/shard_map/ppermute | solution.py:613
  6.9 5.6 %collective-permute-start.1 = (f32[80,128]{1,0:T(8,128)S(1)}, f32[80,128]{1,0:T(8,128)S(1)}, u32[]{:S(2)}, u32[]{:S(2)}) collective-permute-start(f32[80,128]{1,0:T(8,128)S(1)} %get-tuple-element.61), channel_id=1, source_target_pairs={{0,1},{1,0},{2,3},{3,2},{4,5},{5,4},{6,7},{7,6},{8,9},{9,8},{10,11... | collective-permute-start | bytes 122888 | tf_op jit(solution)/shard_map/ppermute | solution.py:613
  9.5 11.7 %collective-permute-start.2 = (f32[976,128]{1,0:T(8,128)S(1)}, f32[976,128]{1,0:T(8,128)S(1)}, u32[]{:S(2)}, u32[]{:S(2)}) collective-permute-start(f32[976,128]{1,0:T(8,128)S(1)} %get-tuple-element.71), channel_id=1, source_target_pairs={{0,8},{8,0},{16,24},{24,16},{32,40},{40,32},{48,56},{56,48},{64,72... | collective-permute-start | bytes 1499144 | tf_op jit(solution)/shard_map/ppermute | solution.py:613
  9.6 11.7 %collective-permute-start.3 = (f32[496,128]{1,0:T(8,128)S(1)}, f32[496,128]{1,0:T(8,128)S(1)}, u32[]{:S(2)}, u32[]{:S(2)}) collective-permute-start(f32[496,128]{1,0:T(8,128)S(1)} %get-tuple-element.72), channel_id=1, source_target_pairs={{8,16},{16,8},{24,32},{32,24},{40,48},{48,40},{56,64},{64,56},{72,... | collective-permute-start | bytes 761864 | tf_op jit(solution)/shard_map/ppermute | solution.py:613
  13.4 7.8 %collective-permute-start.5 = (f32[80,128]{1,0:T(8,128)S(1)}, f32[80,128]{1,0:T(8,128)S(1)}, u32[]{:S(2)}, u32[]{:S(2)}) collective-permute-start(f32[80,128]{1,0:T(8,128)S(1)} %get-tuple-element.74), channel_id=1, source_target_pairs={{0,8},{8,0},{16,24},{24,16},{32,40},{40,32},{48,56},{56,48},{64,72... | collective-permute-start | bytes 122888 | tf_op jit(solution)/shard_map/ppermute | solution.py:613
  15.6 5.6 %collective-permute-start.6 = (f32[80,128]{1,0:T(8,128)S(1)}, f32[80,128]{1,0:T(8,128)S(1)}, u32[]{:S(2)}, u32[]{:S(2)}) collective-permute-start(f32[80,128]{1,0:T(8,128)S(1)} %get-tuple-element.75), channel_id=1, source_target_pairs={{8,16},{16,8},{24,32},{32,24},{40,48},{48,40},{56,64},{64,56},{72,... | collective-permute-start | bytes 122888 | tf_op jit(solution)/shard_map/ppermute | solution.py:613
  17.5 11.7 %collective-permute-start.4 = (f32[496,128]{1,0:T(8,128)S(1)}, f32[496,128]{1,0:T(8,128)S(1)}, u32[]{:S(2)}, u32[]{:S(2)}) collective-permute-start(f32[496,128]{1,0:T(8,128)S(1)} %get-tuple-element.73), channel_id=1, source_target_pairs={{8,16},{16,8},{24,32},{32,24},{40,48},{48,40},{56,64},{64,56},{72,... | collective-permute-start | bytes 761864 | tf_op jit(solution)/shard_map/ppermute | solution.py:613
  22.4 15.9 %collective-permute-start.12 = (f32[528,128]{1,0:T(8,128)S(1)}, f32[528,128]{1,0:T(8,128)S(1)}, u32[]{:S(2)}, u32[]{:S(2)}) collective-permute-start(f32[528,128]{1,0:T(8,128)S(1)} %shard_map.142), channel_id=1, source_target_pairs={{8,16},{16,8},{24,32},{32,24},{40,48},{48,40},{56,64},{64,56},{72,... | collective-permute-start | bytes 811016 | tf_op jit(solution)/shard_map/ppermute | solution.py:613
  30.4 10.8 %collective-permute-start.9 = (f32[528,128]{1,0:T(8,128)S(1)}, f32[528,128]{1,0:T(8,128)S(1)}, u32[]{:S(2)}, u32[]{:S(2)}) collective-permute-start(f32[528,128]{1,0:T(8,128)S(1)} %shard_map.141), channel_id=1, source_target_pairs={{8,16},{16,8},{24,32},{32,24},{40,48},{48,40},{56,64},{64,56},{72,... | collective-permute-start | bytes 811016 | tf_op jit(solution)/shard_map/ppermute | solution.py:613
  36.7 1.4 %collective-permute-start.11 = (f32[240,128]{1,0:T(8,128)S(1)}, f32[240,128]{1,0:T(8,128)S(1)}, u32[]{:S(2)}, u32[]{:S(2)}) collective-permute-start(f32[240,128]{1,0:T(8,128)S(1)} %get-tuple-element.86.c1), channel_id=1, source_target_pairs={{0,8},{8,0},{16,24},{24,16},{32,40},{40,32},{48,56},{56,48},{64,72... | collective-permute-start | bytes 368648 | tf_op jit(solution)/shard_map/ppermute | solution.py:613
  36.9 1.4 %collective-permute-start.10 = (f32[288,128]{1,0:T(8,128)S(1)}, f32[288,128]{1,0:T(8,128)S(1)}, u32[]{:S(2)}, u32[]{:S(2)}) collective-permute-start(f32[288,128]{1,0:T(8,128)S(1)} %get-tuple-element.89), channel_id=1, source_target_pairs={{0,8},{8,0},{16,24},{24,16},{32,40},{40,32},{48,56},{56,48},{64,72... | collective-permute-start | bytes 442376 | tf_op jit(solution)/shard_map/ppermute | solution.py:613
  37.3 2.2 %collective-permute-start.7 = (f32[288,128]{1,0:T(8,128)S(1)}, f32[288,128]{1,0:T(8,128)S(1)}, u32[]{:S(2)}, u32[]{:S(2)}) collective-permute-start(f32[288,128]{1,0:T(8,128)S(1)} %get-tuple-element.81), channel_id=1, source_target_pairs={{0,8},{8,0},{16,24},{24,16},{32,40},{40,32},{48,56},{56,48},{64,72... | collective-permute-start | bytes 442376 | tf_op jit(solution)/shard_map/ppermute | solution.py:613
  38.1 1.3 %collective-permute-start.8 = (f32[240,128]{1,0:T(8,128)S(1)}, f32[240,128]{1,0:T(8,128)S(1)}, u32[]{:S(2)}, u32[]{:S(2)}) collective-permute-start(f32[240,128]{1,0:T(8,128)S(1)} %get-tuple-element.78.c1g.c1), channel_id=1, source_target_pairs={{0,8},{8,0},{16,24},{24,16},{32,40},{40,32},{48,56},{56,48},{64,72... | collective-permute-start | bytes 368648 | tf_op jit(solution)/shard_map/ppermute | solution.py:613
